TPU v7x, 32 devices: a whole 2x2x4 slice. The times are simulated.
32 devices in a mesh: ctx: 8 (over y, x, core), tp: 4 (over z).
Axes of the slice: x: 2, y: 2, z: 4, core: 2. Of those that a mesh axis runs over, the one named last changes fastest.
Arguments:
- tokens: bfloat16 [4096, 2048], P(('ctx', 'tp')), may hold values from -8 to 8
- projection: bfloat16 [2048, 640], P(None, 'tp'), may hold values from -0.125 to 0.125
- conv_weight: float32 [4, 640], P(None, 'tp'), may hold values from -2.5 to 2.5
Outputs:
- attended: bfloat16 [4096, 512], P('ctx', 'tp')
All inputs are finite; a program needn't handle non-finite values.
Results may differ from a plain program's by a relative error of at most 0.0032.
The roundings to bfloat16 on the way count: a program that leaves them out, or rounds other values in their place, can miss the bound.
Values may be sent and summed in bfloat16 or wider, within the bound.
No kernel may reach another device: no remote copies, remote signals or barrier semaphores. Data moves between devices by JAX's collectives and lax.ppermute only.
A program may use at most 64 MiB of HBM per device.

v0:
```python
import functools
import math

import jax
import jax.numpy as jnp
from jax import lax
from jax.experimental import pallas as pl
from jax.experimental.pallas import tpu as pltpu
from jax.sharding import PartitionSpec as P


FEAT = 16
HALO = 8
PIECES = 8
LANES = 128
QUAD_FEATS = FEAT * (FEAT + 1) // 2
NUM_FEAT = QUAD_FEATS + FEAT + 8
STATE_ROWS = NUM_FEAT + 8
F32 = jnp.float32
BF16 = jnp.bfloat16
HBM = pl.BlockSpec(memory_space=pltpu.HBM)
VMEM = pl.BlockSpec(memory_space=pltpu.VMEM)
LAST = (((1,), (1,)), ((), ()))


def call(kernel, outs, operands, scratch=(), flops=1 << 20, moved=1 << 20, space=VMEM):
    return pl.pallas_call(
        kernel,
        out_shape=outs,
        in_specs=[space] * len(operands),
        out_specs=[VMEM] * len(outs),
        scratch_shapes=list(scratch),
        compiler_params=pltpu.CompilerParams(vmem_limit_bytes=16 << 20),
        cost_estimate=pl.CostEstimate(flops=flops, bytes_accessed=moved, transcendentals=0),
    )(*operands)


def hbm(array):
    return pltpu.with_memory_space_constraint(array, pltpu.HBM)


def dot_last(left, right):
    return lax.dot_general(left, right, LAST, preferred_element_type=F32)


def own_share():
    return lax.axis_index("ctx") & PIECES - 1


def pack_kernel(weight_ref, tokens_ref, sent_ref, last_ref, sems):
    width = sent_ref.shape[1]
    start = pl.multiple_of(own_share() * width, LANES)
    weights = pltpu.make_async_copy(weight_ref.at[:, pl.ds(start, width)], sent_ref, sems.at[0])
    last = pltpu.make_async_copy(
        tokens_ref.at[tokens_ref.shape[0] - HALO :, :], last_ref, sems.at[1]
    )
    weights.start()
    last.start()
    weights.wait()
    last.wait()


def own_kernel(tail_ref, tokens_ref, paired_ref, weight_ref, halo_ref, own_ref, other_ref):
    weight = weight_ref[...]
    own_ref[...] = dot_last(weight, tokens_ref[...]).astype(BF16)
    other_ref[...] = dot_last(weight, paired_ref[...]).astype(BF16)
    padded = jnp.concatenate(
        [jnp.zeros((halo_ref.shape[1] - HALO, tail_ref.shape[1]), BF16), tail_ref[...]], axis=0
    )
    halo_ref[...] = dot_last(weight, padded).astype(BF16)


def gathered(share, tokens_ref, pieces):
    depth = pieces[0].shape[1]
    total = None
    for index, piece in zip((0, 2, 4, 6, 1, 3, 5, 7), pieces):
        start = pl.multiple_of((share ^ index) * depth, depth)
        part = dot_last(piece[...], tokens_ref[:, pl.ds(start, depth)])
        total = part if total is None else total + part
    return total.astype(BF16)


def other_heads_kernel(tokens_ref, *refs):
    share = own_share()
    count = len(refs) // (PIECES + 1)
    for turn in range(count):
        refs[PIECES * count + turn][...] = gathered(
            share, tokens_ref, refs[PIECES * turn : PIECES * turn + PIECES]
        )


def features(raw, weighted):
    scale = 1.0 / (math.sqrt(2.0) * math.sqrt(FEAT))
    parts = []
    for shift in range(FEAT // 2 + 1):
        pair = raw * (pltpu.roll(raw, shift, 0) if shift else raw) * scale
        if shift == FEAT // 2:
            pair = pair[: FEAT // 2]
        pair = pair.astype(BF16).astype(F32)
        parts.append(pair * 2.0 if weighted and shift else pair)
    parts.append(raw * FEAT ** (-0.25))
    row = lax.broadcasted_iota(jnp.int32, (8, raw.shape[1]), 0)
    parts.append(jnp.where(row == 0, 1.0, 0.0).astype(F32))
    return jnp.concatenate(parts, axis=0).astype(BF16)


def feature_kernel(conv_ref, halo_ref, *refs):
    count = len(refs) - 5
    head = lax.axis_index("tp")
    places = []
    for turn in range(count // 2):
        source = (head + count - 2 * turn) % count
        places += [source, source ^ 1]
    blocks = refs[:count]
    query_ref, key_ref, value_ref, state_ref, wide = refs[count:]
    width = halo_ref.shape[1]
    local_rows = width * count
    wide[:, :width] = halo_ref[...].astype(F32)
    for index, block in enumerate(blocks):
        start = pl.multiple_of((places[index] + 1) * width, LANES)
        wide[:, pl.ds(start, width)] = block[...].astype(F32)
    padded = wide[...]
    convolved = jnp.zeros((padded.shape[0], local_rows), F32)
    taps = conv_ref[...].T
    for offset in range(taps.shape[1]):
        moved = pltpu.roll(padded, offset, 1) if offset else padded
        convolved += taps[:, offset : offset + 1] * moved[:, width:]
    value = convolved[2 * FEAT :].astype(BF16)
    value_ref[...] = value
    query_ref[...] = convolved[:FEAT]
    key = features(convolved[FEAT : 2 * FEAT], True)
    key_ref[...] = key
    state_ref[:NUM_FEAT, :] = dot_last(key, value)
    total = dot_last(jnp.ones((8, local_rows), BF16), key)
    lanes = state_ref.shape[1]
    rest = NUM_FEAT - lanes
    more = jnp.concatenate([total[:, lanes:], jnp.zeros((8, lanes - rest), F32)], axis=1)
    row = lax.broadcasted_iota(jnp.int32, (8, lanes), 0)
    state_ref[NUM_FEAT:, :] = jnp.where(row == 0, total[:, :lanes], jnp.where(row == 1, more, 0.0))


def inner_kernel(raw_ref, key_ref, value_ref, query_ref, numerator_ref, denominator_ref):
    query_ref[...] = features(raw_ref[...], False).T
    local_rows = query_ref.shape[0]
    width = value_ref.shape[0]
    step = LANES
    for start in range(0, local_rows, step):
        size = start + step
        scores = jnp.dot(query_ref[start:size, :], key_ref[:, :size], preferred_element_type=F32)
        row = lax.broadcasted_iota(jnp.int32, (step, size), 0) + start
        column = lax.broadcasted_iota(jnp.int32, (step, size), 1)
        scores = jnp.where(row >= column, scores, 0.0)
        numerator_ref[start:size, :] = dot_last(scores.astype(BF16), value_ref[:, :size])
        denominator_ref[start:size, :] = jnp.broadcast_to(
            jnp.sum(scores, axis=1, keepdims=True), (step, width)
        )


def finish_kernel(query_ref, numerator_ref, denominator_ref, *refs):
    states, out_ref = refs[:-1], refs[-1]
    state = states[0][...]
    for other in states[1:]:
        state += other[...]
    width = numerator_ref.shape[1]
    query = query_ref[...]
    rest = state[:NUM_FEAT, :]
    parts = []
    for _ in range(3):
        parts.append(rest.astype(BF16))
        rest = rest - parts[-1].astype(F32)
    product = jnp.dot(query, jnp.concatenate(parts, axis=1), preferred_element_type=F32)
    numerator = numerator_ref[...]
    for start in range(0, 3 * width, width):
        numerator += product[:, start : start + width]
    totals = jnp.concatenate(
        [state[NUM_FEAT : NUM_FEAT + 1, :], state[NUM_FEAT + 1 : NUM_FEAT + 2, : NUM_FEAT - width]], axis=1
    )
    denominator = denominator_ref[:, :1] + jnp.sum(query.astype(F32) * totals, axis=1, keepdims=True)
    out_ref[...] = (numerator / denominator).astype(BF16)


def per_device(ctx, tp, tokens, projection, conv_weight):
    both = ("ctx", "tp")
    rows, depth = tokens.shape
    row_width = projection.shape[1]
    val_width = row_width - 2 * FEAT
    local_rows = rows * tp
    turns = range(1, tp // 2)
    me = lax.axis_index("ctx")
    weight = projection.T
    piece = depth // PIECES

    def swap(array, bit):
        return lax.ppermute(array, "ctx", [(i, i ^ bit) for i in range(ctx)])

    mine, last_rows = call(
        pack_kernel,
        [
            jax.ShapeDtypeStruct((row_width, piece), BF16),
            jax.ShapeDtypeStruct((HALO, depth), BF16),
        ],
        [hbm(weight), hbm(tokens)],
        [pltpu.SemaphoreType.DMA((2,))],
        space=HBM,
    )
    pieces = []
    for turn in turns:
        first = lax.ppermute(mine, "tp", [((z + 2 * turn) % tp, z) for z in range(tp)])
        parts = [first] + [swap(first, bits) for bits in (2, 4, 6)]
        pieces += parts + [swap(part, 1) for part in parts]
    paired = lax.ppermute(tokens, "tp", [(z, z ^ 1) for z in range(tp)])

    pairs = [((c - 1) * tp + tp - 1, c * tp + tp - 1) for c in range(1, ctx)]
    ahead = lax.ppermute(last_rows, both, pairs)
    tail = ahead
    for z in range(tp - 1):
        pairs = [(c * tp + tp - 1, c * tp + z) for c in range(1, ctx)]
        tail = tail + lax.ppermute(ahead, both, pairs)

    shape = jax.ShapeDtypeStruct((row_width, rows), BF16)
    work = 2 * rows * depth * row_width
    halo, own, other = call(own_kernel, [shape] * 3, [tail, tokens, paired, weight], flops=3 * work)
    early = call(other_heads_kernel, [shape] * len(turns), [tokens] + pieces, flops=work)
    late = call(other_heads_kernel, [shape] * len(turns), [paired] + pieces, flops=work)
    blocks = [own, other]
    for turn, one, two in zip(turns, early, late):
        pairs = [(z, (z + 2 * turn) % tp) for z in range(tp)]
        blocks += [lax.ppermute(one, "tp", pairs), lax.ppermute(two, "tp", pairs)]
    raw, key, value, state = call(
        feature_kernel,
        [
            jax.ShapeDtypeStruct((FEAT, local_rows), F32),
            jax.ShapeDtypeStruct((NUM_FEAT, local_rows), BF16),
            jax.ShapeDtypeStruct((val_width, local_rows), BF16),
            jax.ShapeDtypeStruct((STATE_ROWS, val_width), F32),
        ],
        [conv_weight, halo] + blocks,
        [pltpu.VMEM((row_width, rows + local_rows), F32)],
    )
    query, numerator, denominator = call(
        inner_kernel,
        [jax.ShapeDtypeStruct((local_rows, NUM_FEAT), BF16)]
        + [jax.ShapeDtypeStruct((local_rows, val_width), F32)] * 2,
        [raw, key, value],
        flops=2 * local_rows * local_rows * (NUM_FEAT + val_width),
    )
    received = swap(state, 1)
    terms = [jnp.where(me % 2 == 1, received, 0.0)]
    total = state + received
    bit = 2
    while bit < ctx:
        radix = min(4, ctx // bit)
        last = bit * radix >= ctx
        digit = me // bit % radix
        parts = []
        for delta in range(1, radix):
            pairs = [(c, c ^ delta * bit) for c in range(ctx)]
            parts.append(lax.ppermute(total, "ctx", pairs))
            terms.append(jnp.where(digit > digit ^ delta, parts[-1], 0.0))
        if not last:
            total = functools.reduce(jnp.add, parts, total)
        bit *= radix
    return call(
        finish_kernel,
        [jax.ShapeDtypeStruct((local_rows, val_width), BF16)],
        [query, numerator, denominator] + terms,
        flops=6 * local_rows * NUM_FEAT * val_width,
    )[0]


def solution(mesh):
    ctx, tp = mesh.shape["ctx"], mesh.shape["tp"]
    if tp % 2 or tp < 4 or ctx < 8 or ctx & (ctx - 1):
        raise ValueError("unsupported mesh")

    def body(*arrays):
        return per_device(ctx, tp, *arrays)

    return jax.shard_map(
        body,
        mesh=mesh,
        in_specs=(P(("ctx", "tp"), None), P(None, "tp"), P(None, "tp")),
        out_specs=P("ctx", "tp"),
        check_vma=False,
    )
```

profile of v0, /device:TPU:0, one launch (start us, length us, event | category | flops | bytes accessed | tf_op | source)
XLA Modules:
  0.0 48.8 jit_solution(14839798254091531486)
XLA Ops:
  0.0 3.1 %collective-permute-start.4 = (bf16[128,2048]{1,0:T(8,128)(2,1)}, bf16[128,2048]{1,0:T(8,128)(2,1)S(1)}, u32[]{:S(2)}, u32[]{:S(2)}) collective-permute-start(bf16[128,2048]{1,0:T(8,128)(2,1)} %tokens_ref.5), channel_id=1, source_target_pairs={{0,1},{1,0},{2,3},{3,2},{4,5},{5,4},{6,7},{7,6},{8,9},{9,8},{10,11... | collective-permute-start | bytes 1572872 | tf_op jit(solution)/shard_map/ppermute | solution.py:211
  3.1 1.0 %shard_map.37 = (bf16[160,256]{1,0:T(8,128)(2,1)S(1)}, bf16[8,2048]{1,0:T(8,128)(2,1)S(1)}) custom-call(bf16[160,2048]{1,0:T(8,128)(2,1)} %bitcast.1, bf16[128,2048]{1,0:T(8,128)(2,1)} %tokens_ref.5), custom_call_target="tpu_custom_call" | custom-call | flops 1048576 | bytes 1048576 | tf_op jit(solution)/shard_map/pallas_call | solution.py:27
  4.0 2.7 %collective-permute-start.5 = (bf16[160,256]{1,0:T(8,128)(2,1)S(1)}, bf16[160,256]{1,0:T(8,128)(2,1)S(1)}, u32[]{:S(2)}, u32[]{:S(2)}) collective-permute-start(bf16[160,256]{1,0:T(8,128)(2,1)S(1)} %get-tuple-element.21), channel_id=1, source_target_pairs={{2,0},{3,1},{0,2},{1,3},{6,4},{7,5},{4,6},{5,7},{10,8},{11,9},{8,1... | collective-permute-start | bytes 245768 | tf_op jit(solution)/shard_map/ppermute | solution.py:208
  6.7 9.5 %collective-permute-done.5.refs_0_ = bf16[160,256]{1,0:T(8,128)(2,1)S(1)} collective-permute-done((bf16[160,256]{1,0:T(8,128)(2,1)S(1)}, bf16[160,256]{1,0:T(8,128)(2,1)S(1)}, u32[]{:S(2)}, u32[]{:S(2)}) %collective-permute-start.5) | collective-permute-done | bytes 81952 | tf_op jit(solution)/shard_map/ppermute | solution.py:208
  16.2 1.5 %collective-permute-start.6 = (bf16[160,256]{1,0:T(8,128)(2,1)S(1)}, bf16[160,256]{1,0:T(8,128)(2,1)S(1)}, u32[]{:S(2)}, u32[]{:S(2)}) collective-permute-start(bf16[160,256]{1,0:T(8,128)(2,1)S(1)} %collective-permute-done.5.refs_0_), channel_id=1, source_target_pairs={{0,8},{4,12},{8,0},{12,4},{16,24},{20,28},{24,16},{28,20},{1,9},{5... | collective-permute-start | bytes 245768 | tf_op jit(solution)/shard_map/ppermute | solution.py:194
  17.7 1.5 %collective-permute-start.7 = (bf16[160,256]{1,0:T(8,128)(2,1)S(1)}, bf16[160,256]{1,0:T(8,128)(2,1)S(1)}, u32[]{:S(2)}, u32[]{:S(2)}) collective-permute-start(bf16[160,256]{1,0:T(8,128)(2,1)S(1)} %collective-permute-done.5.refs_0_), channel_id=1, source_target_pairs={{0,16},{4,20},{8,24},{12,28},{16,0},{20,4},{24,8},{28,12},{1,17},{... | collective-permute-start | bytes 245768 | tf_op jit(solution)/shard_map/ppermute | solution.py:194
  20.4 0.7 %collective-permute-done.6.refs_1_ = bf16[160,256]{1,0:T(8,128)(2,1)S(1)} collective-permute-done((bf16[160,256]{1,0:T(8,128)(2,1)S(1)}, bf16[160,256]{1,0:T(8,128)(2,1)S(1)}, u32[]{:S(2)}, u32[]{:S(2)}) %collective-permute-start.6) | collective-permute-done | bytes 81952 | tf_op jit(solution)/shard_map/ppermute | solution.py:194
  21.1 1.8 %collective-permute-done.7.refs_2_ = bf16[160,256]{1,0:T(8,128)(2,1)S(1)} collective-permute-done((bf16[160,256]{1,0:T(8,128)(2,1)S(1)}, bf16[160,256]{1,0:T(8,128)(2,1)S(1)}, u32[]{:S(2)}, u32[]{:S(2)}) %collective-permute-start.7) | collective-permute-done | bytes 81952 | tf_op jit(solution)/shard_map/ppermute | solution.py:194
  22.9 1.6 %collective-permute-done.8.refs_3_ = bf16[160,256]{1,0:T(8,128)(2,1)S(1)} collective-permute-done((bf16[160,256]{1,0:T(8,128)(2,1)S(1)}, bf16[160,256]{1,0:T(8,128)(2,1)S(1)}, u32[]{:S(2)}, u32[]{:S(2)}) %collective-permute-start.8) | collective-permute-done | bytes 81952 | tf_op jit(solution)/shard_map/ppermute | solution.py:194
  24.6 0.7 %collective-permute-start.3 = (bf16[8,2048]{1,0:T(8,128)(2,1)S(1)}, bf16[8,2048]{1,0:T(8,128)(2,1)S(1)}, u32[]{:S(2)}, u32[]{:S(2)}) collective-permute-start(bf16[8,2048]{1,0:T(8,128)(2,1)S(1)} %collective-permute-done), channel_id=1, source_target_pairs={{7,6},{11,10},{15,14},{19,18},{23,22},{27,26},{31,30}} | collective-permute-start | bytes 98312 | tf_op jit(solution)/shard_map/ppermute | solution.py:218
  25.2 0.7 %collective-permute-start.2 = (bf16[8,2048]{1,0:T(8,128)(2,1)S(1)}, bf16[8,2048]{1,0:T(8,128)(2,1)S(1)}, u32[]{:S(2)}, u32[]{:S(2)}) collective-permute-start(bf16[8,2048]{1,0:T(8,128)(2,1)S(1)} %collective-permute-done), channel_id=1, source_target_pairs={{7,5},{11,9},{15,13},{19,17},{23,21},{27,25},{31,29}} | collective-permute-start | bytes 98312 | tf_op jit(solution)/shard_map/ppermute | solution.py:218
  25.9 0.7 %collective-permute-start.1 = (bf16[8,2048]{1,0:T(8,128)(2,1)S(1)}, bf16[8,2048]{1,0:T(8,128)(2,1)S(1)}, u32[]{:S(2)}, u32[]{:S(2)}) collective-permute-start(bf16[8,2048]{1,0:T(8,128)(2,1)S(1)} %collective-permute-done), channel_id=1, source_target_pairs={{7,4},{11,8},{15,12},{19,16},{23,20},{27,24},{31,28}} | collective-permute-start | bytes 98312 | tf_op jit(solution)/shard_map/ppermute | solution.py:218
  27.0 3.4 %collective-permute-start.13 = (bf16[160,128]{1,0:T(8,128)(2,1)S(1)}, bf16[160,128]{1,0:T(8,128)(2,1)S(1)}, u32[]{:S(2)}, u32[]{:S(2)}) collective-permute-start(bf16[160,128]{1,0:T(8,128)(2,1)S(1)} %shard_map.39), channel_id=1, source_target_pairs={{0,2},{1,3},{2,0},{3,1},{4,6},{5,7},{6,4},{7,5},{8,10},{9,11},{10,... | collective-permute-start | bytes 122888 | tf_op jit(solution)/shard_map/ppermute | solution.py:228
  30.9 0.7 %shard_map.38 = (bf16[160,128]{1,0:T(8,128)(2,1)S(1)}, bf16[160,128]{1,0:T(8,128)(2,1)S(1)}, bf16[160,128]{1,0:T(8,128)(2,1)S(1)}) custom-call(bf16[8,2048]{1,0:T(8,128)(2,1)S(1)} %add_add_fusion.tail_ref, bf16[128,2048]{1,0:T(8,128)(2,1)S(1)} %copy-done, bf16[128,2048]{1,0:T(8,128)(2,1)S(1)} %collective-permute-done.4.paired_ref.tokens_ref, ...), custom_call_target="tpu_custom_call" | custom-call | flops 251658240 | bytes 1048576 | tf_op jit(solution)/shard_map/pallas_call | solution.py:27
  31.6 0.8 %collective-permute-done.13.refs_2_ = bf16[160,128]{1,0:T(8,128)(2,1)S(1)} collective-permute-done((bf16[160,128]{1,0:T(8,128)(2,1)S(1)}, bf16[160,128]{1,0:T(8,128)(2,1)S(1)}, u32[]{:S(2)}, u32[]{:S(2)}) %collective-permute-start.13) | collective-permute-done | bytes 40992 | tf_op jit(solution)/shard_map/ppermute | solution.py:228
  32.4 4.7 %collective-permute-done.14.refs_3_ = bf16[160,128]{1,0:T(8,128)(2,1)S(1)} collective-permute-done((bf16[160,128]{1,0:T(8,128)(2,1)S(1)}, bf16[160,128]{1,0:T(8,128)(2,1)S(1)}, u32[]{:S(2)}, u32[]{:S(2)}) %collective-permute-start.14) | collective-permute-done | bytes 40992 | tf_op jit(solution)/shard_map/ppermute | solution.py:228
  37.1 0.8 %shard_map.41 = (f32[16,512]{1,0:T(8,128)S(1)}, bf16[160,512]{1,0:T(8,128)(2,1)S(1)}, bf16[128,512]{1,0:T(8,128)(2,1)S(1)}, f32[168,128]{1,0:T(8,128)S(1)}) custom-call(f32[4,160]{1,0:T(4,128)S(1)} %copy-done.2, bf16[160,128]{1,0:T(8,128)(2,1)S(1)} %get-tuple-element.18.halo_ref, bf16[160,128]{1,0:T(8,128)(2,1)S(1)} %get-tuple-element.19.refs_0_, ...), custom_call_target="tpu_custom_call" | custom-call | flops 1048576 | bytes 1048576 | tf_op jit(solution)/shard_map/pallas_call | solution.py:27
  38.0 1.2 %collective-permute-done.15 = f32[168,128]{1,0:T(8,128)S(1)} collective-permute-done((f32[168,128]{1,0:T(8,128)S(1)}, f32[168,128]{1,0:T(8,128)S(1)}, u32[]{:S(2)}, u32[]{:S(2)}) %collective-permute-start.15) | collective-permute-done | bytes 86048 | tf_op jit(solution)/shard_map/ppermute | solution.py:194
  39.2 1.4 %collective-permute-start.16 = (f32[168,128]{1,0:T(8,128)S(1)}, f32[168,128]{1,0:T(8,128)S(1)}, u32[]{:S(2)}, u32[]{:S(2)}) collective-permute-start(f32[168,128]{1,0:T(8,128)S(1)} %get-tuple-element.29), channel_id=1, source_target_pairs={{0,8},{4,12},{8,0},{12,4},{16,24},{20,28},{24,16},{28,20},{1,9},{5... | collective-permute-start | bytes 258056 | tf_op jit(solution)/shard_map/ppermute | solution.py:258
  40.7 0.7 %shard_map.42 = (bf16[512,160]{1,0:T(8,128)(2,1)S(1)}, f32[512,128]{1,0:T(8,128)S(1)}, f32[512,128]{1,0:T(8,128)S(1)}) custom-call(f32[16,512]{1,0:T(8,128)S(1)} %get-tuple-element.22.raw_ref, bf16[160,512]{1,0:T(8,128)(2,1)S(1)} %get-tuple-element.23.key_ref, bf16[128,512]{1,0:T(8,128)(2,1)S(1)} %get-tuple-element.24.value_ref), custom_call_target="tpu_custom_call" | custom-call | flops 150994944 | bytes 1048576 | tf_op jit(solution)/shard_map/pallas_call | solution.py:27
  41.3 0.8 %collective-permute-start.17 = (f32[168,128]{1,0:T(8,128)S(1)}, f32[168,128]{1,0:T(8,128)S(1)}, u32[]{:S(2)}, u32[]{:S(2)}) collective-permute-start(f32[168,128]{1,0:T(8,128)S(1)} %get-tuple-element.29), channel_id=1, source_target_pairs={{0,16},{4,20},{8,24},{12,28},{16,0},{20,4},{24,8},{28,12},{1,17},{... | collective-permute-start | bytes 258056 | tf_op jit(solution)/shard_map/ppermute | solution.py:258
  42.2 1.4 %collective-permute-start.18 = (f32[168,128]{1,0:T(8,128)S(1)}, f32[168,128]{1,0:T(8,128)S(1)}, u32[]{:S(2)}, u32[]{:S(2)}) collective-permute-start(f32[168,128]{1,0:T(8,128)S(1)} %get-tuple-element.29), channel_id=1, source_target_pairs={{0,24},{4,28},{8,16},{12,20},{16,8},{20,12},{24,0},{28,4},{1,25},{... | collective-permute-start | bytes 258056 | tf_op jit(solution)/shard_map/ppermute | solution.py:258
  43.9 3.8 %collective-permute-done.17 = f32[168,128]{1,0:T(8,128)S(1)} collective-permute-done((f32[168,128]{1,0:T(8,128)S(1)}, f32[168,128]{1,0:T(8,128)S(1)}, u32[]{:S(2)}, u32[]{:S(2)}) %collective-permute-start.17) | collective-permute-done | bytes 86048 | tf_op jit(solution)/shard_map/ppermute | solution.py:258
  47.8 1.0 %shard_map.43 = bf16[512,128]{1,0:T(8,128)(2,1)} custom-call(bf16[512,160]{1,0:T(8,128)(2,1)S(1)} %get-tuple-element.25.query_ref, f32[512,128]{1,0:T(8,128)S(1)} %get-tuple-element.26.numerator_ref, f32[512,128]{1,0:T(8,128)S(1)} %get-tuple-element.27.denominator_ref, f32[168,128]{1,0:T(8,128)S(1)} %get-tuple-element.30.refs_0_, ...), custom_call_target="tpu_custom_call" | custom-call | flops 62914560 | bytes 1048576 | tf_op jit(solution)/shard_map/pallas_call | solution.py:27
  (32 shorter events, 2.6 us)
Async XLA Ops:
  0.0 30.4 %collective-permute-start.4 = (bf16[128,2048]{1,0:T(8,128)(2,1)}, bf16[128,2048]{1,0:T(8,128)(2,1)S(1)}, u32[]{:S(2)}, u32[]{:S(2)}) collective-permute-start(bf16[128,2048]{1,0:T(8,128)(2,1)} %tokens_ref.5), channel_id=1, source_target_pairs={{0,1},{1,0},{2,3},{3,2},{4,5},{5,4},{6,7},{7,6},{8,9},{9,8},{10,11... | collective-permute-start | bytes 1572872 | tf_op jit(solution)/shard_map/ppermute | solution.py:211
  3.1 23.5 %copy-start = (bf16[128,2048]{1,0:T(8,128)(2,1)S(1)}, bf16[128,2048]{1,0:T(8,128)(2,1)}, u32[]{:S(2)}) copy-start(bf16[128,2048]{1,0:T(8,128)(2,1)} %tokens_ref.5) | copy-start | bytes 1572868
  4.0 12.2 %collective-permute-start.5 = (bf16[160,256]{1,0:T(8,128)(2,1)S(1)}, bf16[160,256]{1,0:T(8,128)(2,1)S(1)}, u32[]{:S(2)}, u32[]{:S(2)}) collective-permute-start(bf16[160,256]{1,0:T(8,128)(2,1)S(1)} %get-tuple-element.21), channel_id=1, source_target_pairs={{2,0},{3,1},{0,2},{1,3},{6,4},{7,5},{4,6},{5,7},{10,8},{11,9},{8,1... | collective-permute-start | bytes 245768 | tf_op jit(solution)/shard_map/ppermute | solution.py:208
  16.2 4.9 %collective-permute-start.6 = (bf16[160,256]{1,0:T(8,128)(2,1)S(1)}, bf16[160,256]{1,0:T(8,128)(2,1)S(1)}, u32[]{:S(2)}, u32[]{:S(2)}) collective-permute-start(bf16[160,256]{1,0:T(8,128)(2,1)S(1)} %collective-permute-done.5.refs_0_), channel_id=1, source_target_pairs={{0,8},{4,12},{8,0},{12,4},{16,24},{20,28},{24,16},{28,20},{1,9},{5... | collective-permute-start | bytes 245768 | tf_op jit(solution)/shard_map/ppermute | solution.py:194
  17.7 5.3 %collective-permute-start.7 = (bf16[160,256]{1,0:T(8,128)(2,1)S(1)}, bf16[160,256]{1,0:T(8,128)(2,1)S(1)}, u32[]{:S(2)}, u32[]{:S(2)}) collective-permute-start(bf16[160,256]{1,0:T(8,128)(2,1)S(1)} %collective-permute-done.5.refs_0_), channel_id=1, source_target_pairs={{0,16},{4,20},{8,24},{12,28},{16,0},{20,4},{24,8},{28,12},{1,17},{... | collective-permute-start | bytes 245768 | tf_op jit(solution)/shard_map/ppermute | solution.py:194
  19.2 5.3 %collective-permute-start.8 = (bf16[160,256]{1,0:T(8,128)(2,1)S(1)}, bf16[160,256]{1,0:T(8,128)(2,1)S(1)}, u32[]{:S(2)}, u32[]{:S(2)}) collective-permute-start(bf16[160,256]{1,0:T(8,128)(2,1)S(1)} %collective-permute-done.5.refs_0_), channel_id=1, source_target_pairs={{0,24},{4,28},{8,16},{12,20},{16,8},{20,12},{24,0},{28,4},{1,25},{... | collective-permute-start | bytes 245768 | tf_op jit(solution)/shard_map/ppermute | solution.py:194
  19.7 0.7 %collective-permute-start = (bf16[8,2048]{1,0:T(8,128)(2,1)S(1)}, bf16[8,2048]{1,0:T(8,128)(2,1)S(1)}, u32[]{:S(2)}, u32[]{:S(2)}) collective-permute-start(bf16[8,2048]{1,0:T(8,128)(2,1)S(1)} %get-tuple-element.17), channel_id=1, source_target_pairs={{3,7},{7,11},{11,15},{15,19},{19,23},{23,27},{27,31}} | collective-permute-start | bytes 98312 | tf_op jit(solution)/shard_map/ppermute | solution.py:214
  20.4 4.2 %collective-permute-start.9 = (bf16[160,256]{1,0:T(8,128)(2,1)S(1)}, bf16[160,256]{1,0:T(8,128)(2,1)S(1)}, u32[]{:S(2)}, u32[]{:S(2)}) collective-permute-start(bf16[160,256]{1,0:T(8,128)(2,1)S(1)} %collective-permute-done.5.refs_0_), channel_id=1, source_target_pairs={{0,4},{4,0},{8,12},{12,8},{16,20},{20,16},{24,28},{28,24},{1,5},{5... | collective-permute-start | bytes 245768 | tf_op jit(solution)/shard_map/ppermute | solution.py:194
  21.1 4.1 %collective-permute-start.10 = (bf16[160,256]{1,0:T(8,128)(2,1)S(1)}, bf16[160,256]{1,0:T(8,128)(2,1)S(1)}, u32[]{:S(2)}, u32[]{:S(2)}) collective-permute-start(bf16[160,256]{1,0:T(8,128)(2,1)S(1)} %collective-permute-done.6.refs_1_), channel_id=1, source_target_pairs={{0,4},{4,0},{8,12},{12,8},{16,20},{20,16},{24,28},{28,24},{1,5},{5... | collective-permute-start | bytes 245768 | tf_op jit(solution)/shard_map/ppermute | solution.py:194
  22.9 3.0 %collective-permute-start.11 = (bf16[160,256]{1,0:T(8,128)(2,1)S(1)}, bf16[160,256]{1,0:T(8,128)(2,1)S(1)}, u32[]{:S(2)}, u32[]{:S(2)}) collective-permute-start(bf16[160,256]{1,0:T(8,128)(2,1)S(1)} %collective-permute-done.7.refs_2_), channel_id=1, source_target_pairs={{0,4},{4,0},{8,12},{12,8},{16,20},{20,16},{24,28},{28,24},{1,5},{5... | collective-permute-start | bytes 245768 | tf_op jit(solution)/shard_map/ppermute | solution.py:194
  24.6 2.0 %collective-permute-start.12 = (bf16[160,256]{1,0:T(8,128)(2,1)S(1)}, bf16[160,256]{1,0:T(8,128)(2,1)S(1)}, u32[]{:S(2)}, u32[]{:S(2)}) collective-permute-start(bf16[160,256]{1,0:T(8,128)(2,1)S(1)} %collective-permute-done.8.refs_3_), channel_id=1, source_target_pairs={{0,4},{4,0},{8,12},{12,8},{16,20},{20,16},{24,28},{28,24},{1,5},{5... | collective-permute-start | bytes 245768 | tf_op jit(solution)/shard_map/ppermute | solution.py:194
  24.6 6.3 %collective-permute-start.3 = (bf16[8,2048]{1,0:T(8,128)(2,1)S(1)}, bf16[8,2048]{1,0:T(8,128)(2,1)S(1)}, u32[]{:S(2)}, u32[]{:S(2)}) collective-permute-start(bf16[8,2048]{1,0:T(8,128)(2,1)S(1)} %collective-permute-done), channel_id=1, source_target_pairs={{7,6},{11,10},{15,14},{19,18},{23,22},{27,26},{31,30}} | collective-permute-start | bytes 98312 | tf_op jit(solution)/shard_map/ppermute | solution.py:218
  25.2 5.6 %collective-permute-start.2 = (bf16[8,2048]{1,0:T(8,128)(2,1)S(1)}, bf16[8,2048]{1,0:T(8,128)(2,1)S(1)}, u32[]{:S(2)}, u32[]{:S(2)}) collective-permute-start(bf16[8,2048]{1,0:T(8,128)(2,1)S(1)} %collective-permute-done), channel_id=1, source_target_pairs={{7,5},{11,9},{15,13},{19,17},{23,21},{27,25},{31,29}} | collective-permute-start | bytes 98312 | tf_op jit(solution)/shard_map/ppermute | solution.py:218
  25.9 5.0 %collective-permute-start.1 = (bf16[8,2048]{1,0:T(8,128)(2,1)S(1)}, bf16[8,2048]{1,0:T(8,128)(2,1)S(1)}, u32[]{:S(2)}, u32[]{:S(2)}) collective-permute-start(bf16[8,2048]{1,0:T(8,128)(2,1)S(1)} %collective-permute-done), channel_id=1, source_target_pairs={{7,4},{11,8},{15,12},{19,16},{23,20},{27,24},{31,28}} | collective-permute-start | bytes 98312 | tf_op jit(solution)/shard_map/ppermute | solution.py:218
  27.0 3.9 %copy-start.1 = (bf16[2048,160]{0,1:T(8,128)(2,1)S(1)}, bf16[2048,160]{0,1:T(8,128)(2,1)}, u32[]{:S(2)}) copy-start(bf16[2048,160]{0,1:T(8,128)(2,1)} %param.4) | copy-start | bytes 1966084
  27.0 5.4 %collective-permute-start.13 = (bf16[160,128]{1,0:T(8,128)(2,1)S(1)}, bf16[160,128]{1,0:T(8,128)(2,1)S(1)}, u32[]{:S(2)}, u32[]{:S(2)}) collective-permute-start(bf16[160,128]{1,0:T(8,128)(2,1)S(1)} %shard_map.39), channel_id=1, source_target_pairs={{0,2},{1,3},{2,0},{3,1},{4,6},{5,7},{6,4},{7,5},{8,10},{9,11},{10,... | collective-permute-start | bytes 122888 | tf_op jit(solution)/shard_map/ppermute | solution.py:228
  30.8 6.3 %collective-permute-start.14 = (bf16[160,128]{1,0:T(8,128)(2,1)S(1)}, bf16[160,128]{1,0:T(8,128)(2,1)S(1)}, u32[]{:S(2)}, u32[]{:S(2)}) collective-permute-start(bf16[160,128]{1,0:T(8,128)(2,1)S(1)} %shard_map.40), channel_id=1, source_target_pairs={{0,2},{1,3},{2,0},{3,1},{4,6},{5,7},{6,4},{7,5},{8,10},{9,11},{10,... | collective-permute-start | bytes 122888 | tf_op jit(solution)/shard_map/ppermute | solution.py:228
  31.6 5.5 %copy-start.2 = (f32[4,160]{1,0:T(4,128)S(1)}, f32[4,160]{1,0:T(4,128)}, u32[]{:S(2)}) copy-start(f32[4,160]{1,0:T(4,128)} %conv_ref.1) | copy-start | bytes 7684
  37.9 1.3 %collective-permute-start.15 = (f32[168,128]{1,0:T(8,128)S(1)}, f32[168,128]{1,0:T(8,128)S(1)}, u32[]{:S(2)}, u32[]{:S(2)}) collective-permute-start(f32[168,128]{1,0:T(8,128)S(1)} %get-tuple-element.28), channel_id=1, source_target_pairs={{0,4},{4,0},{8,12},{12,8},{16,20},{20,16},{24,28},{28,24},{1,5},{5... | collective-permute-start | bytes 258056 | tf_op jit(solution)/shard_map/ppermute | solution.py:194
  39.2 4.7 %collective-permute-start.16 = (f32[168,128]{1,0:T(8,128)S(1)}, f32[168,128]{1,0:T(8,128)S(1)}, u32[]{:S(2)}, u32[]{:S(2)}) collective-permute-start(f32[168,128]{1,0:T(8,128)S(1)} %get-tuple-element.29), channel_id=1, source_target_pairs={{0,8},{4,12},{8,0},{12,4},{16,24},{20,28},{24,16},{28,20},{1,9},{5... | collective-permute-start | bytes 258056 | tf_op jit(solution)/shard_map/ppermute | solution.py:258
  41.3 6.4 %collective-permute-start.17 = (f32[168,128]{1,0:T(8,128)S(1)}, f32[168,128]{1,0:T(8,128)S(1)}, u32[]{:S(2)}, u32[]{:S(2)}) collective-permute-start(f32[168,128]{1,0:T(8,128)S(1)} %get-tuple-element.29), channel_id=1, source_target_pairs={{0,16},{4,20},{8,24},{12,28},{16,0},{20,4},{24,8},{28,12},{1,17},{... | collective-permute-start | bytes 258056 | tf_op jit(solution)/shard_map/ppermute | solution.py:258
  42.2 5.6 %collective-permute-start.18 = (f32[168,128]{1,0:T(8,128)S(1)}, f32[168,128]{1,0:T(8,128)S(1)}, u32[]{:S(2)}, u32[]{:S(2)}) collective-permute-start(f32[168,128]{1,0:T(8,128)S(1)} %get-tuple-element.29), channel_id=1, source_target_pairs={{0,24},{4,28},{8,16},{12,20},{16,8},{20,12},{24,0},{28,4},{1,25},{... | collective-permute-start | bytes 258056 | tf_op jit(solution)/shard_map/ppermute | solution.py:258
where the time goes:
time: 49 us; the launch traced here: 48.8 us
  waiting for transfers between devices  24.5 us (50%)
  starting transfers between devices  19.2 us (39%)
  Pallas kernels  4.77 us (10%)
    ppermute x1, waiting for transfers between devices, per_device(): lax.ppermute(mine, 'tp', [((z + 2 * turn) % tp, z) for z in range(tp)])  9.52 us
    ppermute x2, waiting for transfers between devices, per_device(): blocks += [lax.ppermute(one, 'tp', pairs), lax.ppermute(two, 'tp', pairs)]  5.47 us
    ppermute x8, waiting for transfers between devices, swap(): return lax.ppermute(array, 'ctx', [(i, i ^ bit) for i in range(ctx)])  5.3 us
    pallas_call x7, Pallas kernels, call(): pl.pallas_call(kernel, out_shape=outs, in_specs=[space] * len(operands),...  4.77 us
    ppermute x3, waiting for transfers between devices, per_device(): parts.append(lax.ppermute(total, 'ctx', pairs))  4.2 us
    ppermute x8, starting transfers between devices, swap(): return lax.ppermute(array, 'ctx', [(i, i ^ bit) for i in range(ctx)])  3.74 us
    ppermute x3, starting transfers between devices, per_device(): parts.append(lax.ppermute(total, 'ctx', pairs))  3.62 us
    ppermute x2, starting transfers between devices, per_device(): blocks += [lax.ppermute(one, 'tp', pairs), lax.ppermute(two, 'tp', pairs)]  3.55 us
  transfers between devices with their start and end apart: 19, of which 9 were waited for; matrix products, arithmetic and copies ran while one was open for 0% of the time, Pallas kernels for 6%

commit v1 on v0

--- a/solution.py
+++ b/solution.py
@@ -15,7 +15,7 @@
 LANES = 128
 QUAD_FEATS = FEAT * (FEAT + 1) // 2
 NUM_FEAT = QUAD_FEATS + FEAT + 8
-STATE_ROWS = NUM_FEAT + 8
+HALF = NUM_FEAT // 2
 F32 = jnp.float32
 BF16 = jnp.bfloat16
 HBM = pl.BlockSpec(memory_space=pltpu.HBM)
@@ -105,14 +105,14 @@
 
 
 def feature_kernel(conv_ref, halo_ref, *refs):
-    count = len(refs) - 5
+    count = len(refs) - 7
     head = lax.axis_index("tp")
     places = []
     for turn in range(count // 2):
         source = (head + count - 2 * turn) % count
         places += [source, source ^ 1]
     blocks = refs[:count]
-    query_ref, key_ref, value_ref, state_ref, wide = refs[count:]
+    query_ref, key_ref, value_ref, kept_ref, sent_ref, wide, state_ref = refs[count:]
     width = halo_ref.shape[1]
     local_rows = width * count
     wide[:, :width] = halo_ref[...].astype(F32)
@@ -130,13 +130,17 @@
     query_ref[...] = convolved[:FEAT]
     key = features(convolved[FEAT : 2 * FEAT], True)
     key_ref[...] = key
-    state_ref[:NUM_FEAT, :] = dot_last(key, value)
+    state_ref[...] = dot_last(key, value)
     total = dot_last(jnp.ones((8, local_rows), BF16), key)
     lanes = state_ref.shape[1]
     rest = NUM_FEAT - lanes
     more = jnp.concatenate([total[:, lanes:], jnp.zeros((8, lanes - rest), F32)], axis=1)
     row = lax.broadcasted_iota(jnp.int32, (8, lanes), 0)
-    state_ref[NUM_FEAT:, :] = jnp.where(row == 0, total[:, :lanes], jnp.where(row == 1, more, 0.0))
+    tail = state_ref[NUM_FEAT - 8 :, :]
+    state_ref[NUM_FEAT - 8 :, :] = jnp.where(row == 1, total[:, :lanes], jnp.where(row == 2, more, tail))
+    core = lax.axis_index("ctx") & 1
+    kept_ref[...] = state_ref[pl.ds(pl.multiple_of(core * HALF, 8), HALF), :]
+    sent_ref[...] = state_ref[pl.ds(pl.multiple_of(HALF - core * HALF, 8), HALF), :]
 
 
 def inner_kernel(raw_ref, key_ref, value_ref, query_ref, numerator_ref, denominator_ref):
@@ -156,14 +160,14 @@
         )
 
 
-def finish_kernel(query_ref, numerator_ref, denominator_ref, *refs):
-    states, out_ref = refs[:-1], refs[-1]
-    state = states[0][...]
-    for other in states[1:]:
-        state += other[...]
+def finish_kernel(query_ref, numerator_ref, denominator_ref, kept_ref, other_ref, out_ref, state_ref):
+    core = lax.axis_index("ctx") & 1
+    state_ref[pl.ds(pl.multiple_of(core * HALF, 8), HALF), :] = kept_ref[...]
+    state_ref[pl.ds(pl.multiple_of(HALF - core * HALF, 8), HALF), :] = other_ref[...]
+    state = state_ref[...]
     width = numerator_ref.shape[1]
     query = query_ref[...]
-    rest = state[:NUM_FEAT, :]
+    rest = state
     parts = []
     for _ in range(3):
         parts.append(rest.astype(BF16))
@@ -173,7 +177,7 @@
     for start in range(0, 3 * width, width):
         numerator += product[:, start : start + width]
     totals = jnp.concatenate(
-        [state[NUM_FEAT : NUM_FEAT + 1, :], state[NUM_FEAT + 1 : NUM_FEAT + 2, : NUM_FEAT - width]], axis=1
+        [state[NUM_FEAT - 7 : NUM_FEAT - 6, :], state[NUM_FEAT - 6 : NUM_FEAT - 5, : NUM_FEAT - width]], axis=1
     )
     denominator = denominator_ref[:, :1] + jnp.sum(query.astype(F32) * totals, axis=1, keepdims=True)
     out_ref[...] = (numerator / denominator).astype(BF16)
@@ -210,12 +214,11 @@
         pieces += parts + [swap(part, 1) for part in parts]
     paired = lax.ppermute(tokens, "tp", [(z, z ^ 1) for z in range(tp)])
 
-    pairs = [((c - 1) * tp + tp - 1, c * tp + tp - 1) for c in range(1, ctx)]
-    ahead = lax.ppermute(last_rows, both, pairs)
-    tail = ahead
-    for z in range(tp - 1):
-        pairs = [(c * tp + tp - 1, c * tp + z) for c in range(1, ctx)]
-        tail = tail + lax.ppermute(ahead, both, pairs)
+    tail = None
+    for z in range(tp):
+        pairs = [((c - 1) * tp + tp - 1, c * tp + z) for c in range(1, ctx)]
+        part = lax.ppermute(last_rows, both, pairs)
+        tail = part if tail is None else tail + part
 
     shape = jax.ShapeDtypeStruct((row_width, rows), BF16)
     work = 2 * rows * depth * row_width
@@ -226,16 +229,17 @@
     for turn, one, two in zip(turns, early, late):
         pairs = [(z, (z + 2 * turn) % tp) for z in range(tp)]
         blocks += [lax.ppermute(one, "tp", pairs), lax.ppermute(two, "tp", pairs)]
-    raw, key, value, state = call(
+    raw, key, value, mine, theirs = call(
         feature_kernel,
         [
             jax.ShapeDtypeStruct((FEAT, local_rows), F32),
             jax.ShapeDtypeStruct((NUM_FEAT, local_rows), BF16),
             jax.ShapeDtypeStruct((val_width, local_rows), BF16),
-            jax.ShapeDtypeStruct((STATE_ROWS, val_width), F32),
+            jax.ShapeDtypeStruct((HALF, val_width), F32),
+            jax.ShapeDtypeStruct((HALF, val_width), F32),
         ],
         [conv_weight, halo] + blocks,
-        [pltpu.VMEM((row_width, rows + local_rows), F32)],
+        [pltpu.VMEM((row_width, rows + local_rows), F32), pltpu.VMEM((NUM_FEAT, val_width), F32)],
     )
     query, numerator, denominator = call(
         inner_kernel,
@@ -244,9 +248,9 @@
         [raw, key, value],
         flops=2 * local_rows * local_rows * (NUM_FEAT + val_width),
     )
-    received = swap(state, 1)
-    terms = [jnp.where(me % 2 == 1, received, 0.0)]
-    total = state + received
+    received = swap(theirs, 1)
+    total = mine + received
+    earlier = jnp.zeros_like(total)
     bit = 2
     while bit < ctx:
         radix = min(4, ctx // bit)
@@ -256,14 +260,18 @@
         for delta in range(1, radix):
             pairs = [(c, c ^ delta * bit) for c in range(ctx)]
             parts.append(lax.ppermute(total, "ctx", pairs))
-            terms.append(jnp.where(digit > digit ^ delta, parts[-1], 0.0))
+            earlier = earlier + jnp.where(digit > digit ^ delta, parts[-1], 0.0)
         if not last:
             total = functools.reduce(jnp.add, parts, total)
         bit *= radix
+    first = me % 2 == 0
+    other = swap(earlier + jnp.where(first, mine, 0.0), 1)
+    kept = earlier + jnp.where(first, 0.0, received)
     return call(
         finish_kernel,
         [jax.ShapeDtypeStruct((local_rows, val_width), BF16)],
-        [query, numerator, denominator] + terms,
+        [query, numerator, denominator, kept, other],
+        [pltpu.VMEM((NUM_FEAT, val_width), F32)],
         flops=6 * local_rows * NUM_FEAT * val_width,
     )[0]
 

time: 49 us -> 48.7 us (level)
  waiting for transfers between devices: 24.5 us -> 23.6 us
  starting transfers between devices: 19.2 us -> 19.9 us
    ppermute x3, waiting for transfers between devices: 4.2 us -> 1.93 us  [per_device(): parts.append(lax.ppermute(total, 'ctx', pairs))]
    ppermute x8 -> x9, waiting for transfers between devices: 5.3 us -> 6.13 us  [swap(): return lax.ppermute(array, 'ctx', [(i, i ^ bit) for i in range(ctx)])]
    ppermute x2, waiting for transfers between devices: 5.47 us -> 6.02 us  [per_device(): blocks += [lax.ppermute(one, 'tp', pairs), lax.ppermute(two, 'tp', pairs)]]
    ppermute x3, starting transfers between devices: 3.62 us -> 4.13 us  [per_device(): parts.append(lax.ppermute(total, 'ctx', pairs))]
    ppermute x8 -> x9, starting transfers between devices: 3.74 us -> 3.83 us  [swap(): return lax.ppermute(array, 'ctx', [(i, i ^ bit) for i in range(ctx)])]
  transfers between devices with their start and end apart: 19 -> 20, of which waited for: 9 -> 11; matrix products, arithmetic and copies ran while one was open for 0% -> 0% of each run, Pallas kernels for 6% -> 6%
where the time goes in v1:
time: 48.7 us; the launch traced here: 48.5 us
  waiting for transfers between devices  23.6 us (48%)
  starting transfers between devices  19.9 us (41%)
  Pallas kernels  4.79 us (10%)
    ppermute x1, waiting for transfers between devices, per_device(): lax.ppermute(mine, 'tp', [((z + 2 * turn) % tp, z) for z in range(tp)])  9.52 us
    ppermute x9, waiting for transfers between devices, swap(): return lax.ppermute(array, 'ctx', [(i, i ^ bit) for i in range(ctx)])  6.13 us
    ppermute x2, waiting for transfers between devices, per_device(): blocks += [lax.ppermute(one, 'tp', pairs), lax.ppermute(two, 'tp', pairs)]  6.02 us
    pallas_call x7, Pallas kernels, call(): pl.pallas_call(kernel, out_shape=outs, in_specs=[space] * len(operands),...  4.79 us
    ppermute x3, starting transfers between devices, per_device(): parts.append(lax.ppermute(total, 'ctx', pairs))  4.13 us
    ppermute x9, starting transfers between devices, swap(): return lax.ppermute(array, 'ctx', [(i, i ^ bit) for i in range(ctx)])  3.83 us
    ppermute x2, starting transfers between devices, per_device(): blocks += [lax.ppermute(one, 'tp', pairs), lax.ppermute(two, 'tp', pairs)]  3.56 us
    ppermute x1, starting transfers between devices, per_device(): paired = lax.ppermute(tokens, 'tp', [(z, z ^ 1) for z in range(tp)])  3.05 us
  transfers between devices with their start and end apart: 20, of which 11 were waited for; matrix products, arithmetic and copies ran while one was open for 0% of the time, Pallas kernels for 6%

profile of v1, /device:TPU:0, one launch (start us, length us, event | category | flops | bytes accessed | tf_op | source)
XLA Modules:
  0.0 48.5 jit_solution(12308955708760270797)
XLA Ops:
  0.0 3.1 %collective-permute-start.4 = (bf16[128,2048]{1,0:T(8,128)(2,1)}, bf16[128,2048]{1,0:T(8,128)(2,1)S(1)}, u32[]{:S(2)}, u32[]{:S(2)}) collective-permute-start(bf16[128,2048]{1,0:T(8,128)(2,1)} %tokens_ref.5), channel_id=1, source_target_pairs={{0,1},{1,0},{2,3},{3,2},{4,5},{5,4},{6,7},{7,6},{8,9},{9,8},{10,11... | collective-permute-start | bytes 1572872 | tf_op jit(solution)/shard_map/ppermute | solution.py:215
  3.1 1.0 %shard_map.37 = (bf16[160,256]{1,0:T(8,128)(2,1)S(1)}, bf16[8,2048]{1,0:T(8,128)(2,1)S(1)}) custom-call(bf16[160,2048]{1,0:T(8,128)(2,1)} %bitcast.1, bf16[128,2048]{1,0:T(8,128)(2,1)} %tokens_ref.5), custom_call_target="tpu_custom_call" | custom-call | flops 1048576 | bytes 1048576 | tf_op jit(solution)/shard_map/pallas_call | solution.py:27
  4.0 2.7 %collective-permute-start.5 = (bf16[160,256]{1,0:T(8,128)(2,1)S(1)}, bf16[160,256]{1,0:T(8,128)(2,1)S(1)}, u32[]{:S(2)}, u32[]{:S(2)}) collective-permute-start(bf16[160,256]{1,0:T(8,128)(2,1)S(1)} %get-tuple-element.22), channel_id=1, source_target_pairs={{2,0},{3,1},{0,2},{1,3},{6,4},{7,5},{4,6},{5,7},{10,8},{11,9},{8,1... | collective-permute-start | bytes 245768 | tf_op jit(solution)/shard_map/ppermute | solution.py:212
  6.7 9.5 %collective-permute-done.5.refs_0_ = bf16[160,256]{1,0:T(8,128)(2,1)S(1)} collective-permute-done((bf16[160,256]{1,0:T(8,128)(2,1)S(1)}, bf16[160,256]{1,0:T(8,128)(2,1)S(1)}, u32[]{:S(2)}, u32[]{:S(2)}) %collective-permute-start.5) | collective-permute-done | bytes 81952 | tf_op jit(solution)/shard_map/ppermute | solution.py:212
  16.2 2.4 %collective-permute-start.8 = (bf16[160,256]{1,0:T(8,128)(2,1)S(1)}, bf16[160,256]{1,0:T(8,128)(2,1)S(1)}, u32[]{:S(2)}, u32[]{:S(2)}) collective-permute-start(bf16[160,256]{1,0:T(8,128)(2,1)S(1)} %collective-permute-done.5.refs_0_), channel_id=1, source_target_pairs={{0,24},{4,28},{8,16},{12,20},{16,8},{20,12},{24,0},{28,4},{1,25},{... | collective-permute-start | bytes 245768 | tf_op jit(solution)/shard_map/ppermute | solution.py:198
  19.7 2.3 %collective-permute-done.8.refs_3_ = bf16[160,256]{1,0:T(8,128)(2,1)S(1)} collective-permute-done((bf16[160,256]{1,0:T(8,128)(2,1)S(1)}, bf16[160,256]{1,0:T(8,128)(2,1)S(1)}, u32[]{:S(2)}, u32[]{:S(2)}) %collective-permute-start.8) | collective-permute-done | bytes 81952 | tf_op jit(solution)/shard_map/ppermute | solution.py:198
  22.0 1.1 %collective-permute-done.7.refs_2_ = bf16[160,256]{1,0:T(8,128)(2,1)S(1)} collective-permute-done((bf16[160,256]{1,0:T(8,128)(2,1)S(1)}, bf16[160,256]{1,0:T(8,128)(2,1)S(1)}, u32[]{:S(2)}, u32[]{:S(2)}) %collective-permute-start.7) | collective-permute-done | bytes 81952 | tf_op jit(solution)/shard_map/ppermute | solution.py:198
  24.3 0.7 %collective-permute-start.2 = (bf16[8,2048]{1,0:T(8,128)(2,1)S(1)}, bf16[8,2048]{1,0:T(8,128)(2,1)S(1)}, u32[]{:S(2)}, u32[]{:S(2)}) collective-permute-start(bf16[8,2048]{1,0:T(8,128)(2,1)S(1)} %get-tuple-element.18), channel_id=1, source_target_pairs={{3,6},{7,10},{11,14},{15,18},{19,22},{23,26},{27,30}} | collective-permute-start | bytes 98312 | tf_op jit(solution)/shard_map/ppermute | solution.py:220
  25.0 0.7 %collective-permute-start.1 = (bf16[8,2048]{1,0:T(8,128)(2,1)S(1)}, bf16[8,2048]{1,0:T(8,128)(2,1)S(1)}, u32[]{:S(2)}, u32[]{:S(2)}) collective-permute-start(bf16[8,2048]{1,0:T(8,128)(2,1)S(1)} %get-tuple-element.18), channel_id=1, source_target_pairs={{3,5},{7,9},{11,13},{15,17},{19,21},{23,25},{27,29}} | collective-permute-start | bytes 98312 | tf_op jit(solution)/shard_map/ppermute | solution.py:220
  25.6 0.7 %collective-permute-start = (bf16[8,2048]{1,0:T(8,128)(2,1)S(1)}, bf16[8,2048]{1,0:T(8,128)(2,1)S(1)}, u32[]{:S(2)}, u32[]{:S(2)}) collective-permute-start(bf16[8,2048]{1,0:T(8,128)(2,1)S(1)} %get-tuple-element.18), channel_id=1, source_target_pairs={{3,4},{7,8},{11,12},{15,16},{19,20},{23,24},{27,28}} | collective-permute-start | bytes 98312 | tf_op jit(solution)/shard_map/ppermute | solution.py:220
  26.7 3.5 %collective-permute-start.13 = (bf16[160,128]{1,0:T(8,128)(2,1)S(1)}, bf16[160,128]{1,0:T(8,128)(2,1)S(1)}, u32[]{:S(2)}, u32[]{:S(2)}) collective-permute-start(bf16[160,128]{1,0:T(8,128)(2,1)S(1)} %shard_map.39), channel_id=1, source_target_pairs={{0,2},{1,3},{2,0},{3,1},{4,6},{5,7},{6,4},{7,5},{8,10},{9,11},{10,... | collective-permute-start | bytes 122888 | tf_op jit(solution)/shard_map/ppermute | solution.py:231
  30.7 0.7 %shard_map.38 = (bf16[160,128]{1,0:T(8,128)(2,1)S(1)}, bf16[160,128]{1,0:T(8,128)(2,1)S(1)}, bf16[160,128]{1,0:T(8,128)(2,1)S(1)}) custom-call(bf16[8,2048]{1,0:T(8,128)(2,1)S(1)} %add_add_fusion.tail_ref, bf16[128,2048]{1,0:T(8,128)(2,1)S(1)} %copy-done, bf16[128,2048]{1,0:T(8,128)(2,1)S(1)} %collective-permute-done.4.paired_ref.tokens_ref, ...), custom_call_target="tpu_custom_call" | custom-call | flops 251658240 | bytes 1048576 | tf_op jit(solution)/shard_map/pallas_call | solution.py:27
  31.4 0.8 %collective-permute-done.13.refs_2_ = bf16[160,128]{1,0:T(8,128)(2,1)S(1)} collective-permute-done((bf16[160,128]{1,0:T(8,128)(2,1)S(1)}, bf16[160,128]{1,0:T(8,128)(2,1)S(1)}, u32[]{:S(2)}, u32[]{:S(2)}) %collective-permute-start.13) | collective-permute-done | bytes 40992 | tf_op jit(solution)/shard_map/ppermute | solution.py:231
  32.2 5.2 %collective-permute-done.14.refs_3_ = bf16[160,128]{1,0:T(8,128)(2,1)S(1)} collective-permute-done((bf16[160,128]{1,0:T(8,128)(2,1)S(1)}, bf16[160,128]{1,0:T(8,128)(2,1)S(1)}, u32[]{:S(2)}, u32[]{:S(2)}) %collective-permute-start.14) | collective-permute-done | bytes 40992 | tf_op jit(solution)/shard_map/ppermute | solution.py:231
  37.4 0.8 %shard_map.41 = (f32[16,512]{1,0:T(8,128)S(1)}, bf16[160,512]{1,0:T(8,128)(2,1)S(1)}, bf16[128,512]{1,0:T(8,128)(2,1)S(1)}, f32[80,128]{1,0:T(8,128)S(1)}, f32[80,128]{1,0:T(8,128)S(1)}) custom-call(f32[4,160]{1,0:T(4,128)S(1)} %copy-done.2, bf16[160,128]{1,0:T(8,128)(2,1)S(1)} %get-tuple-element.19.halo_ref, ...), custom_call_target="tpu_custom_call" | custom-call | flops 1048576 | bytes 1048576 | tf_op jit(solution)/shard_map/pallas_call | solution.py:27
  38.4 1.0 %collective-permute-done.15 = f32[80,128]{1,0:T(8,128)S(1)} collective-permute-done((f32[80,128]{1,0:T(8,128)S(1)}, f32[80,128]{1,0:T(8,128)S(1)}, u32[]{:S(2)}, u32[]{:S(2)}) %collective-permute-start.15) | collective-permute-done | bytes 40992 | tf_op jit(solution)/shard_map/ppermute | solution.py:198
  39.5 1.8 %collective-permute-start.18 = (f32[80,128]{1,0:T(8,128)S(1)}, f32[80,128]{1,0:T(8,128)S(1)}, u32[]{:S(2)}, u32[]{:S(2)}) collective-permute-start(f32[80,128]{1,0:T(8,128)S(1)} %add.36), channel_id=1, source_target_pairs={{0,24},{4,28},{8,16},{12,20},{16,8},{20,12},{24,0},{28,4},{1,25},{... | collective-permute-start | bytes 122888 | tf_op jit(solution)/shard_map/ppermute | solution.py:262
  41.3 0.9 %collective-permute-start.17 = (f32[80,128]{1,0:T(8,128)S(1)}, f32[80,128]{1,0:T(8,128)S(1)}, u32[]{:S(2)}, u32[]{:S(2)}) collective-permute-start(f32[80,128]{1,0:T(8,128)S(1)} %add.36), channel_id=1, source_target_pairs={{0,16},{4,20},{8,24},{12,28},{16,0},{20,4},{24,8},{28,12},{1,17},{... | collective-permute-start | bytes 122888 | tf_op jit(solution)/shard_map/ppermute | solution.py:262
  42.2 1.4 %collective-permute-start.16 = (f32[80,128]{1,0:T(8,128)S(1)}, f32[80,128]{1,0:T(8,128)S(1)}, u32[]{:S(2)}, u32[]{:S(2)}) collective-permute-start(f32[80,128]{1,0:T(8,128)S(1)} %add.36), channel_id=1, source_target_pairs={{0,8},{4,12},{8,0},{12,4},{16,24},{20,28},{24,16},{28,20},{1,9},{5... | collective-permute-start | bytes 122888 | tf_op jit(solution)/shard_map/ppermute | solution.py:262
  43.6 0.7 %shard_map.42 = (bf16[512,160]{1,0:T(8,128)(2,1)S(1)}, f32[512,128]{1,0:T(8,128)S(1)}, f32[512,128]{1,0:T(8,128)S(1)}) custom-call(f32[16,512]{1,0:T(8,128)S(1)} %get-tuple-element.23.raw_ref, bf16[160,512]{1,0:T(8,128)(2,1)S(1)} %get-tuple-element.24.key_ref, bf16[128,512]{1,0:T(8,128)(2,1)S(1)} %get-tuple-element.25.value_ref), custom_call_target="tpu_custom_call" | custom-call | flops 150994944 | bytes 1048576 | tf_op jit(solution)/shard_map/pallas_call | solution.py:27
  44.5 0.8 %collective-permute-done.17 = f32[80,128]{1,0:T(8,128)S(1)} collective-permute-done((f32[80,128]{1,0:T(8,128)S(1)}, f32[80,128]{1,0:T(8,128)S(1)}, u32[]{:S(2)}, u32[]{:S(2)}) %collective-permute-start.17) | collective-permute-done | bytes 40992 | tf_op jit(solution)/shard_map/ppermute | solution.py:262
  45.3 0.9 %collective-permute-done.16 = f32[80,128]{1,0:T(8,128)S(1)} collective-permute-done((f32[80,128]{1,0:T(8,128)S(1)}, f32[80,128]{1,0:T(8,128)S(1)}, u32[]{:S(2)}, u32[]{:S(2)}) %collective-permute-start.16) | collective-permute-done | bytes 40992 | tf_op jit(solution)/shard_map/ppermute | solution.py:262
  46.3 1.2 %collective-permute-done.19.other_ref = f32[80,128]{1,0:T(8,128)S(1)} collective-permute-done((f32[80,128]{1,0:T(8,128)S(1)}, f32[80,128]{1,0:T(8,128)S(1)}, u32[]{:S(2)}, u32[]{:S(2)}) %collective-permute-start.19) | collective-permute-done | bytes 40992 | tf_op jit(solution)/shard_map/ppermute | solution.py:198
  47.5 1.0 %shard_map.43 = bf16[512,128]{1,0:T(8,128)(2,1)} custom-call(bf16[512,160]{1,0:T(8,128)(2,1)S(1)} %get-tuple-element.26.query_ref, f32[512,128]{1,0:T(8,128)S(1)} %get-tuple-element.27.numerator_ref, f32[512,128]{1,0:T(8,128)S(1)} %get-tuple-element.28.denominator_ref, f32[80,128]{1,0:T(8,128)S(1)} %select_add_fusion.1.kept_ref, ...), custom_call_target="tpu_custom_call" | custom-call | flops 62914560 | bytes 1048576 | tf_op jit(solution)/shard_map/pallas_call | solution.py:27
  (33 shorter events, 3.6 us)
Async XLA Ops:
  0.0 26.7 %collective-permute-start.4 = (bf16[128,2048]{1,0:T(8,128)(2,1)}, bf16[128,2048]{1,0:T(8,128)(2,1)S(1)}, u32[]{:S(2)}, u32[]{:S(2)}) collective-permute-start(bf16[128,2048]{1,0:T(8,128)(2,1)} %tokens_ref.5), channel_id=1, source_target_pairs={{0,1},{1,0},{2,3},{3,2},{4,5},{5,4},{6,7},{7,6},{8,9},{9,8},{10,11... | collective-permute-start | bytes 1572872 | tf_op jit(solution)/shard_map/ppermute | solution.py:215
  3.1 23.3 %copy-start = (bf16[128,2048]{1,0:T(8,128)(2,1)S(1)}, bf16[128,2048]{1,0:T(8,128)(2,1)}, u32[]{:S(2)}) copy-start(bf16[128,2048]{1,0:T(8,128)(2,1)} %tokens_ref.5) | copy-start | bytes 1572868
  4.0 12.2 %collective-permute-start.5 = (bf16[160,256]{1,0:T(8,128)(2,1)S(1)}, bf16[160,256]{1,0:T(8,128)(2,1)S(1)}, u32[]{:S(2)}, u32[]{:S(2)}) collective-permute-start(bf16[160,256]{1,0:T(8,128)(2,1)S(1)} %get-tuple-element.22), channel_id=1, source_target_pairs={{2,0},{3,1},{0,2},{1,3},{6,4},{7,5},{4,6},{5,7},{10,8},{11,9},{8,1... | collective-permute-start | bytes 245768 | tf_op jit(solution)/shard_map/ppermute | solution.py:212
  16.2 5.8 %collective-permute-start.8 = (bf16[160,256]{1,0:T(8,128)(2,1)S(1)}, bf16[160,256]{1,0:T(8,128)(2,1)S(1)}, u32[]{:S(2)}, u32[]{:S(2)}) collective-permute-start(bf16[160,256]{1,0:T(8,128)(2,1)S(1)} %collective-permute-done.5.refs_0_), channel_id=1, source_target_pairs={{0,24},{4,28},{8,16},{12,20},{16,8},{20,12},{24,0},{28,4},{1,25},{... | collective-permute-start | bytes 245768 | tf_op jit(solution)/shard_map/ppermute | solution.py:198
  18.6 4.4 %collective-permute-start.7 = (bf16[160,256]{1,0:T(8,128)(2,1)S(1)}, bf16[160,256]{1,0:T(8,128)(2,1)S(1)}, u32[]{:S(2)}, u32[]{:S(2)}) collective-permute-start(bf16[160,256]{1,0:T(8,128)(2,1)S(1)} %collective-permute-done.5.refs_0_), channel_id=1, source_target_pairs={{0,16},{4,20},{8,24},{12,28},{16,0},{20,4},{24,8},{28,12},{1,17},{... | collective-permute-start | bytes 245768 | tf_op jit(solution)/shard_map/ppermute | solution.py:198
  19.2 4.4 %collective-permute-start.6 = (bf16[160,256]{1,0:T(8,128)(2,1)S(1)}, bf16[160,256]{1,0:T(8,128)(2,1)S(1)}, u32[]{:S(2)}, u32[]{:S(2)}) collective-permute-start(bf16[160,256]{1,0:T(8,128)(2,1)S(1)} %collective-permute-done.5.refs_0_), channel_id=1, source_target_pairs={{0,8},{4,12},{8,0},{12,4},{16,24},{20,28},{24,16},{28,20},{1,9},{5... | collective-permute-start | bytes 245768 | tf_op jit(solution)/shard_map/ppermute | solution.py:198
  19.7 3.9 %collective-permute-start.9 = (bf16[160,256]{1,0:T(8,128)(2,1)S(1)}, bf16[160,256]{1,0:T(8,128)(2,1)S(1)}, u32[]{:S(2)}, u32[]{:S(2)}) collective-permute-start(bf16[160,256]{1,0:T(8,128)(2,1)S(1)} %collective-permute-done.5.refs_0_), channel_id=1, source_target_pairs={{0,4},{4,0},{8,12},{12,8},{16,20},{20,16},{24,28},{28,24},{1,5},{5... | collective-permute-start | bytes 245768 | tf_op jit(solution)/shard_map/ppermute | solution.py:198
  22.0 2.3 %collective-permute-start.12 = (bf16[160,256]{1,0:T(8,128)(2,1)S(1)}, bf16[160,256]{1,0:T(8,128)(2,1)S(1)}, u32[]{:S(2)}, u32[]{:S(2)}) collective-permute-start(bf16[160,256]{1,0:T(8,128)(2,1)S(1)} %collective-permute-done.8.refs_3_), channel_id=1, source_target_pairs={{0,4},{4,0},{8,12},{12,8},{16,20},{20,16},{24,28},{28,24},{1,5},{5... | collective-permute-start | bytes 245768 | tf_op jit(solution)/shard_map/ppermute | solution.py:198
  23.1 1.9 %collective-permute-start.11 = (bf16[160,256]{1,0:T(8,128)(2,1)S(1)}, bf16[160,256]{1,0:T(8,128)(2,1)S(1)}, u32[]{:S(2)}, u32[]{:S(2)}) collective-permute-start(bf16[160,256]{1,0:T(8,128)(2,1)S(1)} %collective-permute-done.7.refs_2_), channel_id=1, source_target_pairs={{0,4},{4,0},{8,12},{12,8},{16,20},{20,16},{24,28},{28,24},{1,5},{5... | collective-permute-start | bytes 245768 | tf_op jit(solution)/shard_map/ppermute | solution.py:198
  23.6 2.0 %collective-permute-start.10 = (bf16[160,256]{1,0:T(8,128)(2,1)S(1)}, bf16[160,256]{1,0:T(8,128)(2,1)S(1)}, u32[]{:S(2)}, u32[]{:S(2)}) collective-permute-start(bf16[160,256]{1,0:T(8,128)(2,1)S(1)} %collective-permute-done.6.refs_1_), channel_id=1, source_target_pairs={{0,4},{4,0},{8,12},{12,8},{16,20},{20,16},{24,28},{28,24},{1,5},{5... | collective-permute-start | bytes 245768 | tf_op jit(solution)/shard_map/ppermute | solution.py:198
  23.6 6.9 %collective-permute-start.3 = (bf16[8,2048]{1,0:T(8,128)(2,1)S(1)}, bf16[8,2048]{1,0:T(8,128)(2,1)S(1)}, u32[]{:S(2)}, u32[]{:S(2)}) collective-permute-start(bf16[8,2048]{1,0:T(8,128)(2,1)S(1)} %get-tuple-element.18), channel_id=1, source_target_pairs={{3,7},{7,11},{11,15},{15,19},{19,23},{23,27},{27,31}} | collective-permute-start | bytes 98312 | tf_op jit(solution)/shard_map/ppermute | solution.py:220
  24.3 6.3 %collective-permute-start.2 = (bf16[8,2048]{1,0:T(8,128)(2,1)S(1)}, bf16[8,2048]{1,0:T(8,128)(2,1)S(1)}, u32[]{:S(2)}, u32[]{:S(2)}) collective-permute-start(bf16[8,2048]{1,0:T(8,128)(2,1)S(1)} %get-tuple-element.18), channel_id=1, source_target_pairs={{3,6},{7,10},{11,14},{15,18},{19,22},{23,26},{27,30}} | collective-permute-start | bytes 98312 | tf_op jit(solution)/shard_map/ppermute | solution.py:220
  25.0 5.7 %collective-permute-start.1 = (bf16[8,2048]{1,0:T(8,128)(2,1)S(1)}, bf16[8,2048]{1,0:T(8,128)(2,1)S(1)}, u32[]{:S(2)}, u32[]{:S(2)}) collective-permute-start(bf16[8,2048]{1,0:T(8,128)(2,1)S(1)} %get-tuple-element.18), channel_id=1, source_target_pairs={{3,5},{7,9},{11,13},{15,17},{19,21},{23,25},{27,29}} | collective-permute-start | bytes 98312 | tf_op jit(solution)/shard_map/ppermute | solution.py:220
  25.6 5.0 %collective-permute-start = (bf16[8,2048]{1,0:T(8,128)(2,1)S(1)}, bf16[8,2048]{1,0:T(8,128)(2,1)S(1)}, u32[]{:S(2)}, u32[]{:S(2)}) collective-permute-start(bf16[8,2048]{1,0:T(8,128)(2,1)S(1)} %get-tuple-element.18), channel_id=1, source_target_pairs={{3,4},{7,8},{11,12},{15,16},{19,20},{23,24},{27,28}} | collective-permute-start | bytes 98312 | tf_op jit(solution)/shard_map/ppermute | solution.py:220
  26.7 4.0 %copy-start.1 = (bf16[2048,160]{0,1:T(8,128)(2,1)S(1)}, bf16[2048,160]{0,1:T(8,128)(2,1)}, u32[]{:S(2)}) copy-start(bf16[2048,160]{0,1:T(8,128)(2,1)} %param.4) | copy-start | bytes 1966084
  26.7 5.5 %collective-permute-start.13 = (bf16[160,128]{1,0:T(8,128)(2,1)S(1)}, bf16[160,128]{1,0:T(8,128)(2,1)S(1)}, u32[]{:S(2)}, u32[]{:S(2)}) collective-permute-start(bf16[160,128]{1,0:T(8,128)(2,1)S(1)} %shard_map.39), channel_id=1, source_target_pairs={{0,2},{1,3},{2,0},{3,1},{4,6},{5,7},{6,4},{7,5},{8,10},{9,11},{10,... | collective-permute-start | bytes 122888 | tf_op jit(solution)/shard_map/ppermute | solution.py:231
  30.5 6.8 %collective-permute-start.14 = (bf16[160,128]{1,0:T(8,128)(2,1)S(1)}, bf16[160,128]{1,0:T(8,128)(2,1)S(1)}, u32[]{:S(2)}, u32[]{:S(2)}) collective-permute-start(bf16[160,128]{1,0:T(8,128)(2,1)S(1)} %shard_map.40), channel_id=1, source_target_pairs={{0,2},{1,3},{2,0},{3,1},{4,6},{5,7},{6,4},{7,5},{8,10},{9,11},{10,... | collective-permute-start | bytes 122888 | tf_op jit(solution)/shard_map/ppermute | solution.py:231
  31.3 6.0 %copy-start.2 = (f32[4,160]{1,0:T(4,128)S(1)}, f32[4,160]{1,0:T(4,128)}, u32[]{:S(2)}) copy-start(f32[4,160]{1,0:T(4,128)} %conv_ref.1) | copy-start | bytes 7684
  38.2 1.3 %collective-permute-start.15 = (f32[80,128]{1,0:T(8,128)S(1)}, f32[80,128]{1,0:T(8,128)S(1)}, u32[]{:S(2)}, u32[]{:S(2)}) collective-permute-start(f32[80,128]{1,0:T(8,128)S(1)} %get-tuple-element.30), channel_id=1, source_target_pairs={{0,4},{4,0},{8,12},{12,8},{16,20},{20,16},{24,28},{28,24},{1,5},{5... | collective-permute-start | bytes 122888 | tf_op jit(solution)/shard_map/ppermute | solution.py:198
  39.5 5.0 %collective-permute-start.18 = (f32[80,128]{1,0:T(8,128)S(1)}, f32[80,128]{1,0:T(8,128)S(1)}, u32[]{:S(2)}, u32[]{:S(2)}) collective-permute-start(f32[80,128]{1,0:T(8,128)S(1)} %add.36), channel_id=1, source_target_pairs={{0,24},{4,28},{8,16},{12,20},{16,8},{20,12},{24,0},{28,4},{1,25},{... | collective-permute-start | bytes 122888 | tf_op jit(solution)/shard_map/ppermute | solution.py:262
  41.3 4.0 %collective-permute-start.17 = (f32[80,128]{1,0:T(8,128)S(1)}, f32[80,128]{1,0:T(8,128)S(1)}, u32[]{:S(2)}, u32[]{:S(2)}) collective-permute-start(f32[80,128]{1,0:T(8,128)S(1)} %add.36), channel_id=1, source_target_pairs={{0,16},{4,20},{8,24},{12,28},{16,0},{20,4},{24,8},{28,12},{1,17},{... | collective-permute-start | bytes 122888 | tf_op jit(solution)/shard_map/ppermute | solution.py:262
  42.2 4.0 %collective-permute-start.16 = (f32[80,128]{1,0:T(8,128)S(1)}, f32[80,128]{1,0:T(8,128)S(1)}, u32[]{:S(2)}, u32[]{:S(2)}) collective-permute-start(f32[80,128]{1,0:T(8,128)S(1)} %add.36), channel_id=1, source_target_pairs={{0,8},{4,12},{8,0},{12,4},{16,24},{20,28},{24,16},{28,20},{1,9},{5... | collective-permute-start | bytes 122888 | tf_op jit(solution)/shard_map/ppermute | solution.py:262
  46.2 1.3 %collective-permute-start.19 = (f32[80,128]{1,0:T(8,128)S(1)}, f32[80,128]{1,0:T(8,128)S(1)}, u32[]{:S(2)}, u32[]{:S(2)}) collective-permute-start(f32[80,128]{1,0:T(8,128)S(1)} %get-tuple-element.31), channel_id=1, source_target_pairs={{0,4},{4,0},{8,12},{12,8},{16,20},{20,16},{24,28},{28,24},{1,5},{5... | collective-permute-start | bytes 122888 | tf_op jit(solution)/shard_map/ppermute | solution.py:198

commit v2 on v0

--- a/solution.py
+++ b/solution.py
@@ -210,12 +210,11 @@
         pieces += parts + [swap(part, 1) for part in parts]
     paired = lax.ppermute(tokens, "tp", [(z, z ^ 1) for z in range(tp)])
 
-    pairs = [((c - 1) * tp + tp - 1, c * tp + tp - 1) for c in range(1, ctx)]
-    ahead = lax.ppermute(last_rows, both, pairs)
-    tail = ahead
-    for z in range(tp - 1):
-        pairs = [(c * tp + tp - 1, c * tp + z) for c in range(1, ctx)]
-        tail = tail + lax.ppermute(ahead, both, pairs)
+    tail = None
+    for z in range(tp):
+        pairs = [((c - 1) * tp + tp - 1, c * tp + z) for c in range(1, ctx)]
+        part = lax.ppermute(last_rows, both, pairs)
+        tail = part if tail is None else tail + part
 
     shape = jax.ShapeDtypeStruct((row_width, rows), BF16)
     work = 2 * rows * depth * row_width

time: 49 us -> 49.3 us (level)
    ppermute x8, waiting for transfers between devices: 5.3 us -> 6.12 us  [swap(): return lax.ppermute(array, 'ctx', [(i, i ^ bit) for i in range(ctx)])]
    ppermute x3, waiting for transfers between devices: 4.2 us -> 3.59 us  [per_device(): parts.append(lax.ppermute(total, 'ctx', pairs))]
where the time goes in v2:
time: 49.3 us; the launch traced here: 49.1 us
  waiting for transfers between devices  24.9 us (51%)
  starting transfers between devices  19.1 us (39%)
  Pallas kernels  4.78 us (10%)
    ppermute x1, waiting for transfers between devices, per_device(): lax.ppermute(mine, 'tp', [((z + 2 * turn) % tp, z) for z in range(tp)])  9.52 us
    ppermute x8, waiting for transfers between devices, swap(): return lax.ppermute(array, 'ctx', [(i, i ^ bit) for i in range(ctx)])  6.12 us
    ppermute x2, waiting for transfers between devices, per_device(): blocks += [lax.ppermute(one, 'tp', pairs), lax.ppermute(two, 'tp', pairs)]  5.69 us
    pallas_call x7, Pallas kernels, call(): pl.pallas_call(kernel, out_shape=outs, in_specs=[space] * len(operands),...  4.78 us
    ppermute x3, starting transfers between devices, per_device(): parts.append(lax.ppermute(total, 'ctx', pairs))  3.62 us
    ppermute x3, waiting for transfers between devices, per_device(): parts.append(lax.ppermute(total, 'ctx', pairs))  3.59 us
    ppermute x8, starting transfers between devices, swap(): return lax.ppermute(array, 'ctx', [(i, i ^ bit) for i in range(ctx)])  3.57 us
    ppermute x2, starting transfers between devices, per_device(): blocks += [lax.ppermute(one, 'tp', pairs), lax.ppermute(two, 'tp', pairs)]  3.53 us
  transfers between devices with their start and end apart: 19, of which 9 were waited for; matrix products, arithmetic and copies ran while one was open for 0% of the time, Pallas kernels for 6%

profile of v2, /device:TPU:0, one launch (start us, length us, event | category | flops | bytes accessed | tf_op | source)
XLA Modules:
  0.0 49.1 jit_solution(13570907301186254417)
XLA Ops:
  0.0 3.1 %collective-permute-start.4 = (bf16[128,2048]{1,0:T(8,128)(2,1)}, bf16[128,2048]{1,0:T(8,128)(2,1)S(1)}, u32[]{:S(2)}, u32[]{:S(2)}) collective-permute-start(bf16[128,2048]{1,0:T(8,128)(2,1)} %tokens_ref.5), channel_id=1, source_target_pairs={{0,1},{1,0},{2,3},{3,2},{4,5},{5,4},{6,7},{7,6},{8,9},{9,8},{10,11... | collective-permute-start | bytes 1572872 | tf_op jit(solution)/shard_map/ppermute | solution.py:211
  3.1 1.0 %shard_map.37 = (bf16[160,256]{1,0:T(8,128)(2,1)S(1)}, bf16[8,2048]{1,0:T(8,128)(2,1)S(1)}) custom-call(bf16[160,2048]{1,0:T(8,128)(2,1)} %bitcast.1, bf16[128,2048]{1,0:T(8,128)(2,1)} %tokens_ref.5), custom_call_target="tpu_custom_call" | custom-call | flops 1048576 | bytes 1048576 | tf_op jit(solution)/shard_map/pallas_call | solution.py:27
  4.0 2.7 %collective-permute-start.5 = (bf16[160,256]{1,0:T(8,128)(2,1)S(1)}, bf16[160,256]{1,0:T(8,128)(2,1)S(1)}, u32[]{:S(2)}, u32[]{:S(2)}) collective-permute-start(bf16[160,256]{1,0:T(8,128)(2,1)S(1)} %get-tuple-element.21), channel_id=1, source_target_pairs={{2,0},{3,1},{0,2},{1,3},{6,4},{7,5},{4,6},{5,7},{10,8},{11,9},{8,1... | collective-permute-start | bytes 245768 | tf_op jit(solution)/shard_map/ppermute | solution.py:208
  6.7 9.5 %collective-permute-done.5.refs_0_ = bf16[160,256]{1,0:T(8,128)(2,1)S(1)} collective-permute-done((bf16[160,256]{1,0:T(8,128)(2,1)S(1)}, bf16[160,256]{1,0:T(8,128)(2,1)S(1)}, u32[]{:S(2)}, u32[]{:S(2)}) %collective-permute-start.5) | collective-permute-done | bytes 81952 | tf_op jit(solution)/shard_map/ppermute | solution.py:208
  16.2 1.5 %collective-permute-start.6 = (bf16[160,256]{1,0:T(8,128)(2,1)S(1)}, bf16[160,256]{1,0:T(8,128)(2,1)S(1)}, u32[]{:S(2)}, u32[]{:S(2)}) collective-permute-start(bf16[160,256]{1,0:T(8,128)(2,1)S(1)} %collective-permute-done.5.refs_0_), channel_id=1, source_target_pairs={{0,8},{4,12},{8,0},{12,4},{16,24},{20,28},{24,16},{28,20},{1,9},{5... | collective-permute-start | bytes 245768 | tf_op jit(solution)/shard_map/ppermute | solution.py:194
  17.7 1.5 %collective-permute-start.7 = (bf16[160,256]{1,0:T(8,128)(2,1)S(1)}, bf16[160,256]{1,0:T(8,128)(2,1)S(1)}, u32[]{:S(2)}, u32[]{:S(2)}) collective-permute-start(bf16[160,256]{1,0:T(8,128)(2,1)S(1)} %collective-permute-done.5.refs_0_), channel_id=1, source_target_pairs={{0,16},{4,20},{8,24},{12,28},{16,0},{20,4},{24,8},{28,12},{1,17},{... | collective-permute-start | bytes 245768 | tf_op jit(solution)/shard_map/ppermute | solution.py:194
  19.7 1.4 %collective-permute-done.6.refs_1_ = bf16[160,256]{1,0:T(8,128)(2,1)S(1)} collective-permute-done((bf16[160,256]{1,0:T(8,128)(2,1)S(1)}, bf16[160,256]{1,0:T(8,128)(2,1)S(1)}, u32[]{:S(2)}, u32[]{:S(2)}) %collective-permute-start.6) | collective-permute-done | bytes 81952 | tf_op jit(solution)/shard_map/ppermute | solution.py:194
  21.1 1.8 %collective-permute-done.7.refs_2_ = bf16[160,256]{1,0:T(8,128)(2,1)S(1)} collective-permute-done((bf16[160,256]{1,0:T(8,128)(2,1)S(1)}, bf16[160,256]{1,0:T(8,128)(2,1)S(1)}, u32[]{:S(2)}, u32[]{:S(2)}) %collective-permute-start.7) | collective-permute-done | bytes 81952 | tf_op jit(solution)/shard_map/ppermute | solution.py:194
  22.9 1.6 %collective-permute-done.8.refs_3_ = bf16[160,256]{1,0:T(8,128)(2,1)S(1)} collective-permute-done((bf16[160,256]{1,0:T(8,128)(2,1)S(1)}, bf16[160,256]{1,0:T(8,128)(2,1)S(1)}, u32[]{:S(2)}, u32[]{:S(2)}) %collective-permute-start.8) | collective-permute-done | bytes 81952 | tf_op jit(solution)/shard_map/ppermute | solution.py:194
  24.6 0.7 %collective-permute-start.3 = (bf16[8,2048]{1,0:T(8,128)(2,1)S(1)}, bf16[8,2048]{1,0:T(8,128)(2,1)S(1)}, u32[]{:S(2)}, u32[]{:S(2)}) collective-permute-start(bf16[8,2048]{1,0:T(8,128)(2,1)S(1)} %get-tuple-element.17), channel_id=1, source_target_pairs={{3,7},{7,11},{11,15},{15,19},{19,23},{23,27},{27,31}} | collective-permute-start | bytes 98312 | tf_op jit(solution)/shard_map/ppermute | solution.py:216
  25.2 0.7 %collective-permute-start.2 = (bf16[8,2048]{1,0:T(8,128)(2,1)S(1)}, bf16[8,2048]{1,0:T(8,128)(2,1)S(1)}, u32[]{:S(2)}, u32[]{:S(2)}) collective-permute-start(bf16[8,2048]{1,0:T(8,128)(2,1)S(1)} %get-tuple-element.17), channel_id=1, source_target_pairs={{3,6},{7,10},{11,14},{15,18},{19,22},{23,26},{27,30}} | collective-permute-start | bytes 98312 | tf_op jit(solution)/shard_map/ppermute | solution.py:216
  25.9 0.7 %collective-permute-start = (bf16[8,2048]{1,0:T(8,128)(2,1)S(1)}, bf16[8,2048]{1,0:T(8,128)(2,1)S(1)}, u32[]{:S(2)}, u32[]{:S(2)}) collective-permute-start(bf16[8,2048]{1,0:T(8,128)(2,1)S(1)} %get-tuple-element.17), channel_id=1, source_target_pairs={{3,4},{7,8},{11,12},{15,16},{19,20},{23,24},{27,28}} | collective-permute-start | bytes 98312 | tf_op jit(solution)/shard_map/ppermute | solution.py:216
  26.6 0.7 %collective-permute-start.1 = (bf16[8,2048]{1,0:T(8,128)(2,1)S(1)}, bf16[8,2048]{1,0:T(8,128)(2,1)S(1)}, u32[]{:S(2)}, u32[]{:S(2)}) collective-permute-start(bf16[8,2048]{1,0:T(8,128)(2,1)S(1)} %get-tuple-element.17), channel_id=1, source_target_pairs={{3,5},{7,9},{11,13},{15,17},{19,21},{23,25},{27,29}} | collective-permute-start | bytes 98312 | tf_op jit(solution)/shard_map/ppermute | solution.py:216
  27.7 3.4 %collective-permute-start.13 = (bf16[160,128]{1,0:T(8,128)(2,1)S(1)}, bf16[160,128]{1,0:T(8,128)(2,1)S(1)}, u32[]{:S(2)}, u32[]{:S(2)}) collective-permute-start(bf16[160,128]{1,0:T(8,128)(2,1)S(1)} %shard_map.39), channel_id=1, source_target_pairs={{0,2},{1,3},{2,0},{3,1},{4,6},{5,7},{6,4},{7,5},{8,10},{9,11},{10,... | collective-permute-start | bytes 122888 | tf_op jit(solution)/shard_map/ppermute | solution.py:227
  31.6 0.7 %shard_map.38 = (bf16[160,128]{1,0:T(8,128)(2,1)S(1)}, bf16[160,128]{1,0:T(8,128)(2,1)S(1)}, bf16[160,128]{1,0:T(8,128)(2,1)S(1)}) custom-call(bf16[8,2048]{1,0:T(8,128)(2,1)S(1)} %add_add_fusion.tail_ref, bf16[128,2048]{1,0:T(8,128)(2,1)S(1)} %copy-done, bf16[128,2048]{1,0:T(8,128)(2,1)S(1)} %collective-permute-done.4.paired_ref.tokens_ref, ...), custom_call_target="tpu_custom_call" | custom-call | flops 251658240 | bytes 1048576 | tf_op jit(solution)/shard_map/pallas_call | solution.py:27
  32.3 0.8 %collective-permute-done.13.refs_2_ = bf16[160,128]{1,0:T(8,128)(2,1)S(1)} collective-permute-done((bf16[160,128]{1,0:T(8,128)(2,1)S(1)}, bf16[160,128]{1,0:T(8,128)(2,1)S(1)}, u32[]{:S(2)}, u32[]{:S(2)}) %collective-permute-start.13) | collective-permute-done | bytes 40992 | tf_op jit(solution)/shard_map/ppermute | solution.py:227
  33.1 4.9 %collective-permute-done.14.refs_3_ = bf16[160,128]{1,0:T(8,128)(2,1)S(1)} collective-permute-done((bf16[160,128]{1,0:T(8,128)(2,1)S(1)}, bf16[160,128]{1,0:T(8,128)(2,1)S(1)}, u32[]{:S(2)}, u32[]{:S(2)}) %collective-permute-start.14) | collective-permute-done | bytes 40992 | tf_op jit(solution)/shard_map/ppermute | solution.py:227
  38.0 0.8 %shard_map.41 = (f32[16,512]{1,0:T(8,128)S(1)}, bf16[160,512]{1,0:T(8,128)(2,1)S(1)}, bf16[128,512]{1,0:T(8,128)(2,1)S(1)}, f32[168,128]{1,0:T(8,128)S(1)}) custom-call(f32[4,160]{1,0:T(4,128)S(1)} %copy-done.2, bf16[160,128]{1,0:T(8,128)(2,1)S(1)} %get-tuple-element.18.halo_ref, bf16[160,128]{1,0:T(8,128)(2,1)S(1)} %get-tuple-element.19.refs_0_, ...), custom_call_target="tpu_custom_call" | custom-call | flops 1048576 | bytes 1048576 | tf_op jit(solution)/shard_map/pallas_call | solution.py:27
  38.9 1.3 %collective-permute-done.15 = f32[168,128]{1,0:T(8,128)S(1)} collective-permute-done((f32[168,128]{1,0:T(8,128)S(1)}, f32[168,128]{1,0:T(8,128)S(1)}, u32[]{:S(2)}, u32[]{:S(2)}) %collective-permute-start.15) | collective-permute-done | bytes 86048 | tf_op jit(solution)/shard_map/ppermute | solution.py:194
  40.1 0.9 %collective-permute-start.16 = (f32[168,128]{1,0:T(8,128)S(1)}, f32[168,128]{1,0:T(8,128)S(1)}, u32[]{:S(2)}, u32[]{:S(2)}) collective-permute-start(f32[168,128]{1,0:T(8,128)S(1)} %get-tuple-element.29), channel_id=1, source_target_pairs={{0,8},{4,12},{8,0},{12,4},{16,24},{20,28},{24,16},{28,20},{1,9},{5... | collective-permute-start | bytes 258056 | tf_op jit(solution)/shard_map/ppermute | solution.py:257
  41.1 0.7 %shard_map.42 = (bf16[512,160]{1,0:T(8,128)(2,1)S(1)}, f32[512,128]{1,0:T(8,128)S(1)}, f32[512,128]{1,0:T(8,128)S(1)}) custom-call(f32[16,512]{1,0:T(8,128)S(1)} %get-tuple-element.22.raw_ref, bf16[160,512]{1,0:T(8,128)(2,1)S(1)} %get-tuple-element.23.key_ref, bf16[128,512]{1,0:T(8,128)(2,1)S(1)} %get-tuple-element.24.value_ref), custom_call_target="tpu_custom_call" | custom-call | flops 150994944 | bytes 1048576 | tf_op jit(solution)/shard_map/pallas_call | solution.py:27
  41.8 2.6 %collective-permute-start.18 = (f32[168,128]{1,0:T(8,128)S(1)}, f32[168,128]{1,0:T(8,128)S(1)}, u32[]{:S(2)}, u32[]{:S(2)}) collective-permute-start(f32[168,128]{1,0:T(8,128)S(1)} %get-tuple-element.29), channel_id=1, source_target_pairs={{0,24},{4,28},{8,16},{12,20},{16,8},{20,12},{24,0},{28,4},{1,25},{... | collective-permute-start | bytes 258056 | tf_op jit(solution)/shard_map/ppermute | solution.py:257
  44.8 3.2 %collective-permute-done.17 = f32[168,128]{1,0:T(8,128)S(1)} collective-permute-done((f32[168,128]{1,0:T(8,128)S(1)}, f32[168,128]{1,0:T(8,128)S(1)}, u32[]{:S(2)}, u32[]{:S(2)}) %collective-permute-start.17) | collective-permute-done | bytes 86048 | tf_op jit(solution)/shard_map/ppermute | solution.py:257
  48.1 1.0 %shard_map.43 = bf16[512,128]{1,0:T(8,128)(2,1)} custom-call(bf16[512,160]{1,0:T(8,128)(2,1)S(1)} %get-tuple-element.25.query_ref, f32[512,128]{1,0:T(8,128)S(1)} %get-tuple-element.26.numerator_ref, f32[512,128]{1,0:T(8,128)S(1)} %get-tuple-element.27.denominator_ref, f32[168,128]{1,0:T(8,128)S(1)} %get-tuple-element.30.refs_0_, ...), custom_call_target="tpu_custom_call" | custom-call | flops 62914560 | bytes 1048576 | tf_op jit(solution)/shard_map/pallas_call | solution.py:27
  (32 shorter events, 1.9 us)
Async XLA Ops:
  0.0 27.6 %collective-permute-start.4 = (bf16[128,2048]{1,0:T(8,128)(2,1)}, bf16[128,2048]{1,0:T(8,128)(2,1)S(1)}, u32[]{:S(2)}, u32[]{:S(2)}) collective-permute-start(bf16[128,2048]{1,0:T(8,128)(2,1)} %tokens_ref.5), channel_id=1, source_target_pairs={{0,1},{1,0},{2,3},{3,2},{4,5},{5,4},{6,7},{7,6},{8,9},{9,8},{10,11... | collective-permute-start | bytes 1572872 | tf_op jit(solution)/shard_map/ppermute | solution.py:211
  3.1 24.2 %copy-start = (bf16[128,2048]{1,0:T(8,128)(2,1)S(1)}, bf16[128,2048]{1,0:T(8,128)(2,1)}, u32[]{:S(2)}) copy-start(bf16[128,2048]{1,0:T(8,128)(2,1)} %tokens_ref.5) | copy-start | bytes 1572868
  4.0 12.2 %collective-permute-start.5 = (bf16[160,256]{1,0:T(8,128)(2,1)S(1)}, bf16[160,256]{1,0:T(8,128)(2,1)S(1)}, u32[]{:S(2)}, u32[]{:S(2)}) collective-permute-start(bf16[160,256]{1,0:T(8,128)(2,1)S(1)} %get-tuple-element.21), channel_id=1, source_target_pairs={{2,0},{3,1},{0,2},{1,3},{6,4},{7,5},{4,6},{5,7},{10,8},{11,9},{8,1... | collective-permute-start | bytes 245768 | tf_op jit(solution)/shard_map/ppermute | solution.py:208
  16.2 4.9 %collective-permute-start.6 = (bf16[160,256]{1,0:T(8,128)(2,1)S(1)}, bf16[160,256]{1,0:T(8,128)(2,1)S(1)}, u32[]{:S(2)}, u32[]{:S(2)}) collective-permute-start(bf16[160,256]{1,0:T(8,128)(2,1)S(1)} %collective-permute-done.5.refs_0_), channel_id=1, source_target_pairs={{0,8},{4,12},{8,0},{12,4},{16,24},{20,28},{24,16},{28,20},{1,9},{5... | collective-permute-start | bytes 245768 | tf_op jit(solution)/shard_map/ppermute | solution.py:194
  17.7 5.3 %collective-permute-start.7 = (bf16[160,256]{1,0:T(8,128)(2,1)S(1)}, bf16[160,256]{1,0:T(8,128)(2,1)S(1)}, u32[]{:S(2)}, u32[]{:S(2)}) collective-permute-start(bf16[160,256]{1,0:T(8,128)(2,1)S(1)} %collective-permute-done.5.refs_0_), channel_id=1, source_target_pairs={{0,16},{4,20},{8,24},{12,28},{16,0},{20,4},{24,8},{28,12},{1,17},{... | collective-permute-start | bytes 245768 | tf_op jit(solution)/shard_map/ppermute | solution.py:194
  19.2 5.3 %collective-permute-start.8 = (bf16[160,256]{1,0:T(8,128)(2,1)S(1)}, bf16[160,256]{1,0:T(8,128)(2,1)S(1)}, u32[]{:S(2)}, u32[]{:S(2)}) collective-permute-start(bf16[160,256]{1,0:T(8,128)(2,1)S(1)} %collective-permute-done.5.refs_0_), channel_id=1, source_target_pairs={{0,24},{4,28},{8,16},{12,20},{16,8},{20,12},{24,0},{28,4},{1,25},{... | collective-permute-start | bytes 245768 | tf_op jit(solution)/shard_map/ppermute | solution.py:194
  19.7 4.9 %collective-permute-start.9 = (bf16[160,256]{1,0:T(8,128)(2,1)S(1)}, bf16[160,256]{1,0:T(8,128)(2,1)S(1)}, u32[]{:S(2)}, u32[]{:S(2)}) collective-permute-start(bf16[160,256]{1,0:T(8,128)(2,1)S(1)} %collective-permute-done.5.refs_0_), channel_id=1, source_target_pairs={{0,4},{4,0},{8,12},{12,8},{16,20},{20,16},{24,28},{28,24},{1,5},{5... | collective-permute-start | bytes 245768 | tf_op jit(solution)/shard_map/ppermute | solution.py:194
  21.1 4.1 %collective-permute-start.10 = (bf16[160,256]{1,0:T(8,128)(2,1)S(1)}, bf16[160,256]{1,0:T(8,128)(2,1)S(1)}, u32[]{:S(2)}, u32[]{:S(2)}) collective-permute-start(bf16[160,256]{1,0:T(8,128)(2,1)S(1)} %collective-permute-done.6.refs_1_), channel_id=1, source_target_pairs={{0,4},{4,0},{8,12},{12,8},{16,20},{20,16},{24,28},{28,24},{1,5},{5... | collective-permute-start | bytes 245768 | tf_op jit(solution)/shard_map/ppermute | solution.py:194
  22.9 3.0 %collective-permute-start.11 = (bf16[160,256]{1,0:T(8,128)(2,1)S(1)}, bf16[160,256]{1,0:T(8,128)(2,1)S(1)}, u32[]{:S(2)}, u32[]{:S(2)}) collective-permute-start(bf16[160,256]{1,0:T(8,128)(2,1)S(1)} %collective-permute-done.7.refs_2_), channel_id=1, source_target_pairs={{0,4},{4,0},{8,12},{12,8},{16,20},{20,16},{24,28},{28,24},{1,5},{5... | collective-permute-start | bytes 245768 | tf_op jit(solution)/shard_map/ppermute | solution.py:194
  24.6 2.0 %collective-permute-start.12 = (bf16[160,256]{1,0:T(8,128)(2,1)S(1)}, bf16[160,256]{1,0:T(8,128)(2,1)S(1)}, u32[]{:S(2)}, u32[]{:S(2)}) collective-permute-start(bf16[160,256]{1,0:T(8,128)(2,1)S(1)} %collective-permute-done.8.refs_3_), channel_id=1, source_target_pairs={{0,4},{4,0},{8,12},{12,8},{16,20},{20,16},{24,28},{28,24},{1,5},{5... | collective-permute-start | bytes 245768 | tf_op jit(solution)/shard_map/ppermute | solution.py:194
  24.6 6.9 %collective-permute-start.3 = (bf16[8,2048]{1,0:T(8,128)(2,1)S(1)}, bf16[8,2048]{1,0:T(8,128)(2,1)S(1)}, u32[]{:S(2)}, u32[]{:S(2)}) collective-permute-start(bf16[8,2048]{1,0:T(8,128)(2,1)S(1)} %get-tuple-element.17), channel_id=1, source_target_pairs={{3,7},{7,11},{11,15},{15,19},{19,23},{23,27},{27,31}} | collective-permute-start | bytes 98312 | tf_op jit(solution)/shard_map/ppermute | solution.py:216
  25.2 6.3 %collective-permute-start.2 = (bf16[8,2048]{1,0:T(8,128)(2,1)S(1)}, bf16[8,2048]{1,0:T(8,128)(2,1)S(1)}, u32[]{:S(2)}, u32[]{:S(2)}) collective-permute-start(bf16[8,2048]{1,0:T(8,128)(2,1)S(1)} %get-tuple-element.17), channel_id=1, source_target_pairs={{3,6},{7,10},{11,14},{15,18},{19,22},{23,26},{27,30}} | collective-permute-start | bytes 98312 | tf_op jit(solution)/shard_map/ppermute | solution.py:216
  25.9 5.6 %collective-permute-start = (bf16[8,2048]{1,0:T(8,128)(2,1)S(1)}, bf16[8,2048]{1,0:T(8,128)(2,1)S(1)}, u32[]{:S(2)}, u32[]{:S(2)}) collective-permute-start(bf16[8,2048]{1,0:T(8,128)(2,1)S(1)} %get-tuple-element.17), channel_id=1, source_target_pairs={{3,4},{7,8},{11,12},{15,16},{19,20},{23,24},{27,28}} | collective-permute-start | bytes 98312 | tf_op jit(solution)/shard_map/ppermute | solution.py:216
  26.6 5.0 %collective-permute-start.1 = (bf16[8,2048]{1,0:T(8,128)(2,1)S(1)}, bf16[8,2048]{1,0:T(8,128)(2,1)S(1)}, u32[]{:S(2)}, u32[]{:S(2)}) collective-permute-start(bf16[8,2048]{1,0:T(8,128)(2,1)S(1)} %get-tuple-element.17), channel_id=1, source_target_pairs={{3,5},{7,9},{11,13},{15,17},{19,21},{23,25},{27,29}} | collective-permute-start | bytes 98312 | tf_op jit(solution)/shard_map/ppermute | solution.py:216
  27.6 4.0 %copy-start.1 = (bf16[2048,160]{0,1:T(8,128)(2,1)S(1)}, bf16[2048,160]{0,1:T(8,128)(2,1)}, u32[]{:S(2)}) copy-start(bf16[2048,160]{0,1:T(8,128)(2,1)} %param.4) | copy-start | bytes 1966084
  27.7 5.4 %collective-permute-start.13 = (bf16[160,128]{1,0:T(8,128)(2,1)S(1)}, bf16[160,128]{1,0:T(8,128)(2,1)S(1)}, u32[]{:S(2)}, u32[]{:S(2)}) collective-permute-start(bf16[160,128]{1,0:T(8,128)(2,1)S(1)} %shard_map.39), channel_id=1, source_target_pairs={{0,2},{1,3},{2,0},{3,1},{4,6},{5,7},{6,4},{7,5},{8,10},{9,11},{10,... | collective-permute-start | bytes 122888 | tf_op jit(solution)/shard_map/ppermute | solution.py:227
  31.5 6.5 %collective-permute-start.14 = (bf16[160,128]{1,0:T(8,128)(2,1)S(1)}, bf16[160,128]{1,0:T(8,128)(2,1)S(1)}, u32[]{:S(2)}, u32[]{:S(2)}) collective-permute-start(bf16[160,128]{1,0:T(8,128)(2,1)S(1)} %shard_map.40), channel_id=1, source_target_pairs={{0,2},{1,3},{2,0},{3,1},{4,6},{5,7},{6,4},{7,5},{8,10},{9,11},{10,... | collective-permute-start | bytes 122888 | tf_op jit(solution)/shard_map/ppermute | solution.py:227
  32.3 5.7 %copy-start.2 = (f32[4,160]{1,0:T(4,128)S(1)}, f32[4,160]{1,0:T(4,128)}, u32[]{:S(2)}) copy-start(f32[4,160]{1,0:T(4,128)} %conv_ref.1) | copy-start | bytes 7684
  38.8 1.3 %collective-permute-start.15 = (f32[168,128]{1,0:T(8,128)S(1)}, f32[168,128]{1,0:T(8,128)S(1)}, u32[]{:S(2)}, u32[]{:S(2)}) collective-permute-start(f32[168,128]{1,0:T(8,128)S(1)} %get-tuple-element.28), channel_id=1, source_target_pairs={{0,4},{4,0},{8,12},{12,8},{16,20},{20,16},{24,28},{28,24},{1,5},{5... | collective-permute-start | bytes 258056 | tf_op jit(solution)/shard_map/ppermute | solution.py:194
  40.1 4.7 %collective-permute-start.16 = (f32[168,128]{1,0:T(8,128)S(1)}, f32[168,128]{1,0:T(8,128)S(1)}, u32[]{:S(2)}, u32[]{:S(2)}) collective-permute-start(f32[168,128]{1,0:T(8,128)S(1)} %get-tuple-element.29), channel_id=1, source_target_pairs={{0,8},{4,12},{8,0},{12,4},{16,24},{20,28},{24,16},{28,20},{1,9},{5... | collective-permute-start | bytes 258056 | tf_op jit(solution)/shard_map/ppermute | solution.py:257
  41.8 6.3 %collective-permute-start.17 = (f32[168,128]{1,0:T(8,128)S(1)}, f32[168,128]{1,0:T(8,128)S(1)}, u32[]{:S(2)}, u32[]{:S(2)}) collective-permute-start(f32[168,128]{1,0:T(8,128)S(1)} %get-tuple-element.29), channel_id=1, source_target_pairs={{0,16},{4,20},{8,24},{12,28},{16,0},{20,4},{24,8},{28,12},{1,17},{... | collective-permute-start | bytes 258056 | tf_op jit(solution)/shard_map/ppermute | solution.py:257
  41.8 6.2 %collective-permute-start.18 = (f32[168,128]{1,0:T(8,128)S(1)}, f32[168,128]{1,0:T(8,128)S(1)}, u32[]{:S(2)}, u32[]{:S(2)}) collective-permute-start(f32[168,128]{1,0:T(8,128)S(1)} %get-tuple-element.29), channel_id=1, source_target_pairs={{0,24},{4,28},{8,16},{12,20},{16,8},{20,12},{24,0},{28,4},{1,25},{... | collective-permute-start | bytes 258056 | tf_op jit(solution)/shard_map/ppermute | solution.py:257

commit v3 on v2

--- a/solution.py
+++ b/solution.py
@@ -60,10 +60,9 @@
     last.wait()
 
 
-def own_kernel(tail_ref, tokens_ref, paired_ref, weight_ref, halo_ref, own_ref, other_ref):
+def own_kernel(tail_ref, tokens_ref, weight_ref, halo_ref, own_ref):
     weight = weight_ref[...]
     own_ref[...] = dot_last(weight, tokens_ref[...]).astype(BF16)
-    other_ref[...] = dot_last(weight, paired_ref[...]).astype(BF16)
     padded = jnp.concatenate(
         [jnp.zeros((halo_ref.shape[1] - HALO, tail_ref.shape[1]), BF16), tail_ref[...]], axis=0
     )
@@ -80,13 +79,23 @@
     return total.astype(BF16)
 
 
-def other_heads_kernel(tokens_ref, *refs):
+def early_kernel(tokens_ref, *refs):
     share = own_share()
     count = len(refs) // (PIECES + 1)
     for turn in range(count):
         refs[PIECES * count + turn][...] = gathered(
             share, tokens_ref, refs[PIECES * turn : PIECES * turn + PIECES]
         )
+
+
+def late_kernel(tokens_ref, weight_ref, *refs):
+    share = own_share()
+    count = len(refs) // (PIECES + 1)
+    for turn in range(count):
+        refs[PIECES * count + turn][...] = gathered(
+            share, tokens_ref, refs[PIECES * turn : PIECES * turn + PIECES]
+        )
+    refs[-1][...] = dot_last(weight_ref[...], tokens_ref[...]).astype(BF16)
 
 
 def features(raw, weighted):
@@ -218,9 +227,11 @@
 
     shape = jax.ShapeDtypeStruct((row_width, rows), BF16)
     work = 2 * rows * depth * row_width
-    halo, own, other = call(own_kernel, [shape] * 3, [tail, tokens, paired, weight], flops=3 * work)
-    early = call(other_heads_kernel, [shape] * len(turns), [tokens] + pieces, flops=work)
-    late = call(other_heads_kernel, [shape] * len(turns), [paired] + pieces, flops=work)
+    halo, own = call(own_kernel, [shape] * 2, [tail, tokens, weight], flops=2 * work)
+    early = call(early_kernel, [shape] * len(turns), [tokens] + pieces, flops=work)
+    *late, other = call(
+        late_kernel, [shape] * (len(turns) + 1), [paired, weight] + pieces, flops=2 * work
+    )
     blocks = [own, other]
     for turn, one, two in zip(turns, early, late):
         pairs = [(z, (z + 2 * turn) % tp) for z in range(tp)]
@@ -248,7 +259,7 @@
     total = state + received
     bit = 2
     while bit < ctx:
-        radix = min(4, ctx // bit)
+        radix = 2
         last = bit * radix >= ctx
         digit = me // bit % radix
         parts = []

time: 49.3 us -> 50.7 us (1.028)
  waiting for transfers between devices: 24.9 us -> 28.3 us
  starting transfers between devices: 19.1 us -> 17.1 us
    ppermute x3 -> x2, waiting for transfers between devices: 3.59 us -> 6.95 us  [per_device(): parts.append(lax.ppermute(total, 'ctx', pairs))]
    ppermute x3 -> x2, starting transfers between devices: 3.62 us -> 1.57 us  [per_device(): parts.append(lax.ppermute(total, 'ctx', pairs))]
  transfers between devices with their start and end apart: 19 -> 18, of which waited for: 9 -> 9; matrix products, arithmetic and copies ran while one was open for 0% -> 0% of each run, Pallas kernels for 6% -> 6%
where the time goes in v3:
time: 50.7 us; the launch traced here: 50.5 us
  waiting for transfers between devices  28.3 us (56%)
  starting transfers between devices  17.1 us (34%)
  Pallas kernels  4.77 us (9%)
    ppermute x1, waiting for transfers between devices, per_device(): lax.ppermute(mine, 'tp', [((z + 2 * turn) % tp, z) for z in range(tp)])  9.51 us
    ppermute x2, waiting for transfers between devices, per_device(): parts.append(lax.ppermute(total, 'ctx', pairs))  6.95 us
    ppermute x8, waiting for transfers between devices, swap(): return lax.ppermute(array, 'ctx', [(i, i ^ bit) for i in range(ctx)])  6.04 us
    ppermute x2, waiting for transfers between devices, per_device(): blocks += [lax.ppermute(one, 'tp', pairs), lax.ppermute(two, 'tp', pairs)]  5.83 us
    pallas_call x7, Pallas kernels, call(): pl.pallas_call(kernel, out_shape=outs, in_specs=[space] * len(operands),...  4.77 us
    ppermute x8, starting transfers between devices, swap(): return lax.ppermute(array, 'ctx', [(i, i ^ bit) for i in range(ctx)])  3.67 us
    ppermute x2, starting transfers between devices, per_device(): blocks += [lax.ppermute(one, 'tp', pairs), lax.ppermute(two, 'tp', pairs)]  3.53 us
    ppermute x1, starting transfers between devices, per_device(): paired = lax.ppermute(tokens, 'tp', [(z, z ^ 1) for z in range(tp)])  3.05 us
  transfers between devices with their start and end apart: 18, of which 9 were waited for; matrix products, arithmetic and copies ran while one was open for 0% of the time, Pallas kernels for 6%

profile of v3, /device:TPU:0, one launch (start us, length us, event | category | flops | bytes accessed | tf_op | source)
XLA Modules:
  0.0 50.5 jit_solution(962858122446850855)
XLA Ops:
  0.0 3.1 %collective-permute-start.4 = (bf16[128,2048]{1,0:T(8,128)(2,1)}, bf16[128,2048]{1,0:T(8,128)(2,1)S(1)}, u32[]{:S(2)}, u32[]{:S(2)}) collective-permute-start(bf16[128,2048]{1,0:T(8,128)(2,1)} %tokens_ref.5), channel_id=1, source_target_pairs={{0,1},{1,0},{2,3},{3,2},{4,5},{5,4},{6,7},{7,6},{8,9},{9,8},{10,11... | collective-permute-start | bytes 1572872 | tf_op jit(solution)/shard_map/ppermute | solution.py:220
  3.1 1.0 %shard_map.37 = (bf16[160,256]{1,0:T(8,128)(2,1)S(1)}, bf16[8,2048]{1,0:T(8,128)(2,1)S(1)}) custom-call(bf16[160,2048]{1,0:T(8,128)(2,1)} %bitcast.1, bf16[128,2048]{1,0:T(8,128)(2,1)} %tokens_ref.5), custom_call_target="tpu_custom_call" | custom-call | flops 1048576 | bytes 1048576 | tf_op jit(solution)/shard_map/pallas_call | solution.py:27
  4.0 2.7 %collective-permute-start.5 = (bf16[160,256]{1,0:T(8,128)(2,1)S(1)}, bf16[160,256]{1,0:T(8,128)(2,1)S(1)}, u32[]{:S(2)}, u32[]{:S(2)}) collective-permute-start(bf16[160,256]{1,0:T(8,128)(2,1)S(1)} %get-tuple-element.21), channel_id=1, source_target_pairs={{2,0},{3,1},{0,2},{1,3},{6,4},{7,5},{4,6},{5,7},{10,8},{11,9},{8,1... | collective-permute-start | bytes 245768 | tf_op jit(solution)/shard_map/ppermute | solution.py:217
  6.7 9.5 %collective-permute-done.5.refs_0_ = bf16[160,256]{1,0:T(8,128)(2,1)S(1)} collective-permute-done((bf16[160,256]{1,0:T(8,128)(2,1)S(1)}, bf16[160,256]{1,0:T(8,128)(2,1)S(1)}, u32[]{:S(2)}, u32[]{:S(2)}) %collective-permute-start.5) | collective-permute-done | bytes 81952 | tf_op jit(solution)/shard_map/ppermute | solution.py:217
  16.2 1.5 %collective-permute-start.6 = (bf16[160,256]{1,0:T(8,128)(2,1)S(1)}, bf16[160,256]{1,0:T(8,128)(2,1)S(1)}, u32[]{:S(2)}, u32[]{:S(2)}) collective-permute-start(bf16[160,256]{1,0:T(8,128)(2,1)S(1)} %collective-permute-done.5.refs_0_), channel_id=1, source_target_pairs={{0,8},{4,12},{8,0},{12,4},{16,24},{20,28},{24,16},{28,20},{1,9},{5... | collective-permute-start | bytes 245768 | tf_op jit(solution)/shard_map/ppermute | solution.py:203
  17.7 1.5 %collective-permute-start.7 = (bf16[160,256]{1,0:T(8,128)(2,1)S(1)}, bf16[160,256]{1,0:T(8,128)(2,1)S(1)}, u32[]{:S(2)}, u32[]{:S(2)}) collective-permute-start(bf16[160,256]{1,0:T(8,128)(2,1)S(1)} %collective-permute-done.5.refs_0_), channel_id=1, source_target_pairs={{0,16},{4,20},{8,24},{12,28},{16,0},{20,4},{24,8},{28,12},{1,17},{... | collective-permute-start | bytes 245768 | tf_op jit(solution)/shard_map/ppermute | solution.py:203
  19.7 1.4 %collective-permute-done.6.refs_1_ = bf16[160,256]{1,0:T(8,128)(2,1)S(1)} collective-permute-done((bf16[160,256]{1,0:T(8,128)(2,1)S(1)}, bf16[160,256]{1,0:T(8,128)(2,1)S(1)}, u32[]{:S(2)}, u32[]{:S(2)}) %collective-permute-start.6) | collective-permute-done | bytes 81952 | tf_op jit(solution)/shard_map/ppermute | solution.py:203
  21.1 1.8 %collective-permute-done.7.refs_2_ = bf16[160,256]{1,0:T(8,128)(2,1)S(1)} collective-permute-done((bf16[160,256]{1,0:T(8,128)(2,1)S(1)}, bf16[160,256]{1,0:T(8,128)(2,1)S(1)}, u32[]{:S(2)}, u32[]{:S(2)}) %collective-permute-start.7) | collective-permute-done | bytes 81952 | tf_op jit(solution)/shard_map/ppermute | solution.py:203
  22.9 1.6 %collective-permute-done.8.refs_3_ = bf16[160,256]{1,0:T(8,128)(2,1)S(1)} collective-permute-done((bf16[160,256]{1,0:T(8,128)(2,1)S(1)}, bf16[160,256]{1,0:T(8,128)(2,1)S(1)}, u32[]{:S(2)}, u32[]{:S(2)}) %collective-permute-start.8) | collective-permute-done | bytes 81952 | tf_op jit(solution)/shard_map/ppermute | solution.py:203
  24.6 0.7 %collective-permute-start.3 = (bf16[8,2048]{1,0:T(8,128)(2,1)S(1)}, bf16[8,2048]{1,0:T(8,128)(2,1)S(1)}, u32[]{:S(2)}, u32[]{:S(2)}) collective-permute-start(bf16[8,2048]{1,0:T(8,128)(2,1)S(1)} %get-tuple-element.18), channel_id=1, source_target_pairs={{3,7},{7,11},{11,15},{15,19},{19,23},{23,27},{27,31}} | collective-permute-start | bytes 98312 | tf_op jit(solution)/shard_map/ppermute | solution.py:225
  25.2 0.7 %collective-permute-start.2 = (bf16[8,2048]{1,0:T(8,128)(2,1)S(1)}, bf16[8,2048]{1,0:T(8,128)(2,1)S(1)}, u32[]{:S(2)}, u32[]{:S(2)}) collective-permute-start(bf16[8,2048]{1,0:T(8,128)(2,1)S(1)} %get-tuple-element.18), channel_id=1, source_target_pairs={{3,6},{7,10},{11,14},{15,18},{19,22},{23,26},{27,30}} | collective-permute-start | bytes 98312 | tf_op jit(solution)/shard_map/ppermute | solution.py:225
  25.9 0.7 %collective-permute-start = (bf16[8,2048]{1,0:T(8,128)(2,1)S(1)}, bf16[8,2048]{1,0:T(8,128)(2,1)S(1)}, u32[]{:S(2)}, u32[]{:S(2)}) collective-permute-start(bf16[8,2048]{1,0:T(8,128)(2,1)S(1)} %get-tuple-element.18), channel_id=1, source_target_pairs={{3,4},{7,8},{11,12},{15,16},{19,20},{23,24},{27,28}} | collective-permute-start | bytes 98312 | tf_op jit(solution)/shard_map/ppermute | solution.py:225
  26.6 0.7 %collective-permute-start.1 = (bf16[8,2048]{1,0:T(8,128)(2,1)S(1)}, bf16[8,2048]{1,0:T(8,128)(2,1)S(1)}, u32[]{:S(2)}, u32[]{:S(2)}) collective-permute-start(bf16[8,2048]{1,0:T(8,128)(2,1)S(1)} %get-tuple-element.18), channel_id=1, source_target_pairs={{3,5},{7,9},{11,13},{15,17},{19,21},{23,25},{27,29}} | collective-permute-start | bytes 98312 | tf_op jit(solution)/shard_map/ppermute | solution.py:225
  27.6 3.4 %collective-permute-start.13 = (bf16[160,128]{1,0:T(8,128)(2,1)S(1)}, bf16[160,128]{1,0:T(8,128)(2,1)S(1)}, u32[]{:S(2)}, u32[]{:S(2)}) collective-permute-start(bf16[160,128]{1,0:T(8,128)(2,1)S(1)} %shard_map.40), channel_id=1, source_target_pairs={{0,2},{1,3},{2,0},{3,1},{4,6},{5,7},{6,4},{7,5},{8,10},{9,11},{10,... | collective-permute-start | bytes 122888 | tf_op jit(solution)/shard_map/ppermute | solution.py:238
  32.3 0.8 %collective-permute-done.13.refs_2_ = bf16[160,128]{1,0:T(8,128)(2,1)S(1)} collective-permute-done((bf16[160,128]{1,0:T(8,128)(2,1)S(1)}, bf16[160,128]{1,0:T(8,128)(2,1)S(1)}, u32[]{:S(2)}, u32[]{:S(2)}) %collective-permute-start.13) | collective-permute-done | bytes 40992 | tf_op jit(solution)/shard_map/ppermute | solution.py:238
  33.1 5.0 %collective-permute-done.14.refs_3_ = bf16[160,128]{1,0:T(8,128)(2,1)S(1)} collective-permute-done((bf16[160,128]{1,0:T(8,128)(2,1)S(1)}, bf16[160,128]{1,0:T(8,128)(2,1)S(1)}, u32[]{:S(2)}, u32[]{:S(2)}) %collective-permute-start.14) | collective-permute-done | bytes 40992 | tf_op jit(solution)/shard_map/ppermute | solution.py:238
  38.1 0.8 %shard_map.41 = (f32[16,512]{1,0:T(8,128)S(1)}, bf16[160,512]{1,0:T(8,128)(2,1)S(1)}, bf16[128,512]{1,0:T(8,128)(2,1)S(1)}, f32[168,128]{1,0:T(8,128)S(1)}) custom-call(f32[4,160]{1,0:T(4,128)S(1)} %copy-done.2, bf16[160,128]{1,0:T(8,128)(2,1)S(1)} %get-tuple-element.19.halo_ref, bf16[160,128]{1,0:T(8,128)(2,1)S(1)} %get-tuple-element.20.refs_0_, ...), custom_call_target="tpu_custom_call" | custom-call | flops 1048576 | bytes 1048576 | tf_op jit(solution)/shard_map/pallas_call | solution.py:27
  39.1 1.2 %collective-permute-done.15 = f32[168,128]{1,0:T(8,128)S(1)} collective-permute-done((f32[168,128]{1,0:T(8,128)S(1)}, f32[168,128]{1,0:T(8,128)S(1)}, u32[]{:S(2)}, u32[]{:S(2)}) %collective-permute-start.15) | collective-permute-done | bytes 86048 | tf_op jit(solution)/shard_map/ppermute | solution.py:203
  40.3 1.0 %collective-permute-start.16 = (f32[168,128]{1,0:T(8,128)S(1)}, f32[168,128]{1,0:T(8,128)S(1)}, u32[]{:S(2)}, u32[]{:S(2)}) collective-permute-start(f32[168,128]{1,0:T(8,128)S(1)} %get-tuple-element.33), channel_id=1, source_target_pairs={{0,8},{4,12},{8,0},{12,4},{16,24},{20,28},{24,16},{28,20},{1,9},{5... | collective-permute-start | bytes 258056 | tf_op jit(solution)/shard_map/ppermute | solution.py:268
  41.3 3.7 %collective-permute-done.16 = f32[168,128]{1,0:T(8,128)S(1)} collective-permute-done((f32[168,128]{1,0:T(8,128)S(1)}, f32[168,128]{1,0:T(8,128)S(1)}, u32[]{:S(2)}, u32[]{:S(2)}) %collective-permute-start.16) | collective-permute-done | bytes 86048 | tf_op jit(solution)/shard_map/ppermute | solution.py:268
  44.9 0.6 %collective-permute-start.17 = (f32[168,128]{1,0:T(8,128)S(1)}, f32[168,128]{1,0:T(8,128)S(1)}, u32[]{:S(2)}, u32[]{:S(2)}) collective-permute-start(f32[168,128]{1,0:T(8,128)S(1)} %get-tuple-element.31), channel_id=1, source_target_pairs={{0,16},{4,20},{8,24},{12,28},{16,0},{20,4},{24,8},{28,12},{1,17},{... | collective-permute-start | bytes 258056 | tf_op jit(solution)/shard_map/ppermute | solution.py:268
  45.5 0.7 %shard_map.42 = (bf16[512,160]{1,0:T(8,128)(2,1)S(1)}, f32[512,128]{1,0:T(8,128)S(1)}, f32[512,128]{1,0:T(8,128)S(1)}) custom-call(f32[16,512]{1,0:T(8,128)S(1)} %get-tuple-element.24.raw_ref, bf16[160,512]{1,0:T(8,128)(2,1)S(1)} %get-tuple-element.25.key_ref, bf16[128,512]{1,0:T(8,128)(2,1)S(1)} %get-tuple-element.26.value_ref), custom_call_target="tpu_custom_call" | custom-call | flops 150994944 | bytes 1048576 | tf_op jit(solution)/shard_map/pallas_call | solution.py:27
  46.2 3.3 %collective-permute-done.17 = f32[168,128]{1,0:T(8,128)S(1)} collective-permute-done((f32[168,128]{1,0:T(8,128)S(1)}, f32[168,128]{1,0:T(8,128)S(1)}, u32[]{:S(2)}, u32[]{:S(2)}) %collective-permute-start.17) | collective-permute-done | bytes 86048 | tf_op jit(solution)/shard_map/ppermute | solution.py:268
  49.5 1.0 %shard_map.43 = bf16[512,128]{1,0:T(8,128)(2,1)} custom-call(bf16[512,160]{1,0:T(8,128)(2,1)S(1)} %get-tuple-element.27.query_ref, f32[512,128]{1,0:T(8,128)S(1)} %get-tuple-element.28.numerator_ref, f32[512,128]{1,0:T(8,128)S(1)} %get-tuple-element.29.denominator_ref, f32[168,128]{1,0:T(8,128)S(1)} %get-tuple-element.34.refs_0_, ...), custom_call_target="tpu_custom_call" | custom-call | flops 62914560 | bytes 1048576 | tf_op jit(solution)/shard_map/pallas_call | solution.py:27
  (29 shorter events, 2.2 us)
Async XLA Ops:
  0.0 27.6 %collective-permute-start.4 = (bf16[128,2048]{1,0:T(8,128)(2,1)}, bf16[128,2048]{1,0:T(8,128)(2,1)S(1)}, u32[]{:S(2)}, u32[]{:S(2)}) collective-permute-start(bf16[128,2048]{1,0:T(8,128)(2,1)} %tokens_ref.5), channel_id=1, source_target_pairs={{0,1},{1,0},{2,3},{3,2},{4,5},{5,4},{6,7},{7,6},{8,9},{9,8},{10,11... | collective-permute-start | bytes 1572872 | tf_op jit(solution)/shard_map/ppermute | solution.py:220
  3.1 24.2 %copy-start.1 = (bf16[128,2048]{1,0:T(8,128)(2,1)S(1)}, bf16[128,2048]{1,0:T(8,128)(2,1)}, u32[]{:S(2)}) copy-start(bf16[128,2048]{1,0:T(8,128)(2,1)} %tokens_ref.5) | copy-start | bytes 1572868
  4.0 27.1 %copy-start = (bf16[2048,160]{0,1:T(8,128)(2,1)S(1)}, bf16[2048,160]{0,1:T(8,128)(2,1)}, u32[]{:S(2)}) copy-start(bf16[2048,160]{0,1:T(8,128)(2,1)} %param.4) | copy-start | bytes 1966084
  4.0 12.2 %collective-permute-start.5 = (bf16[160,256]{1,0:T(8,128)(2,1)S(1)}, bf16[160,256]{1,0:T(8,128)(2,1)S(1)}, u32[]{:S(2)}, u32[]{:S(2)}) collective-permute-start(bf16[160,256]{1,0:T(8,128)(2,1)S(1)} %get-tuple-element.21), channel_id=1, source_target_pairs={{2,0},{3,1},{0,2},{1,3},{6,4},{7,5},{4,6},{5,7},{10,8},{11,9},{8,1... | collective-permute-start | bytes 245768 | tf_op jit(solution)/shard_map/ppermute | solution.py:217
  16.2 4.9 %collective-permute-start.6 = (bf16[160,256]{1,0:T(8,128)(2,1)S(1)}, bf16[160,256]{1,0:T(8,128)(2,1)S(1)}, u32[]{:S(2)}, u32[]{:S(2)}) collective-permute-start(bf16[160,256]{1,0:T(8,128)(2,1)S(1)} %collective-permute-done.5.refs_0_), channel_id=1, source_target_pairs={{0,8},{4,12},{8,0},{12,4},{16,24},{20,28},{24,16},{28,20},{1,9},{5... | collective-permute-start | bytes 245768 | tf_op jit(solution)/shard_map/ppermute | solution.py:203
  17.7 5.3 %collective-permute-start.7 = (bf16[160,256]{1,0:T(8,128)(2,1)S(1)}, bf16[160,256]{1,0:T(8,128)(2,1)S(1)}, u32[]{:S(2)}, u32[]{:S(2)}) collective-permute-start(bf16[160,256]{1,0:T(8,128)(2,1)S(1)} %collective-permute-done.5.refs_0_), channel_id=1, source_target_pairs={{0,16},{4,20},{8,24},{12,28},{16,0},{20,4},{24,8},{28,12},{1,17},{... | collective-permute-start | bytes 245768 | tf_op jit(solution)/shard_map/ppermute | solution.py:203
  19.2 5.3 %collective-permute-start.8 = (bf16[160,256]{1,0:T(8,128)(2,1)S(1)}, bf16[160,256]{1,0:T(8,128)(2,1)S(1)}, u32[]{:S(2)}, u32[]{:S(2)}) collective-permute-start(bf16[160,256]{1,0:T(8,128)(2,1)S(1)} %collective-permute-done.5.refs_0_), channel_id=1, source_target_pairs={{0,24},{4,28},{8,16},{12,20},{16,8},{20,12},{24,0},{28,4},{1,25},{... | collective-permute-start | bytes 245768 | tf_op jit(solution)/shard_map/ppermute | solution.py:203
  19.7 4.9 %collective-permute-start.9 = (bf16[160,256]{1,0:T(8,128)(2,1)S(1)}, bf16[160,256]{1,0:T(8,128)(2,1)S(1)}, u32[]{:S(2)}, u32[]{:S(2)}) collective-permute-start(bf16[160,256]{1,0:T(8,128)(2,1)S(1)} %collective-permute-done.5.refs_0_), channel_id=1, source_target_pairs={{0,4},{4,0},{8,12},{12,8},{16,20},{20,16},{24,28},{28,24},{1,5},{5... | collective-permute-start | bytes 245768 | tf_op jit(solution)/shard_map/ppermute | solution.py:203
  21.1 4.1 %collective-permute-start.10 = (bf16[160,256]{1,0:T(8,128)(2,1)S(1)}, bf16[160,256]{1,0:T(8,128)(2,1)S(1)}, u32[]{:S(2)}, u32[]{:S(2)}) collective-permute-start(bf16[160,256]{1,0:T(8,128)(2,1)S(1)} %collective-permute-done.6.refs_1_), channel_id=1, source_target_pairs={{0,4},{4,0},{8,12},{12,8},{16,20},{20,16},{24,28},{28,24},{1,5},{5... | collective-permute-start | bytes 245768 | tf_op jit(solution)/shard_map/ppermute | solution.py:203
  22.9 3.0 %collective-permute-start.11 = (bf16[160,256]{1,0:T(8,128)(2,1)S(1)}, bf16[160,256]{1,0:T(8,128)(2,1)S(1)}, u32[]{:S(2)}, u32[]{:S(2)}) collective-permute-start(bf16[160,256]{1,0:T(8,128)(2,1)S(1)} %collective-permute-done.7.refs_2_), channel_id=1, source_target_pairs={{0,4},{4,0},{8,12},{12,8},{16,20},{20,16},{24,28},{28,24},{1,5},{5... | collective-permute-start | bytes 245768 | tf_op jit(solution)/shard_map/ppermute | solution.py:203
  24.6 2.0 %collective-permute-start.12 = (bf16[160,256]{1,0:T(8,128)(2,1)S(1)}, bf16[160,256]{1,0:T(8,128)(2,1)S(1)}, u32[]{:S(2)}, u32[]{:S(2)}) collective-permute-start(bf16[160,256]{1,0:T(8,128)(2,1)S(1)} %collective-permute-done.8.refs_3_), channel_id=1, source_target_pairs={{0,4},{4,0},{8,12},{12,8},{16,20},{20,16},{24,28},{28,24},{1,5},{5... | collective-permute-start | bytes 245768 | tf_op jit(solution)/shard_map/ppermute | solution.py:203
  24.6 7.0 %collective-permute-start.3 = (bf16[8,2048]{1,0:T(8,128)(2,1)S(1)}, bf16[8,2048]{1,0:T(8,128)(2,1)S(1)}, u32[]{:S(2)}, u32[]{:S(2)}) collective-permute-start(bf16[8,2048]{1,0:T(8,128)(2,1)S(1)} %get-tuple-element.18), channel_id=1, source_target_pairs={{3,7},{7,11},{11,15},{15,19},{19,23},{23,27},{27,31}} | collective-permute-start | bytes 98312 | tf_op jit(solution)/shard_map/ppermute | solution.py:225
  25.2 6.5 %collective-permute-start.2 = (bf16[8,2048]{1,0:T(8,128)(2,1)S(1)}, bf16[8,2048]{1,0:T(8,128)(2,1)S(1)}, u32[]{:S(2)}, u32[]{:S(2)}) collective-permute-start(bf16[8,2048]{1,0:T(8,128)(2,1)S(1)} %get-tuple-element.18), channel_id=1, source_target_pairs={{3,6},{7,10},{11,14},{15,18},{19,22},{23,26},{27,30}} | collective-permute-start | bytes 98312 | tf_op jit(solution)/shard_map/ppermute | solution.py:225
  25.9 5.8 %collective-permute-start = (bf16[8,2048]{1,0:T(8,128)(2,1)S(1)}, bf16[8,2048]{1,0:T(8,128)(2,1)S(1)}, u32[]{:S(2)}, u32[]{:S(2)}) collective-permute-start(bf16[8,2048]{1,0:T(8,128)(2,1)S(1)} %get-tuple-element.18), channel_id=1, source_target_pairs={{3,4},{7,8},{11,12},{15,16},{19,20},{23,24},{27,28}} | collective-permute-start | bytes 98312 | tf_op jit(solution)/shard_map/ppermute | solution.py:225
  26.6 5.1 %collective-permute-start.1 = (bf16[8,2048]{1,0:T(8,128)(2,1)S(1)}, bf16[8,2048]{1,0:T(8,128)(2,1)S(1)}, u32[]{:S(2)}, u32[]{:S(2)}) collective-permute-start(bf16[8,2048]{1,0:T(8,128)(2,1)S(1)} %get-tuple-element.18), channel_id=1, source_target_pairs={{3,5},{7,9},{11,13},{15,17},{19,21},{23,25},{27,29}} | collective-permute-start | bytes 98312 | tf_op jit(solution)/shard_map/ppermute | solution.py:225
  27.6 5.4 %collective-permute-start.13 = (bf16[160,128]{1,0:T(8,128)(2,1)S(1)}, bf16[160,128]{1,0:T(8,128)(2,1)S(1)}, u32[]{:S(2)}, u32[]{:S(2)}) collective-permute-start(bf16[160,128]{1,0:T(8,128)(2,1)S(1)} %shard_map.40), channel_id=1, source_target_pairs={{0,2},{1,3},{2,0},{3,1},{4,6},{5,7},{6,4},{7,5},{8,10},{9,11},{10,... | collective-permute-start | bytes 122888 | tf_op jit(solution)/shard_map/ppermute | solution.py:238
  31.6 6.5 %collective-permute-start.14 = (bf16[160,128]{1,0:T(8,128)(2,1)S(1)}, bf16[160,128]{1,0:T(8,128)(2,1)S(1)}, u32[]{:S(2)}, u32[]{:S(2)}) collective-permute-start(bf16[160,128]{1,0:T(8,128)(2,1)S(1)} %get-tuple-element.23), channel_id=1, source_target_pairs={{0,2},{1,3},{2,0},{3,1},{4,6},{5,7},{6,4},{7,5},{8,10},{9,11},{10,... | collective-permute-start | bytes 122888 | tf_op jit(solution)/shard_map/ppermute | solution.py:238
  32.3 5.8 %copy-start.2 = (f32[4,160]{1,0:T(4,128)S(1)}, f32[4,160]{1,0:T(4,128)}, u32[]{:S(2)}) copy-start(f32[4,160]{1,0:T(4,128)} %conv_ref.1) | copy-start | bytes 7684
  38.9 1.3 %collective-permute-start.15 = (f32[168,128]{1,0:T(8,128)S(1)}, f32[168,128]{1,0:T(8,128)S(1)}, u32[]{:S(2)}, u32[]{:S(2)}) collective-permute-start(f32[168,128]{1,0:T(8,128)S(1)} %get-tuple-element.30), channel_id=1, source_target_pairs={{0,4},{4,0},{8,12},{12,8},{16,20},{20,16},{24,28},{28,24},{1,5},{5... | collective-permute-start | bytes 258056 | tf_op jit(solution)/shard_map/ppermute | solution.py:203
  40.3 4.7 %collective-permute-start.16 = (f32[168,128]{1,0:T(8,128)S(1)}, f32[168,128]{1,0:T(8,128)S(1)}, u32[]{:S(2)}, u32[]{:S(2)}) collective-permute-start(f32[168,128]{1,0:T(8,128)S(1)} %get-tuple-element.33), channel_id=1, source_target_pairs={{0,8},{4,12},{8,0},{12,4},{16,24},{20,28},{24,16},{28,20},{1,9},{5... | collective-permute-start | bytes 258056 | tf_op jit(solution)/shard_map/ppermute | solution.py:268
  44.9 4.6 %collective-permute-start.17 = (f32[168,128]{1,0:T(8,128)S(1)}, f32[168,128]{1,0:T(8,128)S(1)}, u32[]{:S(2)}, u32[]{:S(2)}) collective-permute-start(f32[168,128]{1,0:T(8,128)S(1)} %get-tuple-element.31), channel_id=1, source_target_pairs={{0,16},{4,20},{8,24},{12,28},{16,0},{20,4},{24,8},{28,12},{1,17},{... | collective-permute-start | bytes 258056 | tf_op jit(solution)/shard_map/ppermute | solution.py:268

commit v4 on v3

--- a/solution.py
+++ b/solution.py
@@ -15,7 +15,6 @@
 LANES = 128
 QUAD_FEATS = FEAT * (FEAT + 1) // 2
 NUM_FEAT = QUAD_FEATS + FEAT + 8
-STATE_ROWS = NUM_FEAT + 8
 F32 = jnp.float32
 BF16 = jnp.bfloat16
 HBM = pl.BlockSpec(memory_space=pltpu.HBM)
@@ -139,13 +138,14 @@
     query_ref[...] = convolved[:FEAT]
     key = features(convolved[FEAT : 2 * FEAT], True)
     key_ref[...] = key
-    state_ref[:NUM_FEAT, :] = dot_last(key, value)
+    state_ref[...] = dot_last(key, value)
     total = dot_last(jnp.ones((8, local_rows), BF16), key)
     lanes = state_ref.shape[1]
     rest = NUM_FEAT - lanes
     more = jnp.concatenate([total[:, lanes:], jnp.zeros((8, lanes - rest), F32)], axis=1)
     row = lax.broadcasted_iota(jnp.int32, (8, lanes), 0)
-    state_ref[NUM_FEAT:, :] = jnp.where(row == 0, total[:, :lanes], jnp.where(row == 1, more, 0.0))
+    tail = state_ref[NUM_FEAT - 8 :, :]
+    state_ref[NUM_FEAT - 8 :, :] = jnp.where(row == 1, total[:, :lanes], jnp.where(row == 2, more, tail))
 
 
 def inner_kernel(raw_ref, key_ref, value_ref, query_ref, numerator_ref, denominator_ref):
@@ -172,7 +172,7 @@
         state += other[...]
     width = numerator_ref.shape[1]
     query = query_ref[...]
-    rest = state[:NUM_FEAT, :]
+    rest = state
     parts = []
     for _ in range(3):
         parts.append(rest.astype(BF16))
@@ -182,7 +182,7 @@
     for start in range(0, 3 * width, width):
         numerator += product[:, start : start + width]
     totals = jnp.concatenate(
-        [state[NUM_FEAT : NUM_FEAT + 1, :], state[NUM_FEAT + 1 : NUM_FEAT + 2, : NUM_FEAT - width]], axis=1
+        [state[NUM_FEAT - 7 : NUM_FEAT - 6, :], state[NUM_FEAT - 6 : NUM_FEAT - 5, : NUM_FEAT - width]], axis=1
     )
     denominator = denominator_ref[:, :1] + jnp.sum(query.astype(F32) * totals, axis=1, keepdims=True)
     out_ref[...] = (numerator / denominator).astype(BF16)
@@ -242,7 +242,7 @@
             jax.ShapeDtypeStruct((FEAT, local_rows), F32),
             jax.ShapeDtypeStruct((NUM_FEAT, local_rows), BF16),
             jax.ShapeDtypeStruct((val_width, local_rows), BF16),
-            jax.ShapeDtypeStruct((STATE_ROWS, val_width), F32),
+            jax.ShapeDtypeStruct((NUM_FEAT, val_width), F32),
         ],
         [conv_weight, halo] + blocks,
         [pltpu.VMEM((row_width, rows + local_rows), F32)],
@@ -259,7 +259,7 @@
     total = state + received
     bit = 2
     while bit < ctx:
-        radix = 2
+        radix = min(4, ctx // bit)
         last = bit * radix >= ctx
         digit = me // bit % radix
         parts = []

time: 50.7 us -> 49.3 us (0.972)
  waiting for transfers between devices: 28.3 us -> 24.9 us
  starting transfers between devices: 17.1 us -> 19.2 us
    ppermute x2 -> x3, waiting for transfers between devices: 6.95 us -> 3.52 us  [per_device(): parts.append(lax.ppermute(total, 'ctx', pairs))]
    ppermute x2 -> x3, starting transfers between devices: 1.57 us -> 3.62 us  [per_device(): parts.append(lax.ppermute(total, 'ctx', pairs))]
  transfers between devices with their start and end apart: 18 -> 19, of which waited for: 9 -> 9; matrix products, arithmetic and copies ran while one was open for 0% -> 0% of each run, Pallas kernels for 6% -> 6%
where the time goes in v4:
time: 49.3 us; the launch traced here: 49.1 us
  waiting for transfers between devices  24.9 us (51%)
  starting transfers between devices  19.2 us (39%)
  Pallas kernels  4.78 us (10%)
    ppermute x1, waiting for transfers between devices, per_device(): lax.ppermute(mine, 'tp', [((z + 2 * turn) % tp, z) for z in range(tp)])  9.51 us
    ppermute x8, waiting for transfers between devices, swap(): return lax.ppermute(array, 'ctx', [(i, i ^ bit) for i in range(ctx)])  6.04 us
    ppermute x2, waiting for transfers between devices, per_device(): blocks += [lax.ppermute(one, 'tp', pairs), lax.ppermute(two, 'tp', pairs)]  5.83 us
    pallas_call x7, Pallas kernels, call(): pl.pallas_call(kernel, out_shape=outs, in_specs=[space] * len(operands),...  4.78 us
    ppermute x8, starting transfers between devices, swap(): return lax.ppermute(array, 'ctx', [(i, i ^ bit) for i in range(ctx)])  3.67 us
    ppermute x3, starting transfers between devices, per_device(): parts.append(lax.ppermute(total, 'ctx', pairs))  3.62 us
    ppermute x2, starting transfers between devices, per_device(): blocks += [lax.ppermute(one, 'tp', pairs), lax.ppermute(two, 'tp', pairs)]  3.53 us
    ppermute x3, waiting for transfers between devices, per_device(): parts.append(lax.ppermute(total, 'ctx', pairs))  3.52 us
  transfers between devices with their start and end apart: 19, of which 9 were waited for; matrix products, arithmetic and copies ran while one was open for 0% of the time, Pallas kernels for 6%

profile of v4, /device:TPU:0, one launch (start us, length us, event | category | flops | bytes accessed | tf_op | source)
XLA Modules:
  0.0 49.1 jit_solution(15702647592422821089)
XLA Ops:
  0.0 3.1 %collective-permute-start.4 = (bf16[128,2048]{1,0:T(8,128)(2,1)}, bf16[128,2048]{1,0:T(8,128)(2,1)S(1)}, u32[]{:S(2)}, u32[]{:S(2)}) collective-permute-start(bf16[128,2048]{1,0:T(8,128)(2,1)} %tokens_ref.5), channel_id=1, source_target_pairs={{0,1},{1,0},{2,3},{3,2},{4,5},{5,4},{6,7},{7,6},{8,9},{9,8},{10,11... | collective-permute-start | bytes 1572872 | tf_op jit(solution)/shard_map/ppermute | solution.py:220
  3.1 1.0 %shard_map.37 = (bf16[160,256]{1,0:T(8,128)(2,1)S(1)}, bf16[8,2048]{1,0:T(8,128)(2,1)S(1)}) custom-call(bf16[160,2048]{1,0:T(8,128)(2,1)} %bitcast.1, bf16[128,2048]{1,0:T(8,128)(2,1)} %tokens_ref.5), custom_call_target="tpu_custom_call" | custom-call | flops 1048576 | bytes 1048576 | tf_op jit(solution)/shard_map/pallas_call | solution.py:26
  4.0 2.7 %collective-permute-start.5 = (bf16[160,256]{1,0:T(8,128)(2,1)S(1)}, bf16[160,256]{1,0:T(8,128)(2,1)S(1)}, u32[]{:S(2)}, u32[]{:S(2)}) collective-permute-start(bf16[160,256]{1,0:T(8,128)(2,1)S(1)} %get-tuple-element.21), channel_id=1, source_target_pairs={{2,0},{3,1},{0,2},{1,3},{6,4},{7,5},{4,6},{5,7},{10,8},{11,9},{8,1... | collective-permute-start | bytes 245768 | tf_op jit(solution)/shard_map/ppermute | solution.py:217
  6.7 9.5 %collective-permute-done.5.refs_0_ = bf16[160,256]{1,0:T(8,128)(2,1)S(1)} collective-permute-done((bf16[160,256]{1,0:T(8,128)(2,1)S(1)}, bf16[160,256]{1,0:T(8,128)(2,1)S(1)}, u32[]{:S(2)}, u32[]{:S(2)}) %collective-permute-start.5) | collective-permute-done | bytes 81952 | tf_op jit(solution)/shard_map/ppermute | solution.py:217
  16.2 1.5 %collective-permute-start.6 = (bf16[160,256]{1,0:T(8,128)(2,1)S(1)}, bf16[160,256]{1,0:T(8,128)(2,1)S(1)}, u32[]{:S(2)}, u32[]{:S(2)}) collective-permute-start(bf16[160,256]{1,0:T(8,128)(2,1)S(1)} %collective-permute-done.5.refs_0_), channel_id=1, source_target_pairs={{0,8},{4,12},{8,0},{12,4},{16,24},{20,28},{24,16},{28,20},{1,9},{5... | collective-permute-start | bytes 245768 | tf_op jit(solution)/shard_map/ppermute | solution.py:203
  17.7 1.5 %collective-permute-start.7 = (bf16[160,256]{1,0:T(8,128)(2,1)S(1)}, bf16[160,256]{1,0:T(8,128)(2,1)S(1)}, u32[]{:S(2)}, u32[]{:S(2)}) collective-permute-start(bf16[160,256]{1,0:T(8,128)(2,1)S(1)} %collective-permute-done.5.refs_0_), channel_id=1, source_target_pairs={{0,16},{4,20},{8,24},{12,28},{16,0},{20,4},{24,8},{28,12},{1,17},{... | collective-permute-start | bytes 245768 | tf_op jit(solution)/shard_map/ppermute | solution.py:203
  19.7 1.4 %collective-permute-done.6.refs_1_ = bf16[160,256]{1,0:T(8,128)(2,1)S(1)} collective-permute-done((bf16[160,256]{1,0:T(8,128)(2,1)S(1)}, bf16[160,256]{1,0:T(8,128)(2,1)S(1)}, u32[]{:S(2)}, u32[]{:S(2)}) %collective-permute-start.6) | collective-permute-done | bytes 81952 | tf_op jit(solution)/shard_map/ppermute | solution.py:203
  21.1 1.8 %collective-permute-done.7.refs_2_ = bf16[160,256]{1,0:T(8,128)(2,1)S(1)} collective-permute-done((bf16[160,256]{1,0:T(8,128)(2,1)S(1)}, bf16[160,256]{1,0:T(8,128)(2,1)S(1)}, u32[]{:S(2)}, u32[]{:S(2)}) %collective-permute-start.7) | collective-permute-done | bytes 81952 | tf_op jit(solution)/shard_map/ppermute | solution.py:203
  22.9 1.6 %collective-permute-done.8.refs_3_ = bf16[160,256]{1,0:T(8,128)(2,1)S(1)} collective-permute-done((bf16[160,256]{1,0:T(8,128)(2,1)S(1)}, bf16[160,256]{1,0:T(8,128)(2,1)S(1)}, u32[]{:S(2)}, u32[]{:S(2)}) %collective-permute-start.8) | collective-permute-done | bytes 81952 | tf_op jit(solution)/shard_map/ppermute | solution.py:203
  24.6 0.7 %collective-permute-start.3 = (bf16[8,2048]{1,0:T(8,128)(2,1)S(1)}, bf16[8,2048]{1,0:T(8,128)(2,1)S(1)}, u32[]{:S(2)}, u32[]{:S(2)}) collective-permute-start(bf16[8,2048]{1,0:T(8,128)(2,1)S(1)} %get-tuple-element.18), channel_id=1, source_target_pairs={{3,7},{7,11},{11,15},{15,19},{19,23},{23,27},{27,31}} | collective-permute-start | bytes 98312 | tf_op jit(solution)/shard_map/ppermute | solution.py:225
  25.2 0.7 %collective-permute-start.2 = (bf16[8,2048]{1,0:T(8,128)(2,1)S(1)}, bf16[8,2048]{1,0:T(8,128)(2,1)S(1)}, u32[]{:S(2)}, u32[]{:S(2)}) collective-permute-start(bf16[8,2048]{1,0:T(8,128)(2,1)S(1)} %get-tuple-element.18), channel_id=1, source_target_pairs={{3,6},{7,10},{11,14},{15,18},{19,22},{23,26},{27,30}} | collective-permute-start | bytes 98312 | tf_op jit(solution)/shard_map/ppermute | solution.py:225
  25.9 0.7 %collective-permute-start = (bf16[8,2048]{1,0:T(8,128)(2,1)S(1)}, bf16[8,2048]{1,0:T(8,128)(2,1)S(1)}, u32[]{:S(2)}, u32[]{:S(2)}) collective-permute-start(bf16[8,2048]{1,0:T(8,128)(2,1)S(1)} %get-tuple-element.18), channel_id=1, source_target_pairs={{3,4},{7,8},{11,12},{15,16},{19,20},{23,24},{27,28}} | collective-permute-start | bytes 98312 | tf_op jit(solution)/shard_map/ppermute | solution.py:225
  26.6 0.7 %collective-permute-start.1 = (bf16[8,2048]{1,0:T(8,128)(2,1)S(1)}, bf16[8,2048]{1,0:T(8,128)(2,1)S(1)}, u32[]{:S(2)}, u32[]{:S(2)}) collective-permute-start(bf16[8,2048]{1,0:T(8,128)(2,1)S(1)} %get-tuple-element.18), channel_id=1, source_target_pairs={{3,5},{7,9},{11,13},{15,17},{19,21},{23,25},{27,29}} | collective-permute-start | bytes 98312 | tf_op jit(solution)/shard_map/ppermute | solution.py:225
  27.6 3.4 %collective-permute-start.13 = (bf16[160,128]{1,0:T(8,128)(2,1)S(1)}, bf16[160,128]{1,0:T(8,128)(2,1)S(1)}, u32[]{:S(2)}, u32[]{:S(2)}) collective-permute-start(bf16[160,128]{1,0:T(8,128)(2,1)S(1)} %shard_map.40), channel_id=1, source_target_pairs={{0,2},{1,3},{2,0},{3,1},{4,6},{5,7},{6,4},{7,5},{8,10},{9,11},{10,... | collective-permute-start | bytes 122888 | tf_op jit(solution)/shard_map/ppermute | solution.py:238
  31.1 0.5 %shard_map.39 = (bf16[160,128]{1,0:T(8,128)(2,1)S(1)}, bf16[160,128]{1,0:T(8,128)(2,1)S(1)}) custom-call(bf16[128,2048]{1,0:T(8,128)(2,1)S(1)} %collective-permute-done.4.tokens_ref, bf16[160,2048]{1,0:T(8,128)(2,1)S(1)} %bitcast.2, bf16[160,256]{1,0:T(8,128)(2,1)S(1)} %collective-permute-done.5.refs_0_, ...), custom_call_target="tpu_custom_call" | custom-call | flops 167772160 | bytes 1048576 | tf_op jit(solution)/shard_map/pallas_call | solution.py:26
  32.3 0.8 %collective-permute-done.13.refs_2_ = bf16[160,128]{1,0:T(8,128)(2,1)S(1)} collective-permute-done((bf16[160,128]{1,0:T(8,128)(2,1)S(1)}, bf16[160,128]{1,0:T(8,128)(2,1)S(1)}, u32[]{:S(2)}, u32[]{:S(2)}) %collective-permute-start.13) | collective-permute-done | bytes 40992 | tf_op jit(solution)/shard_map/ppermute | solution.py:238
  33.1 5.0 %collective-permute-done.14.refs_3_ = bf16[160,128]{1,0:T(8,128)(2,1)S(1)} collective-permute-done((bf16[160,128]{1,0:T(8,128)(2,1)S(1)}, bf16[160,128]{1,0:T(8,128)(2,1)S(1)}, u32[]{:S(2)}, u32[]{:S(2)}) %collective-permute-start.14) | collective-permute-done | bytes 40992 | tf_op jit(solution)/shard_map/ppermute | solution.py:238
  38.1 0.8 %shard_map.41 = (f32[16,512]{1,0:T(8,128)S(1)}, bf16[160,512]{1,0:T(8,128)(2,1)S(1)}, bf16[128,512]{1,0:T(8,128)(2,1)S(1)}, f32[160,128]{1,0:T(8,128)S(1)}) custom-call(f32[4,160]{1,0:T(4,128)S(1)} %copy-done.2, bf16[160,128]{1,0:T(8,128)(2,1)S(1)} %get-tuple-element.19.halo_ref, bf16[160,128]{1,0:T(8,128)(2,1)S(1)} %get-tuple-element.20.refs_0_, ...), custom_call_target="tpu_custom_call" | custom-call | flops 1048576 | bytes 1048576 | tf_op jit(solution)/shard_map/pallas_call | solution.py:26
  39.1 1.2 %collective-permute-done.15 = f32[160,128]{1,0:T(8,128)S(1)} collective-permute-done((f32[160,128]{1,0:T(8,128)S(1)}, f32[160,128]{1,0:T(8,128)S(1)}, u32[]{:S(2)}, u32[]{:S(2)}) %collective-permute-start.15) | collective-permute-done | bytes 81952 | tf_op jit(solution)/shard_map/ppermute | solution.py:203
  40.2 1.0 %collective-permute-start.16 = (f32[160,128]{1,0:T(8,128)S(1)}, f32[160,128]{1,0:T(8,128)S(1)}, u32[]{:S(2)}, u32[]{:S(2)}) collective-permute-start(f32[160,128]{1,0:T(8,128)S(1)} %get-tuple-element.31), channel_id=1, source_target_pairs={{0,8},{4,12},{8,0},{12,4},{16,24},{20,28},{24,16},{28,20},{1,9},{5... | collective-permute-start | bytes 245768 | tf_op jit(solution)/shard_map/ppermute | solution.py:268
  41.3 0.7 %shard_map.42 = (bf16[512,160]{1,0:T(8,128)(2,1)S(1)}, f32[512,128]{1,0:T(8,128)S(1)}, f32[512,128]{1,0:T(8,128)S(1)}) custom-call(f32[16,512]{1,0:T(8,128)S(1)} %get-tuple-element.24.raw_ref, bf16[160,512]{1,0:T(8,128)(2,1)S(1)} %get-tuple-element.25.key_ref, bf16[128,512]{1,0:T(8,128)(2,1)S(1)} %get-tuple-element.26.value_ref), custom_call_target="tpu_custom_call" | custom-call | flops 150994944 | bytes 1048576 | tf_op jit(solution)/shard_map/pallas_call | solution.py:26
  42.0 2.5 %collective-permute-start.18 = (f32[160,128]{1,0:T(8,128)S(1)}, f32[160,128]{1,0:T(8,128)S(1)}, u32[]{:S(2)}, u32[]{:S(2)}) collective-permute-start(f32[160,128]{1,0:T(8,128)S(1)} %get-tuple-element.31), channel_id=1, source_target_pairs={{0,24},{4,28},{8,16},{12,20},{16,8},{20,12},{24,0},{28,4},{1,25},{... | collective-permute-start | bytes 245768 | tf_op jit(solution)/shard_map/ppermute | solution.py:268
  44.8 3.2 %collective-permute-done.17 = f32[160,128]{1,0:T(8,128)S(1)} collective-permute-done((f32[160,128]{1,0:T(8,128)S(1)}, f32[160,128]{1,0:T(8,128)S(1)}, u32[]{:S(2)}, u32[]{:S(2)}) %collective-permute-start.17) | collective-permute-done | bytes 81952 | tf_op jit(solution)/shard_map/ppermute | solution.py:268
  48.1 1.0 %shard_map.43 = bf16[512,128]{1,0:T(8,128)(2,1)} custom-call(bf16[512,160]{1,0:T(8,128)(2,1)S(1)} %get-tuple-element.27.query_ref, f32[512,128]{1,0:T(8,128)S(1)} %get-tuple-element.28.numerator_ref, f32[512,128]{1,0:T(8,128)S(1)} %get-tuple-element.29.denominator_ref, f32[160,128]{1,0:T(8,128)S(1)} %get-tuple-element.32.refs_0_, ...), custom_call_target="tpu_custom_call" | custom-call | flops 62914560 | bytes 1048576 | tf_op jit(solution)/shard_map/pallas_call | solution.py:26
  (32 shorter events, 2.0 us)
Async XLA Ops:
  0.0 27.6 %collective-permute-start.4 = (bf16[128,2048]{1,0:T(8,128)(2,1)}, bf16[128,2048]{1,0:T(8,128)(2,1)S(1)}, u32[]{:S(2)}, u32[]{:S(2)}) collective-permute-start(bf16[128,2048]{1,0:T(8,128)(2,1)} %tokens_ref.5), channel_id=1, source_target_pairs={{0,1},{1,0},{2,3},{3,2},{4,5},{5,4},{6,7},{7,6},{8,9},{9,8},{10,11... | collective-permute-start | bytes 1572872 | tf_op jit(solution)/shard_map/ppermute | solution.py:220
  3.1 24.2 %copy-start.1 = (bf16[128,2048]{1,0:T(8,128)(2,1)S(1)}, bf16[128,2048]{1,0:T(8,128)(2,1)}, u32[]{:S(2)}) copy-start(bf16[128,2048]{1,0:T(8,128)(2,1)} %tokens_ref.5) | copy-start | bytes 1572868
  4.0 27.1 %copy-start = (bf16[2048,160]{0,1:T(8,128)(2,1)S(1)}, bf16[2048,160]{0,1:T(8,128)(2,1)}, u32[]{:S(2)}) copy-start(bf16[2048,160]{0,1:T(8,128)(2,1)} %param.4) | copy-start | bytes 1966084
  4.0 12.2 %collective-permute-start.5 = (bf16[160,256]{1,0:T(8,128)(2,1)S(1)}, bf16[160,256]{1,0:T(8,128)(2,1)S(1)}, u32[]{:S(2)}, u32[]{:S(2)}) collective-permute-start(bf16[160,256]{1,0:T(8,128)(2,1)S(1)} %get-tuple-element.21), channel_id=1, source_target_pairs={{2,0},{3,1},{0,2},{1,3},{6,4},{7,5},{4,6},{5,7},{10,8},{11,9},{8,1... | collective-permute-start | bytes 245768 | tf_op jit(solution)/shard_map/ppermute | solution.py:217
  16.2 4.9 %collective-permute-start.6 = (bf16[160,256]{1,0:T(8,128)(2,1)S(1)}, bf16[160,256]{1,0:T(8,128)(2,1)S(1)}, u32[]{:S(2)}, u32[]{:S(2)}) collective-permute-start(bf16[160,256]{1,0:T(8,128)(2,1)S(1)} %collective-permute-done.5.refs_0_), channel_id=1, source_target_pairs={{0,8},{4,12},{8,0},{12,4},{16,24},{20,28},{24,16},{28,20},{1,9},{5... | collective-permute-start | bytes 245768 | tf_op jit(solution)/shard_map/ppermute | solution.py:203
  17.7 5.3 %collective-permute-start.7 = (bf16[160,256]{1,0:T(8,128)(2,1)S(1)}, bf16[160,256]{1,0:T(8,128)(2,1)S(1)}, u32[]{:S(2)}, u32[]{:S(2)}) collective-permute-start(bf16[160,256]{1,0:T(8,128)(2,1)S(1)} %collective-permute-done.5.refs_0_), channel_id=1, source_target_pairs={{0,16},{4,20},{8,24},{12,28},{16,0},{20,4},{24,8},{28,12},{1,17},{... | collective-permute-start | bytes 245768 | tf_op jit(solution)/shard_map/ppermute | solution.py:203
  19.2 5.3 %collective-permute-start.8 = (bf16[160,256]{1,0:T(8,128)(2,1)S(1)}, bf16[160,256]{1,0:T(8,128)(2,1)S(1)}, u32[]{:S(2)}, u32[]{:S(2)}) collective-permute-start(bf16[160,256]{1,0:T(8,128)(2,1)S(1)} %collective-permute-done.5.refs_0_), channel_id=1, source_target_pairs={{0,24},{4,28},{8,16},{12,20},{16,8},{20,12},{24,0},{28,4},{1,25},{... | collective-permute-start | bytes 245768 | tf_op jit(solution)/shard_map/ppermute | solution.py:203
  19.7 4.9 %collective-permute-start.9 = (bf16[160,256]{1,0:T(8,128)(2,1)S(1)}, bf16[160,256]{1,0:T(8,128)(2,1)S(1)}, u32[]{:S(2)}, u32[]{:S(2)}) collective-permute-start(bf16[160,256]{1,0:T(8,128)(2,1)S(1)} %collective-permute-done.5.refs_0_), channel_id=1, source_target_pairs={{0,4},{4,0},{8,12},{12,8},{16,20},{20,16},{24,28},{28,24},{1,5},{5... | collective-permute-start | bytes 245768 | tf_op jit(solution)/shard_map/ppermute | solution.py:203
  21.1 4.1 %collective-permute-start.10 = (bf16[160,256]{1,0:T(8,128)(2,1)S(1)}, bf16[160,256]{1,0:T(8,128)(2,1)S(1)}, u32[]{:S(2)}, u32[]{:S(2)}) collective-permute-start(bf16[160,256]{1,0:T(8,128)(2,1)S(1)} %collective-permute-done.6.refs_1_), channel_id=1, source_target_pairs={{0,4},{4,0},{8,12},{12,8},{16,20},{20,16},{24,28},{28,24},{1,5},{5... | collective-permute-start | bytes 245768 | tf_op jit(solution)/shard_map/ppermute | solution.py:203
  22.9 3.0 %collective-permute-start.11 = (bf16[160,256]{1,0:T(8,128)(2,1)S(1)}, bf16[160,256]{1,0:T(8,128)(2,1)S(1)}, u32[]{:S(2)}, u32[]{:S(2)}) collective-permute-start(bf16[160,256]{1,0:T(8,128)(2,1)S(1)} %collective-permute-done.7.refs_2_), channel_id=1, source_target_pairs={{0,4},{4,0},{8,12},{12,8},{16,20},{20,16},{24,28},{28,24},{1,5},{5... | collective-permute-start | bytes 245768 | tf_op jit(solution)/shard_map/ppermute | solution.py:203
  24.6 2.0 %collective-permute-start.12 = (bf16[160,256]{1,0:T(8,128)(2,1)S(1)}, bf16[160,256]{1,0:T(8,128)(2,1)S(1)}, u32[]{:S(2)}, u32[]{:S(2)}) collective-permute-start(bf16[160,256]{1,0:T(8,128)(2,1)S(1)} %collective-permute-done.8.refs_3_), channel_id=1, source_target_pairs={{0,4},{4,0},{8,12},{12,8},{16,20},{20,16},{24,28},{28,24},{1,5},{5... | collective-permute-start | bytes 245768 | tf_op jit(solution)/shard_map/ppermute | solution.py:203
  24.6 7.0 %collective-permute-start.3 = (bf16[8,2048]{1,0:T(8,128)(2,1)S(1)}, bf16[8,2048]{1,0:T(8,128)(2,1)S(1)}, u32[]{:S(2)}, u32[]{:S(2)}) collective-permute-start(bf16[8,2048]{1,0:T(8,128)(2,1)S(1)} %get-tuple-element.18), channel_id=1, source_target_pairs={{3,7},{7,11},{11,15},{15,19},{19,23},{23,27},{27,31}} | collective-permute-start | bytes 98312 | tf_op jit(solution)/shard_map/ppermute | solution.py:225
  25.2 6.5 %collective-permute-start.2 = (bf16[8,2048]{1,0:T(8,128)(2,1)S(1)}, bf16[8,2048]{1,0:T(8,128)(2,1)S(1)}, u32[]{:S(2)}, u32[]{:S(2)}) collective-permute-start(bf16[8,2048]{1,0:T(8,128)(2,1)S(1)} %get-tuple-element.18), channel_id=1, source_target_pairs={{3,6},{7,10},{11,14},{15,18},{19,22},{23,26},{27,30}} | collective-permute-start | bytes 98312 | tf_op jit(solution)/shard_map/ppermute | solution.py:225
  25.9 5.8 %collective-permute-start = (bf16[8,2048]{1,0:T(8,128)(2,1)S(1)}, bf16[8,2048]{1,0:T(8,128)(2,1)S(1)}, u32[]{:S(2)}, u32[]{:S(2)}) collective-permute-start(bf16[8,2048]{1,0:T(8,128)(2,1)S(1)} %get-tuple-element.18), channel_id=1, source_target_pairs={{3,4},{7,8},{11,12},{15,16},{19,20},{23,24},{27,28}} | collective-permute-start | bytes 98312 | tf_op jit(solution)/shard_map/ppermute | solution.py:225
  26.6 5.1 %collective-permute-start.1 = (bf16[8,2048]{1,0:T(8,128)(2,1)S(1)}, bf16[8,2048]{1,0:T(8,128)(2,1)S(1)}, u32[]{:S(2)}, u32[]{:S(2)}) collective-permute-start(bf16[8,2048]{1,0:T(8,128)(2,1)S(1)} %get-tuple-element.18), channel_id=1, source_target_pairs={{3,5},{7,9},{11,13},{15,17},{19,21},{23,25},{27,29}} | collective-permute-start | bytes 98312 | tf_op jit(solution)/shard_map/ppermute | solution.py:225
  27.6 5.4 %collective-permute-start.13 = (bf16[160,128]{1,0:T(8,128)(2,1)S(1)}, bf16[160,128]{1,0:T(8,128)(2,1)S(1)}, u32[]{:S(2)}, u32[]{:S(2)}) collective-permute-start(bf16[160,128]{1,0:T(8,128)(2,1)S(1)} %shard_map.40), channel_id=1, source_target_pairs={{0,2},{1,3},{2,0},{3,1},{4,6},{5,7},{6,4},{7,5},{8,10},{9,11},{10,... | collective-permute-start | bytes 122888 | tf_op jit(solution)/shard_map/ppermute | solution.py:238
  31.6 6.5 %collective-permute-start.14 = (bf16[160,128]{1,0:T(8,128)(2,1)S(1)}, bf16[160,128]{1,0:T(8,128)(2,1)S(1)}, u32[]{:S(2)}, u32[]{:S(2)}) collective-permute-start(bf16[160,128]{1,0:T(8,128)(2,1)S(1)} %get-tuple-element.23), channel_id=1, source_target_pairs={{0,2},{1,3},{2,0},{3,1},{4,6},{5,7},{6,4},{7,5},{8,10},{9,11},{10,... | collective-permute-start | bytes 122888 | tf_op jit(solution)/shard_map/ppermute | solution.py:238
  32.3 5.8 %copy-start.2 = (f32[4,160]{1,0:T(4,128)S(1)}, f32[4,160]{1,0:T(4,128)}, u32[]{:S(2)}) copy-start(f32[4,160]{1,0:T(4,128)} %conv_ref.1) | copy-start | bytes 7684
  38.9 1.3 %collective-permute-start.15 = (f32[160,128]{1,0:T(8,128)S(1)}, f32[160,128]{1,0:T(8,128)S(1)}, u32[]{:S(2)}, u32[]{:S(2)}) collective-permute-start(f32[160,128]{1,0:T(8,128)S(1)} %get-tuple-element.30), channel_id=1, source_target_pairs={{0,4},{4,0},{8,12},{12,8},{16,20},{20,16},{24,28},{28,24},{1,5},{5... | collective-permute-start | bytes 245768 | tf_op jit(solution)/shard_map/ppermute | solution.py:203
  40.2 4.6 %collective-permute-start.16 = (f32[160,128]{1,0:T(8,128)S(1)}, f32[160,128]{1,0:T(8,128)S(1)}, u32[]{:S(2)}, u32[]{:S(2)}) collective-permute-start(f32[160,128]{1,0:T(8,128)S(1)} %get-tuple-element.31), channel_id=1, source_target_pairs={{0,8},{4,12},{8,0},{12,4},{16,24},{20,28},{24,16},{28,20},{1,9},{5... | collective-permute-start | bytes 245768 | tf_op jit(solution)/shard_map/ppermute | solution.py:268
  41.9 6.1 %collective-permute-start.17 = (f32[160,128]{1,0:T(8,128)S(1)}, f32[160,128]{1,0:T(8,128)S(1)}, u32[]{:S(2)}, u32[]{:S(2)}) collective-permute-start(f32[160,128]{1,0:T(8,128)S(1)} %get-tuple-element.31), channel_id=1, source_target_pairs={{0,16},{4,20},{8,24},{12,28},{16,0},{20,4},{24,8},{28,12},{1,17},{... | collective-permute-start | bytes 245768 | tf_op jit(solution)/shard_map/ppermute | solution.py:268
  42.0 6.1 %collective-permute-start.18 = (f32[160,128]{1,0:T(8,128)S(1)}, f32[160,128]{1,0:T(8,128)S(1)}, u32[]{:S(2)}, u32[]{:S(2)}) collective-permute-start(f32[160,128]{1,0:T(8,128)S(1)} %get-tuple-element.31), channel_id=1, source_target_pairs={{0,24},{4,28},{8,16},{12,20},{16,8},{20,12},{24,0},{28,4},{1,25},{... | collective-permute-start | bytes 245768 | tf_op jit(solution)/shard_map/ppermute | solution.py:268

commit v5 on v2

--- a/solution.py
+++ b/solution.py
@@ -15,7 +15,6 @@
 LANES = 128
 QUAD_FEATS = FEAT * (FEAT + 1) // 2
 NUM_FEAT = QUAD_FEATS + FEAT + 8
-STATE_ROWS = NUM_FEAT + 8
 F32 = jnp.float32
 BF16 = jnp.bfloat16
 HBM = pl.BlockSpec(memory_space=pltpu.HBM)
@@ -130,13 +129,14 @@
     query_ref[...] = convolved[:FEAT]
     key = features(convolved[FEAT : 2 * FEAT], True)
     key_ref[...] = key
-    state_ref[:NUM_FEAT, :] = dot_last(key, value)
+    state_ref[...] = dot_last(key, value)
     total = dot_last(jnp.ones((8, local_rows), BF16), key)
     lanes = state_ref.shape[1]
     rest = NUM_FEAT - lanes
     more = jnp.concatenate([total[:, lanes:], jnp.zeros((8, lanes - rest), F32)], axis=1)
     row = lax.broadcasted_iota(jnp.int32, (8, lanes), 0)
-    state_ref[NUM_FEAT:, :] = jnp.where(row == 0, total[:, :lanes], jnp.where(row == 1, more, 0.0))
+    tail = state_ref[NUM_FEAT - 8 :, :]
+    state_ref[NUM_FEAT - 8 :, :] = jnp.where(row == 1, total[:, :lanes], jnp.where(row == 2, more, tail))
 
 
 def inner_kernel(raw_ref, key_ref, value_ref, query_ref, numerator_ref, denominator_ref):
@@ -163,7 +163,7 @@
         state += other[...]
     width = numerator_ref.shape[1]
     query = query_ref[...]
-    rest = state[:NUM_FEAT, :]
+    rest = state
     parts = []
     for _ in range(3):
         parts.append(rest.astype(BF16))
@@ -173,7 +173,7 @@
     for start in range(0, 3 * width, width):
         numerator += product[:, start : start + width]
     totals = jnp.concatenate(
-        [state[NUM_FEAT : NUM_FEAT + 1, :], state[NUM_FEAT + 1 : NUM_FEAT + 2, : NUM_FEAT - width]], axis=1
+        [state[NUM_FEAT - 7 : NUM_FEAT - 6, :], state[NUM_FEAT - 6 : NUM_FEAT - 5, : NUM_FEAT - width]], axis=1
     )
     denominator = denominator_ref[:, :1] + jnp.sum(query.astype(F32) * totals, axis=1, keepdims=True)
     out_ref[...] = (numerator / denominator).astype(BF16)
@@ -231,7 +231,7 @@
             jax.ShapeDtypeStruct((FEAT, local_rows), F32),
             jax.ShapeDtypeStruct((NUM_FEAT, local_rows), BF16),
             jax.ShapeDtypeStruct((val_width, local_rows), BF16),
-            jax.ShapeDtypeStruct((STATE_ROWS, val_width), F32),
+            jax.ShapeDtypeStruct((NUM_FEAT, val_width), F32),
         ],
         [conv_weight, halo] + blocks,
         [pltpu.VMEM((row_width, rows + local_rows), F32)],

time: 49.3 us -> 49.1 us (level)
  no operation moved by 1% of the time
where the time goes in v5:
time: 49.1 us; the launch traced here: 48.9 us
  waiting for transfers between devices  24.8 us (51%)
  starting transfers between devices  19.1 us (39%)
  Pallas kernels  4.77 us (10%)
    ppermute x1, waiting for transfers between devices, per_device(): lax.ppermute(mine, 'tp', [((z + 2 * turn) % tp, z) for z in range(tp)])  9.52 us
    ppermute x8, waiting for transfers between devices, swap(): return lax.ppermute(array, 'ctx', [(i, i ^ bit) for i in range(ctx)])  6.11 us
    ppermute x2, waiting for transfers between devices, per_device(): blocks += [lax.ppermute(one, 'tp', pairs), lax.ppermute(two, 'tp', pairs)]  5.69 us
    pallas_call x7, Pallas kernels, call(): pl.pallas_call(kernel, out_shape=outs, in_specs=[space] * len(operands),...  4.77 us
    ppermute x3, starting transfers between devices, per_device(): parts.append(lax.ppermute(total, 'ctx', pairs))  3.62 us
    ppermute x8, starting transfers between devices, swap(): return lax.ppermute(array, 'ctx', [(i, i ^ bit) for i in range(ctx)])  3.57 us
    ppermute x2, starting transfers between devices, per_device(): blocks += [lax.ppermute(one, 'tp', pairs), lax.ppermute(two, 'tp', pairs)]  3.53 us
    ppermute x3, waiting for transfers between devices, per_device(): parts.append(lax.ppermute(total, 'ctx', pairs))  3.46 us
  transfers between devices with their start and end apart: 19, of which 9 were waited for; matrix products, arithmetic and copies ran while one was open for 0% of the time, Pallas kernels for 6%

profile of v5, /device:TPU:0, one launch (start us, length us, event | category | flops | bytes accessed | tf_op | source)
XLA Modules:
  0.0 48.9 jit_solution(11758960486958054841)
XLA Ops:
  0.0 3.1 %collective-permute-start.4 = (bf16[128,2048]{1,0:T(8,128)(2,1)}, bf16[128,2048]{1,0:T(8,128)(2,1)S(1)}, u32[]{:S(2)}, u32[]{:S(2)}) collective-permute-start(bf16[128,2048]{1,0:T(8,128)(2,1)} %tokens_ref.5), channel_id=1, source_target_pairs={{0,1},{1,0},{2,3},{3,2},{4,5},{5,4},{6,7},{7,6},{8,9},{9,8},{10,11... | collective-permute-start | bytes 1572872 | tf_op jit(solution)/shard_map/ppermute | solution.py:211
  3.1 1.0 %shard_map.37 = (bf16[160,256]{1,0:T(8,128)(2,1)S(1)}, bf16[8,2048]{1,0:T(8,128)(2,1)S(1)}) custom-call(bf16[160,2048]{1,0:T(8,128)(2,1)} %bitcast.1, bf16[128,2048]{1,0:T(8,128)(2,1)} %tokens_ref.5), custom_call_target="tpu_custom_call" | custom-call | flops 1048576 | bytes 1048576 | tf_op jit(solution)/shard_map/pallas_call | solution.py:26
  4.0 2.7 %collective-permute-start.5 = (bf16[160,256]{1,0:T(8,128)(2,1)S(1)}, bf16[160,256]{1,0:T(8,128)(2,1)S(1)}, u32[]{:S(2)}, u32[]{:S(2)}) collective-permute-start(bf16[160,256]{1,0:T(8,128)(2,1)S(1)} %get-tuple-element.21), channel_id=1, source_target_pairs={{2,0},{3,1},{0,2},{1,3},{6,4},{7,5},{4,6},{5,7},{10,8},{11,9},{8,1... | collective-permute-start | bytes 245768 | tf_op jit(solution)/shard_map/ppermute | solution.py:208
  6.7 9.5 %collective-permute-done.5.refs_0_ = bf16[160,256]{1,0:T(8,128)(2,1)S(1)} collective-permute-done((bf16[160,256]{1,0:T(8,128)(2,1)S(1)}, bf16[160,256]{1,0:T(8,128)(2,1)S(1)}, u32[]{:S(2)}, u32[]{:S(2)}) %collective-permute-start.5) | collective-permute-done | bytes 81952 | tf_op jit(solution)/shard_map/ppermute | solution.py:208
  16.2 1.5 %collective-permute-start.6 = (bf16[160,256]{1,0:T(8,128)(2,1)S(1)}, bf16[160,256]{1,0:T(8,128)(2,1)S(1)}, u32[]{:S(2)}, u32[]{:S(2)}) collective-permute-start(bf16[160,256]{1,0:T(8,128)(2,1)S(1)} %collective-permute-done.5.refs_0_), channel_id=1, source_target_pairs={{0,8},{4,12},{8,0},{12,4},{16,24},{20,28},{24,16},{28,20},{1,9},{5... | collective-permute-start | bytes 245768 | tf_op jit(solution)/shard_map/ppermute | solution.py:194
  17.7 1.5 %collective-permute-start.7 = (bf16[160,256]{1,0:T(8,128)(2,1)S(1)}, bf16[160,256]{1,0:T(8,128)(2,1)S(1)}, u32[]{:S(2)}, u32[]{:S(2)}) collective-permute-start(bf16[160,256]{1,0:T(8,128)(2,1)S(1)} %collective-permute-done.5.refs_0_), channel_id=1, source_target_pairs={{0,16},{4,20},{8,24},{12,28},{16,0},{20,4},{24,8},{28,12},{1,17},{... | collective-permute-start | bytes 245768 | tf_op jit(solution)/shard_map/ppermute | solution.py:194
  19.7 1.4 %collective-permute-done.6.refs_1_ = bf16[160,256]{1,0:T(8,128)(2,1)S(1)} collective-permute-done((bf16[160,256]{1,0:T(8,128)(2,1)S(1)}, bf16[160,256]{1,0:T(8,128)(2,1)S(1)}, u32[]{:S(2)}, u32[]{:S(2)}) %collective-permute-start.6) | collective-permute-done | bytes 81952 | tf_op jit(solution)/shard_map/ppermute | solution.py:194
  21.1 1.8 %collective-permute-done.7.refs_2_ = bf16[160,256]{1,0:T(8,128)(2,1)S(1)} collective-permute-done((bf16[160,256]{1,0:T(8,128)(2,1)S(1)}, bf16[160,256]{1,0:T(8,128)(2,1)S(1)}, u32[]{:S(2)}, u32[]{:S(2)}) %collective-permute-start.7) | collective-permute-done | bytes 81952 | tf_op jit(solution)/shard_map/ppermute | solution.py:194
  22.9 1.6 %collective-permute-done.8.refs_3_ = bf16[160,256]{1,0:T(8,128)(2,1)S(1)} collective-permute-done((bf16[160,256]{1,0:T(8,128)(2,1)S(1)}, bf16[160,256]{1,0:T(8,128)(2,1)S(1)}, u32[]{:S(2)}, u32[]{:S(2)}) %collective-permute-start.8) | collective-permute-done | bytes 81952 | tf_op jit(solution)/shard_map/ppermute | solution.py:194
  24.6 0.7 %collective-permute-start.3 = (bf16[8,2048]{1,0:T(8,128)(2,1)S(1)}, bf16[8,2048]{1,0:T(8,128)(2,1)S(1)}, u32[]{:S(2)}, u32[]{:S(2)}) collective-permute-start(bf16[8,2048]{1,0:T(8,128)(2,1)S(1)} %get-tuple-element.17), channel_id=1, source_target_pairs={{3,7},{7,11},{11,15},{15,19},{19,23},{23,27},{27,31}} | collective-permute-start | bytes 98312 | tf_op jit(solution)/shard_map/ppermute | solution.py:216
  25.2 0.7 %collective-permute-start.2 = (bf16[8,2048]{1,0:T(8,128)(2,1)S(1)}, bf16[8,2048]{1,0:T(8,128)(2,1)S(1)}, u32[]{:S(2)}, u32[]{:S(2)}) collective-permute-start(bf16[8,2048]{1,0:T(8,128)(2,1)S(1)} %get-tuple-element.17), channel_id=1, source_target_pairs={{3,6},{7,10},{11,14},{15,18},{19,22},{23,26},{27,30}} | collective-permute-start | bytes 98312 | tf_op jit(solution)/shard_map/ppermute | solution.py:216
  25.9 0.7 %collective-permute-start = (bf16[8,2048]{1,0:T(8,128)(2,1)S(1)}, bf16[8,2048]{1,0:T(8,128)(2,1)S(1)}, u32[]{:S(2)}, u32[]{:S(2)}) collective-permute-start(bf16[8,2048]{1,0:T(8,128)(2,1)S(1)} %get-tuple-element.17), channel_id=1, source_target_pairs={{3,4},{7,8},{11,12},{15,16},{19,20},{23,24},{27,28}} | collective-permute-start | bytes 98312 | tf_op jit(solution)/shard_map/ppermute | solution.py:216
  26.6 0.7 %collective-permute-start.1 = (bf16[8,2048]{1,0:T(8,128)(2,1)S(1)}, bf16[8,2048]{1,0:T(8,128)(2,1)S(1)}, u32[]{:S(2)}, u32[]{:S(2)}) collective-permute-start(bf16[8,2048]{1,0:T(8,128)(2,1)S(1)} %get-tuple-element.17), channel_id=1, source_target_pairs={{3,5},{7,9},{11,13},{15,17},{19,21},{23,25},{27,29}} | collective-permute-start | bytes 98312 | tf_op jit(solution)/shard_map/ppermute | solution.py:216
  27.7 3.4 %collective-permute-start.13 = (bf16[160,128]{1,0:T(8,128)(2,1)S(1)}, bf16[160,128]{1,0:T(8,128)(2,1)S(1)}, u32[]{:S(2)}, u32[]{:S(2)}) collective-permute-start(bf16[160,128]{1,0:T(8,128)(2,1)S(1)} %shard_map.39), channel_id=1, source_target_pairs={{0,2},{1,3},{2,0},{3,1},{4,6},{5,7},{6,4},{7,5},{8,10},{9,11},{10,... | collective-permute-start | bytes 122888 | tf_op jit(solution)/shard_map/ppermute | solution.py:227
  31.6 0.7 %shard_map.38 = (bf16[160,128]{1,0:T(8,128)(2,1)S(1)}, bf16[160,128]{1,0:T(8,128)(2,1)S(1)}, bf16[160,128]{1,0:T(8,128)(2,1)S(1)}) custom-call(bf16[8,2048]{1,0:T(8,128)(2,1)S(1)} %add_add_fusion.tail_ref, bf16[128,2048]{1,0:T(8,128)(2,1)S(1)} %copy-done, bf16[128,2048]{1,0:T(8,128)(2,1)S(1)} %collective-permute-done.4.paired_ref.tokens_ref, ...), custom_call_target="tpu_custom_call" | custom-call | flops 251658240 | bytes 1048576 | tf_op jit(solution)/shard_map/pallas_call | solution.py:26
  32.3 0.8 %collective-permute-done.13.refs_2_ = bf16[160,128]{1,0:T(8,128)(2,1)S(1)} collective-permute-done((bf16[160,128]{1,0:T(8,128)(2,1)S(1)}, bf16[160,128]{1,0:T(8,128)(2,1)S(1)}, u32[]{:S(2)}, u32[]{:S(2)}) %collective-permute-start.13) | collective-permute-done | bytes 40992 | tf_op jit(solution)/shard_map/ppermute | solution.py:227
  33.1 4.9 %collective-permute-done.14.refs_3_ = bf16[160,128]{1,0:T(8,128)(2,1)S(1)} collective-permute-done((bf16[160,128]{1,0:T(8,128)(2,1)S(1)}, bf16[160,128]{1,0:T(8,128)(2,1)S(1)}, u32[]{:S(2)}, u32[]{:S(2)}) %collective-permute-start.14) | collective-permute-done | bytes 40992 | tf_op jit(solution)/shard_map/ppermute | solution.py:227
  38.0 0.8 %shard_map.41 = (f32[16,512]{1,0:T(8,128)S(1)}, bf16[160,512]{1,0:T(8,128)(2,1)S(1)}, bf16[128,512]{1,0:T(8,128)(2,1)S(1)}, f32[160,128]{1,0:T(8,128)S(1)}) custom-call(f32[4,160]{1,0:T(4,128)S(1)} %copy-done.2, bf16[160,128]{1,0:T(8,128)(2,1)S(1)} %get-tuple-element.18.halo_ref, bf16[160,128]{1,0:T(8,128)(2,1)S(1)} %get-tuple-element.19.refs_0_, ...), custom_call_target="tpu_custom_call" | custom-call | flops 1048576 | bytes 1048576 | tf_op jit(solution)/shard_map/pallas_call | solution.py:26
  38.9 1.2 %collective-permute-done.15 = f32[160,128]{1,0:T(8,128)S(1)} collective-permute-done((f32[160,128]{1,0:T(8,128)S(1)}, f32[160,128]{1,0:T(8,128)S(1)}, u32[]{:S(2)}, u32[]{:S(2)}) %collective-permute-start.15) | collective-permute-done | bytes 81952 | tf_op jit(solution)/shard_map/ppermute | solution.py:194
  40.1 0.9 %collective-permute-start.16 = (f32[160,128]{1,0:T(8,128)S(1)}, f32[160,128]{1,0:T(8,128)S(1)}, u32[]{:S(2)}, u32[]{:S(2)}) collective-permute-start(f32[160,128]{1,0:T(8,128)S(1)} %get-tuple-element.29), channel_id=1, source_target_pairs={{0,8},{4,12},{8,0},{12,4},{16,24},{20,28},{24,16},{28,20},{1,9},{5... | collective-permute-start | bytes 245768 | tf_op jit(solution)/shard_map/ppermute | solution.py:257
  41.1 0.7 %shard_map.42 = (bf16[512,160]{1,0:T(8,128)(2,1)S(1)}, f32[512,128]{1,0:T(8,128)S(1)}, f32[512,128]{1,0:T(8,128)S(1)}) custom-call(f32[16,512]{1,0:T(8,128)S(1)} %get-tuple-element.22.raw_ref, bf16[160,512]{1,0:T(8,128)(2,1)S(1)} %get-tuple-element.23.key_ref, bf16[128,512]{1,0:T(8,128)(2,1)S(1)} %get-tuple-element.24.value_ref), custom_call_target="tpu_custom_call" | custom-call | flops 150994944 | bytes 1048576 | tf_op jit(solution)/shard_map/pallas_call | solution.py:26
  41.8 2.6 %collective-permute-start.18 = (f32[160,128]{1,0:T(8,128)S(1)}, f32[160,128]{1,0:T(8,128)S(1)}, u32[]{:S(2)}, u32[]{:S(2)}) collective-permute-start(f32[160,128]{1,0:T(8,128)S(1)} %get-tuple-element.29), channel_id=1, source_target_pairs={{0,24},{4,28},{8,16},{12,20},{16,8},{20,12},{24,0},{28,4},{1,25},{... | collective-permute-start | bytes 245768 | tf_op jit(solution)/shard_map/ppermute | solution.py:257
  44.7 3.2 %collective-permute-done.17 = f32[160,128]{1,0:T(8,128)S(1)} collective-permute-done((f32[160,128]{1,0:T(8,128)S(1)}, f32[160,128]{1,0:T(8,128)S(1)}, u32[]{:S(2)}, u32[]{:S(2)}) %collective-permute-start.17) | collective-permute-done | bytes 81952 | tf_op jit(solution)/shard_map/ppermute | solution.py:257
  48.0 1.0 %shard_map.43 = bf16[512,128]{1,0:T(8,128)(2,1)} custom-call(bf16[512,160]{1,0:T(8,128)(2,1)S(1)} %get-tuple-element.25.query_ref, f32[512,128]{1,0:T(8,128)S(1)} %get-tuple-element.26.numerator_ref, f32[512,128]{1,0:T(8,128)S(1)} %get-tuple-element.27.denominator_ref, f32[160,128]{1,0:T(8,128)S(1)} %get-tuple-element.30.refs_0_, ...), custom_call_target="tpu_custom_call" | custom-call | flops 62914560 | bytes 1048576 | tf_op jit(solution)/shard_map/pallas_call | solution.py:26
  (32 shorter events, 1.8 us)
Async XLA Ops:
  0.0 27.6 %collective-permute-start.4 = (bf16[128,2048]{1,0:T(8,128)(2,1)}, bf16[128,2048]{1,0:T(8,128)(2,1)S(1)}, u32[]{:S(2)}, u32[]{:S(2)}) collective-permute-start(bf16[128,2048]{1,0:T(8,128)(2,1)} %tokens_ref.5), channel_id=1, source_target_pairs={{0,1},{1,0},{2,3},{3,2},{4,5},{5,4},{6,7},{7,6},{8,9},{9,8},{10,11... | collective-permute-start | bytes 1572872 | tf_op jit(solution)/shard_map/ppermute | solution.py:211
  3.1 24.2 %copy-start = (bf16[128,2048]{1,0:T(8,128)(2,1)S(1)}, bf16[128,2048]{1,0:T(8,128)(2,1)}, u32[]{:S(2)}) copy-start(bf16[128,2048]{1,0:T(8,128)(2,1)} %tokens_ref.5) | copy-start | bytes 1572868
  4.0 12.2 %collective-permute-start.5 = (bf16[160,256]{1,0:T(8,128)(2,1)S(1)}, bf16[160,256]{1,0:T(8,128)(2,1)S(1)}, u32[]{:S(2)}, u32[]{:S(2)}) collective-permute-start(bf16[160,256]{1,0:T(8,128)(2,1)S(1)} %get-tuple-element.21), channel_id=1, source_target_pairs={{2,0},{3,1},{0,2},{1,3},{6,4},{7,5},{4,6},{5,7},{10,8},{11,9},{8,1... | collective-permute-start | bytes 245768 | tf_op jit(solution)/shard_map/ppermute | solution.py:208
  16.2 4.9 %collective-permute-start.6 = (bf16[160,256]{1,0:T(8,128)(2,1)S(1)}, bf16[160,256]{1,0:T(8,128)(2,1)S(1)}, u32[]{:S(2)}, u32[]{:S(2)}) collective-permute-start(bf16[160,256]{1,0:T(8,128)(2,1)S(1)} %collective-permute-done.5.refs_0_), channel_id=1, source_target_pairs={{0,8},{4,12},{8,0},{12,4},{16,24},{20,28},{24,16},{28,20},{1,9},{5... | collective-permute-start | bytes 245768 | tf_op jit(solution)/shard_map/ppermute | solution.py:194
  17.7 5.3 %collective-permute-start.7 = (bf16[160,256]{1,0:T(8,128)(2,1)S(1)}, bf16[160,256]{1,0:T(8,128)(2,1)S(1)}, u32[]{:S(2)}, u32[]{:S(2)}) collective-permute-start(bf16[160,256]{1,0:T(8,128)(2,1)S(1)} %collective-permute-done.5.refs_0_), channel_id=1, source_target_pairs={{0,16},{4,20},{8,24},{12,28},{16,0},{20,4},{24,8},{28,12},{1,17},{... | collective-permute-start | bytes 245768 | tf_op jit(solution)/shard_map/ppermute | solution.py:194
  19.2 5.3 %collective-permute-start.8 = (bf16[160,256]{1,0:T(8,128)(2,1)S(1)}, bf16[160,256]{1,0:T(8,128)(2,1)S(1)}, u32[]{:S(2)}, u32[]{:S(2)}) collective-permute-start(bf16[160,256]{1,0:T(8,128)(2,1)S(1)} %collective-permute-done.5.refs_0_), channel_id=1, source_target_pairs={{0,24},{4,28},{8,16},{12,20},{16,8},{20,12},{24,0},{28,4},{1,25},{... | collective-permute-start | bytes 245768 | tf_op jit(solution)/shard_map/ppermute | solution.py:194
  19.7 4.9 %collective-permute-start.9 = (bf16[160,256]{1,0:T(8,128)(2,1)S(1)}, bf16[160,256]{1,0:T(8,128)(2,1)S(1)}, u32[]{:S(2)}, u32[]{:S(2)}) collective-permute-start(bf16[160,256]{1,0:T(8,128)(2,1)S(1)} %collective-permute-done.5.refs_0_), channel_id=1, source_target_pairs={{0,4},{4,0},{8,12},{12,8},{16,20},{20,16},{24,28},{28,24},{1,5},{5... | collective-permute-start | bytes 245768 | tf_op jit(solution)/shard_map/ppermute | solution.py:194
  21.1 4.1 %collective-permute-start.10 = (bf16[160,256]{1,0:T(8,128)(2,1)S(1)}, bf16[160,256]{1,0:T(8,128)(2,1)S(1)}, u32[]{:S(2)}, u32[]{:S(2)}) collective-permute-start(bf16[160,256]{1,0:T(8,128)(2,1)S(1)} %collective-permute-done.6.refs_1_), channel_id=1, source_target_pairs={{0,4},{4,0},{8,12},{12,8},{16,20},{20,16},{24,28},{28,24},{1,5},{5... | collective-permute-start | bytes 245768 | tf_op jit(solution)/shard_map/ppermute | solution.py:194
  22.9 3.0 %collective-permute-start.11 = (bf16[160,256]{1,0:T(8,128)(2,1)S(1)}, bf16[160,256]{1,0:T(8,128)(2,1)S(1)}, u32[]{:S(2)}, u32[]{:S(2)}) collective-permute-start(bf16[160,256]{1,0:T(8,128)(2,1)S(1)} %collective-permute-done.7.refs_2_), channel_id=1, source_target_pairs={{0,4},{4,0},{8,12},{12,8},{16,20},{20,16},{24,28},{28,24},{1,5},{5... | collective-permute-start | bytes 245768 | tf_op jit(solution)/shard_map/ppermute | solution.py:194
  24.6 2.0 %collective-permute-start.12 = (bf16[160,256]{1,0:T(8,128)(2,1)S(1)}, bf16[160,256]{1,0:T(8,128)(2,1)S(1)}, u32[]{:S(2)}, u32[]{:S(2)}) collective-permute-start(bf16[160,256]{1,0:T(8,128)(2,1)S(1)} %collective-permute-done.8.refs_3_), channel_id=1, source_target_pairs={{0,4},{4,0},{8,12},{12,8},{16,20},{20,16},{24,28},{28,24},{1,5},{5... | collective-permute-start | bytes 245768 | tf_op jit(solution)/shard_map/ppermute | solution.py:194
  24.6 6.9 %collective-permute-start.3 = (bf16[8,2048]{1,0:T(8,128)(2,1)S(1)}, bf16[8,2048]{1,0:T(8,128)(2,1)S(1)}, u32[]{:S(2)}, u32[]{:S(2)}) collective-permute-start(bf16[8,2048]{1,0:T(8,128)(2,1)S(1)} %get-tuple-element.17), channel_id=1, source_target_pairs={{3,7},{7,11},{11,15},{15,19},{19,23},{23,27},{27,31}} | collective-permute-start | bytes 98312 | tf_op jit(solution)/shard_map/ppermute | solution.py:216
  25.2 6.3 %collective-permute-start.2 = (bf16[8,2048]{1,0:T(8,128)(2,1)S(1)}, bf16[8,2048]{1,0:T(8,128)(2,1)S(1)}, u32[]{:S(2)}, u32[]{:S(2)}) collective-permute-start(bf16[8,2048]{1,0:T(8,128)(2,1)S(1)} %get-tuple-element.17), channel_id=1, source_target_pairs={{3,6},{7,10},{11,14},{15,18},{19,22},{23,26},{27,30}} | collective-permute-start | bytes 98312 | tf_op jit(solution)/shard_map/ppermute | solution.py:216
  25.9 5.6 %collective-permute-start = (bf16[8,2048]{1,0:T(8,128)(2,1)S(1)}, bf16[8,2048]{1,0:T(8,128)(2,1)S(1)}, u32[]{:S(2)}, u32[]{:S(2)}) collective-permute-start(bf16[8,2048]{1,0:T(8,128)(2,1)S(1)} %get-tuple-element.17), channel_id=1, source_target_pairs={{3,4},{7,8},{11,12},{15,16},{19,20},{23,24},{27,28}} | collective-permute-start | bytes 98312 | tf_op jit(solution)/shard_map/ppermute | solution.py:216
  26.6 5.0 %collective-permute-start.1 = (bf16[8,2048]{1,0:T(8,128)(2,1)S(1)}, bf16[8,2048]{1,0:T(8,128)(2,1)S(1)}, u32[]{:S(2)}, u32[]{:S(2)}) collective-permute-start(bf16[8,2048]{1,0:T(8,128)(2,1)S(1)} %get-tuple-element.17), channel_id=1, source_target_pairs={{3,5},{7,9},{11,13},{15,17},{19,21},{23,25},{27,29}} | collective-permute-start | bytes 98312 | tf_op jit(solution)/shard_map/ppermute | solution.py:216
  27.6 4.0 %copy-start.1 = (bf16[2048,160]{0,1:T(8,128)(2,1)S(1)}, bf16[2048,160]{0,1:T(8,128)(2,1)}, u32[]{:S(2)}) copy-start(bf16[2048,160]{0,1:T(8,128)(2,1)} %param.4) | copy-start | bytes 1966084
  27.7 5.4 %collective-permute-start.13 = (bf16[160,128]{1,0:T(8,128)(2,1)S(1)}, bf16[160,128]{1,0:T(8,128)(2,1)S(1)}, u32[]{:S(2)}, u32[]{:S(2)}) collective-permute-start(bf16[160,128]{1,0:T(8,128)(2,1)S(1)} %shard_map.39), channel_id=1, source_target_pairs={{0,2},{1,3},{2,0},{3,1},{4,6},{5,7},{6,4},{7,5},{8,10},{9,11},{10,... | collective-permute-start | bytes 122888 | tf_op jit(solution)/shard_map/ppermute | solution.py:227
  31.5 6.5 %collective-permute-start.14 = (bf16[160,128]{1,0:T(8,128)(2,1)S(1)}, bf16[160,128]{1,0:T(8,128)(2,1)S(1)}, u32[]{:S(2)}, u32[]{:S(2)}) collective-permute-start(bf16[160,128]{1,0:T(8,128)(2,1)S(1)} %shard_map.40), channel_id=1, source_target_pairs={{0,2},{1,3},{2,0},{3,1},{4,6},{5,7},{6,4},{7,5},{8,10},{9,11},{10,... | collective-permute-start | bytes 122888 | tf_op jit(solution)/shard_map/ppermute | solution.py:227
  32.3 5.7 %copy-start.2 = (f32[4,160]{1,0:T(4,128)S(1)}, f32[4,160]{1,0:T(4,128)}, u32[]{:S(2)}) copy-start(f32[4,160]{1,0:T(4,128)} %conv_ref.1) | copy-start | bytes 7684
  38.8 1.3 %collective-permute-start.15 = (f32[160,128]{1,0:T(8,128)S(1)}, f32[160,128]{1,0:T(8,128)S(1)}, u32[]{:S(2)}, u32[]{:S(2)}) collective-permute-start(f32[160,128]{1,0:T(8,128)S(1)} %get-tuple-element.28), channel_id=1, source_target_pairs={{0,4},{4,0},{8,12},{12,8},{16,20},{20,16},{24,28},{28,24},{1,5},{5... | collective-permute-start | bytes 245768 | tf_op jit(solution)/shard_map/ppermute | solution.py:194
  40.1 4.6 %collective-permute-start.16 = (f32[160,128]{1,0:T(8,128)S(1)}, f32[160,128]{1,0:T(8,128)S(1)}, u32[]{:S(2)}, u32[]{:S(2)}) collective-permute-start(f32[160,128]{1,0:T(8,128)S(1)} %get-tuple-element.29), channel_id=1, source_target_pairs={{0,8},{4,12},{8,0},{12,4},{16,24},{20,28},{24,16},{28,20},{1,9},{5... | collective-permute-start | bytes 245768 | tf_op jit(solution)/shard_map/ppermute | solution.py:257
  41.8 6.1 %collective-permute-start.17 = (f32[160,128]{1,0:T(8,128)S(1)}, f32[160,128]{1,0:T(8,128)S(1)}, u32[]{:S(2)}, u32[]{:S(2)}) collective-permute-start(f32[160,128]{1,0:T(8,128)S(1)} %get-tuple-element.29), channel_id=1, source_target_pairs={{0,16},{4,20},{8,24},{12,28},{16,0},{20,4},{24,8},{28,12},{1,17},{... | collective-permute-start | bytes 245768 | tf_op jit(solution)/shard_map/ppermute | solution.py:257
  41.8 6.1 %collective-permute-start.18 = (f32[160,128]{1,0:T(8,128)S(1)}, f32[160,128]{1,0:T(8,128)S(1)}, u32[]{:S(2)}, u32[]{:S(2)}) collective-permute-start(f32[160,128]{1,0:T(8,128)S(1)} %get-tuple-element.29), channel_id=1, source_target_pairs={{0,24},{4,28},{8,16},{12,20},{16,8},{20,12},{24,0},{28,4},{1,25},{... | collective-permute-start | bytes 245768 | tf_op jit(solution)/shard_map/ppermute | solution.py:257
